TPU v7x, 32 devices: a whole 2x2x4 slice. The times are simulated.
32 devices in a mesh: dp: 16 (over z, y, core), fsdp: 2 (over x).
Axes of the slice: x: 2, y: 2, z: 4, core: 2. Of those that a mesh axis runs over, the one named last changes fastest.
Arguments:
- tile_embeds: bfloat16 [2, 32, 256, 768], P(None, ('dp', 'fsdp')), may hold values from -6 to 6
- sentence_embeds: bfloat16 [2, 96, 64, 768], P(None, ('dp', 'fsdp')), may hold values from -6 to 6
- sentence_picture_map: int32 [2, 96], replicated, may hold values from 0 to 31, as said below
- picture_early_scaler: bfloat16 [768], P(('dp', 'fsdp')), may hold values from 0.5 to 1.5
- picture_early_shifter: bfloat16 [768], P(('dp', 'fsdp')), may hold values from -0.59765625 to 0.59765625
- picture_triplet_matrix: bfloat16 [768, 2304], P(('dp', 'fsdp')), may hold values from -0.375 to 0.375
- picture_mixer_projector: bfloat16 [768, 768], P(('dp', 'fsdp')), may hold values from -0.15625 to 0.15625
- picture_later_scaler: bfloat16 [768], P(('dp', 'fsdp')), may hold values from 0.5 to 1.5
- picture_later_shifter: bfloat16 [768], P(('dp', 'fsdp')), may hold values from -0.59765625 to 0.59765625
- picture_widen_matrix: bfloat16 [768, 3072], P(('dp', 'fsdp')), may hold values from -0.21875 to 0.21875
- picture_shrink_matrix: bfloat16 [3072, 768], P(('dp', 'fsdp')), may hold values from -0.109375 to 0.109375
- pregather_scaler: bfloat16 [768], P(('dp', 'fsdp')), may hold values from 0.5 to 1.5
- pregather_shifter: bfloat16 [768], P(('dp', 'fsdp')), may hold values from -0.59765625 to 0.59765625
- gather_probe_vectors: bfloat16 [768], P(('dp', 'fsdp')), may hold values from -5 to 5
- gather_lookup_matrix: bfloat16 [768, 1536], P(('dp', 'fsdp')), may hold values from -0.21875 to 0.21875
- gather_result_matrix: bfloat16 [768, 768], P(('dp', 'fsdp')), may hold values from -0.21875 to 0.21875
- wording_early_scaler: bfloat16 [768], P(('dp', 'fsdp')), may hold values from 0.5 to 1.5
- wording_early_shifter: bfloat16 [768], P(('dp', 'fsdp')), may hold values from -0.59765625 to 0.59765625
- wording_triplet_matrix: bfloat16 [768, 2304], P(('dp', 'fsdp')), may hold values from -0.375 to 0.375
- wording_mixer_projector: bfloat16 [768, 768], P(('dp', 'fsdp')), may hold values from -0.15625 to 0.15625
- wording_later_scaler: bfloat16 [768], P(('dp', 'fsdp')), may hold values from 0.5 to 1.5
- wording_later_shifter: bfloat16 [768], P(('dp', 'fsdp')), may hold values from -0.59765625 to 0.59765625
- wording_widen_matrix: bfloat16 [768, 3072], P(('dp', 'fsdp')), may hold values from -0.21875 to 0.21875
- wording_shrink_matrix: bfloat16 [3072, 768], P(('dp', 'fsdp')), may hold values from -0.109375 to 0.109375
- wording_closing_scaler: bfloat16 [768], P(('dp', 'fsdp')), may hold values from 0.5 to 1.5
- wording_closing_shifter: bfloat16 [768], P(('dp', 'fsdp')), may hold values from -0.59765625 to 0.59765625
- wording_readout_matrix: bfloat16 [768, 768], P(('dp', 'fsdp')), may hold values from -0.21875 to 0.21875
- sharpness_exponent: float32 [1], replicated, may hold values from 2 to 2.5
- match_score_offset: float32 [1], replicated, may hold values from -6 to -3
Outputs:
- image_embedding: float32 [2, 32, 768], P(None, ('dp', 'fsdp'))
- text_embedding: float32 [2, 96, 768], P(None, ('dp', 'fsdp'))
- penalty_amount: float32 [], replicated
- patches_grad: float32 [2, 32, 256, 768], P(None, ('dp', 'fsdp'))
- captions_grad: float32 [2, 96, 64, 768], P(None, ('dp', 'fsdp'))
- visual_gain_grad: float32 [768], P(('dp', 'fsdp'))
- visual_shift_grad: float32 [768], P(('dp', 'fsdp'))
- visual_triple_grad: float32 [768, 2304], P(('dp', 'fsdp'))
- visual_merge_grad: float32 [768, 768], P(('dp', 'fsdp'))
- visual_scale_grad: float32 [768], P(('dp', 'fsdp'))
- visual_offset_grad: float32 [768], P(('dp', 'fsdp'))
- visual_expand_grad: float32 [768, 3072], P(('dp', 'fsdp'))
- visual_reduce_grad: float32 [3072, 768], P(('dp', 'fsdp'))
- pooling_gain_grad: float32 [768], P(('dp', 'fsdp'))
- pooling_shift_grad: float32 [768], P(('dp', 'fsdp'))
- pooling_probe_grad: float32 [768], P(('dp', 'fsdp'))
- pooling_keyval_grad: float32 [768, 1536], P(('dp', 'fsdp'))
- pooling_output_grad: float32 [768, 768], P(('dp', 'fsdp'))
- textual_gain_grad: float32 [768], P(('dp', 'fsdp'))
- textual_shift_grad: float32 [768], P(('dp', 'fsdp'))
- textual_triple_grad: float32 [768, 2304], P(('dp', 'fsdp'))
- textual_merge_grad: float32 [768, 768], P(('dp', 'fsdp'))
- textual_scale_grad: float32 [768], P(('dp', 'fsdp'))
- textual_offset_grad: float32 [768], P(('dp', 'fsdp'))
- textual_expand_grad: float32 [768, 3072], P(('dp', 'fsdp'))
- textual_reduce_grad: float32 [3072, 768], P(('dp', 'fsdp'))
- closing_gain_grad: float32 [768], P(('dp', 'fsdp'))
- closing_shift_grad: float32 [768], P(('dp', 'fsdp'))
- textual_head_grad: float32 [768, 768], P(('dp', 'fsdp'))
- log_temperature_grad: float32 [1], replicated
- logit_bias_grad: float32 [1], replicated
Inputs may be any that keep to these rules, and one draw needn't show every extreme that they name: `sentence_picture_map`: in each micro-batch every image is described by 2 to 5 captions: 4 images by 5, 8 by 4, 4 by 3 and the other half by 2; the captions stand in no order.
All inputs are finite; a program needn't handle non-finite values.
Results may differ from a plain program's by a relative error of at most 0.025.
Values may be sent and summed in bfloat16 or wider, within the bound.
No kernel may reach another device: no remote copies, remote signals or barrier semaphores. Data moves between devices by JAX's collectives and lax.ppermute only.
A program may use at most 320 MiB of HBM per device.

v0:
```python
import functools

import jax
import jax.numpy as jnp
from jax import lax
from jax.experimental import pallas as pl
from jax.experimental.pallas import tpu as pltpu
from jax.sharding import PartitionSpec as P

HD = 64
AXES = ("dp", "fsdp")
GELU_COEF = 0.7978845608028654
GELU_CUBE = 0.044715
F32 = jnp.float32
LOW = jnp.bfloat16
SCALE = HD ** (-0.5)

BLOCKS = 15
CHAIN_BLOCKS = 5
VEC_ROWS = 8


def dot(left, right, left_dim, right_dim):
    return lax.dot_general(
        left, right, (((left_dim,), (right_dim,)), ((), ())), preferred_element_type=F32
    )


def normalize_rows(values):
    centred = values - jnp.mean(values, axis=-1, keepdims=True)
    inverse = lax.rsqrt(jnp.mean(centred * centred, axis=-1, keepdims=True) + 1e-06)
    return (centred * inverse, inverse)


def normalize_back(grad_hat, hat_rows, inverse):
    first = jnp.mean(grad_hat, axis=-1, keepdims=True)
    second = jnp.mean(grad_hat * hat_rows, axis=-1, keepdims=True)
    return inverse * (grad_hat - first - hat_rows * second)


def gelu_tanh(values):
    return (
        0.5 * values * (1.0 + jnp.tanh(GELU_COEF * (values + GELU_CUBE * values * values * values)))
    )


def gelu_slope(values):
    tanh_val = jnp.tanh(GELU_COEF * (values + GELU_CUBE * values * values * values))
    return 0.5 * (1.0 + tanh_val) + 0.5 * values * (1.0 - tanh_val * tanh_val) * GELU_COEF * (
        1.0 + 3.0 * GELU_CUBE * values * values
    )


def head_probs(allowed, query, key):
    scores = dot(query, key, 1, 1) * SCALE
    scores = jnp.where(allowed, scores, -1e30)
    row_exp = jnp.exp(scores - jnp.max(scores, axis=-1, keepdims=True))
    return row_exp * (1.0 / jnp.sum(row_exp, axis=-1, keepdims=True))


def allowed_pairs(side_ref, seq_len, group):
    row = lax.broadcasted_iota(jnp.int32, (seq_len, seq_len), 0)
    col = lax.broadcasted_iota(jnp.int32, (seq_len, seq_len), 1)
    causal = jnp.logical_and(row // group == col // group, row >= col)
    return jnp.logical_or(causal, side_ref[0] == 0)


def attend_kernel(group, side_ref, q_ref, k_ref, v_ref, out_ref):
    allowed = allowed_pairs(side_ref, q_ref.shape[0], group)
    parts = []
    for head in range(2):
        lanes = slice(head * HD, (head + 1) * HD)
        probs = head_probs(allowed, q_ref[:, lanes], k_ref[:, lanes]).astype(LOW)
        parts.append(dot(probs, v_ref[:, lanes], 1, 0))
    out_ref[...] = jnp.concatenate(parts, axis=1).astype(LOW)


def attend_back_kernel(group, width, side_ref, q_ref, k_ref, v_ref, grad_ref, out_ref):
    pair = pl.program_id(1)
    allowed = allowed_pairs(side_ref, q_ref.shape[0], group)
    parts = ([], [], [])
    for head in range(2):
        lanes = slice(head * HD, (head + 1) * HD)
        query, key, value = q_ref[:, lanes], k_ref[:, lanes], v_ref[:, lanes]
        grad = grad_ref[:, lanes]
        probs = head_probs(allowed, query, key)
        grad_probs = dot(grad, value, 1, 1)
        delta = jnp.sum(grad_probs * probs, axis=-1, keepdims=True)
        grad_scores = (probs * (grad_probs - delta)).astype(LOW)
        parts[0].append(dot(grad_scores, key, 1, 0) * SCALE)
        parts[1].append(dot(grad_scores, query, 0, 0) * SCALE)
        parts[2].append(dot(probs.astype(LOW), grad, 0, 0))
    for place in range(3):
        start = pl.multiple_of(place * width + pair * 2 * HD, 2 * HD)
        out_ref[:, pl.ds(start, 2 * HD)] = jnp.concatenate(parts[place], axis=1).astype(LOW)


def triple_specs(seq_len, pairs):
    return [
        pl.BlockSpec((seq_len, 2 * HD), lambda b, p, s, place=place: (b, place * pairs + p))
        for place in range(3)
    ]


def attend(side, triples, seq_len, group):
    rows, wide = triples.shape
    width = wide // 3
    pairs = width // (2 * HD)
    return pl.pallas_call(
        functools.partial(attend_kernel, group),
        out_shape=jax.ShapeDtypeStruct((rows, width), LOW),
        grid_spec=pltpu.PrefetchScalarGridSpec(
            num_scalar_prefetch=1,
            grid=(rows // seq_len, pairs),
            in_specs=triple_specs(seq_len, pairs),
            out_specs=pl.BlockSpec((seq_len, 2 * HD), lambda b, p, s: (b, p)),
        ),
        cost_estimate=pl.CostEstimate(
            flops=4 * rows * seq_len * width,
            bytes_accessed=8 * rows * width,
            transcendentals=rows * seq_len * width // HD,
        ),
        name="attend",
    )(side, triples, triples, triples)


def attend_back(side, triples, grad_mixed, seq_len, group):
    rows, wide = triples.shape
    width = wide // 3
    pairs = width // (2 * HD)
    return pl.pallas_call(
        functools.partial(attend_back_kernel, group, width),
        out_shape=jax.ShapeDtypeStruct((rows, wide), LOW),
        grid_spec=pltpu.PrefetchScalarGridSpec(
            num_scalar_prefetch=1,
            grid=(rows // seq_len, pairs),
            in_specs=triple_specs(seq_len, pairs)
            + [pl.BlockSpec((seq_len, 2 * HD), lambda b, p, s: (b, p))],
            out_specs=pl.BlockSpec((seq_len, wide), lambda b, p, s: (b, 0)),
        ),
        cost_estimate=pl.CostEstimate(
            flops=10 * rows * seq_len * width,
            bytes_accessed=14 * rows * width,
            transcendentals=rows * seq_len * width // HD,
        ),
        name="attend_back",
    )(side, triples, triples, triples, grad_mixed)


class Links:
    def __init__(self, count):
        self.count = count
        self.half = count // 2
        self.core = 2
        bits = [1 << place for place in range(self.half.bit_length() - 1)]
        outer = [bit for bit in bits if bit != self.core]
        third = max(1, len(outer) // 3)
        self.orders = [outer[place:] + outer[:place] for place in (0, third, 2 * third)]

    def swap(self, value, mask):
        return lax.ppermute(value, AXES, [(place, place ^ mask) for place in range(self.count)])


def gather_chain(links, order, start):
    held, masks = start[None], [0]
    for bit in order[:-1]:
        held = jnp.concatenate((held, links.swap(held, bit)), axis=0)
        masks = masks + [mask ^ bit for mask in masks]
    far = links.swap(held, order[-1])
    far_masks = [mask ^ order[-1] for mask in masks]
    pieces = [held, far, links.swap(held, links.core), links.swap(far, links.core)]
    other = [mask ^ links.core for mask in masks]
    far_other = [mask ^ links.core for mask in far_masks]
    return pieces, [masks, far_masks, other, far_other]


def unpack_chain(links, device, pieces, masks):
    low, side = device % links.half, device // links.half
    flat = [mask for group in masks for mask in group]
    place = [0] * links.half
    for slot, mask in enumerate(flat):
        place[mask] = slot
    slots = jnp.array(place, jnp.int32)[jnp.arange(links.half, dtype=jnp.int32) ^ low]
    whole = jnp.take(jnp.concatenate(pieces, axis=0), slots, axis=0)
    first = jnp.where(side == 0, whole[:, 0], whole[:, 1])
    second = jnp.where(side == 0, whole[:, 1], whole[:, 0])
    return jnp.concatenate((first, second), axis=0)


def pack_chain(links, device, order, whole):
    low, side = device % links.half, device // links.half
    masks = [0]
    for bit in order:
        masks = masks + [mask ^ bit for mask in masks]
    halves = whole.reshape((2, links.half) + whole.shape[1:])
    mine = jnp.where(side == 0, halves[0], halves[1])
    theirs = jnp.where(side == 0, halves[1], halves[0])
    both = jnp.stack((mine, theirs), axis=1)
    keep = jnp.take(both, jnp.array(masks, jnp.int32) ^ low, axis=0)
    send = jnp.take(both, jnp.array(masks, jnp.int32) ^ links.core ^ low, axis=0)
    return keep, send


def scatter_chain(links, order, keep, send):
    received = links.swap(send, links.core)
    total = None
    for bit in order[::-1]:
        near = keep.shape[0] // 2 if total is None else total.shape[0] // 2
        if total is None:
            far = (keep[near:].astype(F32) + received[near:].astype(F32)).astype(LOW)
            arrived = links.swap(far, bit)
            total = keep[:near].astype(F32) + received[:near].astype(F32) + arrived.astype(F32)
        else:
            arrived = links.swap(total[near:].astype(LOW), bit)
            total = total[:near] + arrived.astype(F32)
    return total[0]


def tower_block(matrices, vectors, rows, width):
    parts = []
    for item in matrices:
        if item is None:
            parts.append(jnp.zeros((rows, width), LOW))
        elif item.shape[1] == width:
            parts.append(item)
        else:
            parts.extend(jnp.split(item, item.shape[1] // width, axis=1))
    line = jnp.concatenate(vectors)
    line = jnp.pad(line, (0, width - line.shape[0]))
    parts.append(jnp.pad(line[None], ((0, VEC_ROWS - 1), (0, 0))))
    return jnp.concatenate(parts, axis=0)


def body(*args):
    tile_embeds, sentence_embeds, pairing = args[:3]
    visual_shards, textual_shards = args[3:16], args[16:27]
    sharpness_exponent, match_score_offset = args[27:]
    links = Links(lax.axis_size(AXES))
    count, half = links.count, links.half
    device = lax.axis_index(AXES)
    side, low = device // half, device % half
    on_images = side == 0
    side_word = jnp.reshape(side, (1,)).astype(jnp.int32)
    micro, images, seq_len, width = tile_embeds.shape
    captions, text_len = sentence_embeds.shape[1:3]
    own_rows = micro * images * seq_len
    text_rows = micro * captions * text_len
    row_shards = visual_shards[2].shape[0]

    (v_gain_a, v_shift_a, v_triple, v_merge, v_gain_b, v_shift_b, v_expand, v_shrink) = (
        visual_shards[:8]
    )
    pool_gain, pool_shift, probe, keyval, pool_out = visual_shards[8:]
    (t_gain_a, t_shift_a, t_triple, t_merge, t_gain_b, t_shift_b, t_expand, t_shrink) = (
        textual_shards[:8]
    )
    final_gain, final_shift, readout = textual_shards[8:]
    visual_block = tower_block(
        (v_triple, v_merge, v_expand, v_shrink, keyval, pool_out),
        (v_gain_a, v_shift_a, v_gain_b, v_shift_b, pool_gain, pool_shift, probe),
        row_shards,
        width,
    )
    textual_block = tower_block(
        (t_triple, t_merge, t_expand, t_shrink, None, None, readout),
        (t_gain_a, t_shift_a, t_gain_b, t_shift_b, final_gain, final_shift),
        row_shards,
        width,
    )
    own_block = jnp.where(on_images, visual_block, textual_block)
    their_block = links.swap(jnp.where(on_images, textual_block, visual_block), half)
    chain_rows = CHAIN_BLOCKS * row_shards
    gathered = []
    for chain, order in enumerate(links.orders):
        stop = (chain + 1) * chain_rows + (VEC_ROWS if chain == 2 else 0)
        rows = slice(chain * chain_rows, stop)
        pieces, masks = gather_chain(links, order, jnp.stack((own_block[rows], their_block[rows])))
        gathered.append(unpack_chain(links, device, pieces, masks))

    patch_rows = tile_embeds.reshape(own_rows, width)
    token_rows = jnp.pad(
        sentence_embeds.reshape(text_rows, width), ((0, own_rows - text_rows), (0, 0))
    )
    kept_rows = jnp.where(on_images, patch_rows, token_rows)
    moved_rows = links.swap(jnp.where(on_images, token_rows, patch_rows), half)

    def block_of(index):
        chain, place = divmod(index, CHAIN_BLOCKS)
        return gathered[chain][:, place * row_shards : (place + 1) * row_shards]

    def columns(first, many):
        return jnp.concatenate(
            [block_of(first + k).reshape(width, width) for k in range(many)], axis=1
        )

    triple, merge, expand = columns(0, 3), columns(3, 1), columns(4, 4)
    shrink = jnp.concatenate([block_of(8 + k) for k in range(4)], axis=1).reshape(4 * width, width)
    pool_keyval, head_matrix = columns(12, 2), columns(14, 1)
    lines = gathered[2][:, chain_rows, : 7 * row_shards].reshape(count, 7, row_shards)
    vectors = jnp.transpose(lines, (1, 0, 2)).reshape(7, width).astype(F32)
    gain_a, shift_a, gain_b, shift_b, gain_c, shift_c, probe_line = [vectors[k] for k in range(7)]

    inputs = jnp.concatenate((kept_rows, moved_rows), axis=0).astype(F32)
    hat_a, inverse_a = normalize_rows(inputs)
    normed_a = (hat_a * gain_a + shift_a).astype(LOW)
    triples = dot(normed_a, triple, 1, 0).astype(LOW)
    mixed = attend(side_word, triples, seq_len, text_len)
    middle = inputs + dot(mixed, merge, 1, 0)
    hat_b, inverse_b = normalize_rows(middle)
    normed_b = (hat_b * gain_b + shift_b).astype(LOW)
    upward = dot(normed_b, expand, 1, 0)
    active = gelu_tanh(upward).astype(LOW)
    hidden = middle + dot(active, shrink, 1, 0)

    total_rows = 2 * own_rows
    group_count = total_rows // seq_len
    caption_slots = total_rows // text_len
    heads = width // HD
    hat_c, inverse_c = normalize_rows(hidden)
    normed_c = (hat_c * gain_c + shift_c).astype(LOW)
    pairs = dot(normed_c, pool_keyval, 1, 0).astype(LOW)
    keys, values = pairs[:, :width], pairs[:, width:]
    lane = lax.broadcasted_iota(jnp.int32, (width, 128), 0) // HD
    spread = lane == lax.broadcasted_iota(jnp.int32, (width, 128), 1)
    probe_map = jnp.where(spread, probe_line[:, None], 0.0).astype(LOW)
    spread_low = spread.astype(LOW)
    scores = (dot(keys, probe_map, 1, 0) * SCALE).reshape(group_count, seq_len, 128)
    row_exp = jnp.exp(scores - jnp.max(scores, axis=1, keepdims=True))
    pool_full = row_exp / jnp.sum(row_exp, axis=1, keepdims=True)
    pool_probs = pool_full.astype(LOW).reshape(total_rows, 128)
    probs_wide = dot(pool_probs, spread_low, 1, 1)
    pooled = jnp.sum((probs_wide * values).reshape(group_count, seq_len, width), axis=1)
    pooled = jnp.pad(pooled.astype(LOW), ((0, caption_slots - group_count), (0, 0)))
    last_rows = normed_c.reshape(caption_slots, text_len, width)[:, -1]
    head_in = jnp.where(on_images, pooled, last_rows)
    raw = dot(head_in, head_matrix, 1, 0)
    length_inverse = lax.rsqrt(jnp.sum(raw * raw, axis=-1, keepdims=True) + 1e-06)
    unit = raw * length_inverse

    their_unit = links.swap(unit, half)
    image_units = jnp.where(on_images, unit, their_unit)[:group_count]
    text_units = jnp.where(on_images, their_unit, unit)
    own_texts = micro * captions
    caption_half = caption_slots // 2
    text_units = jnp.concatenate(
        (text_units[:own_texts], text_units[caption_half : caption_half + own_texts]), axis=0
    )
    held = jnp.concatenate((image_units, text_units), axis=0).astype(LOW)[None]
    masks = [0]
    for bit in links.orders[0] + [links.core]:
        held = jnp.concatenate((held, links.swap(held, bit)), axis=0)
        masks = masks + [mask ^ bit for mask in masks]
    slot_device = jnp.array(masks, jnp.int32) ^ low
    image_side = jnp.arange(2, dtype=jnp.int32)
    image_device = image_side[None, :] * half + slot_device[:, None]
    text_device = (1 - image_side)[None, :] * half + slot_device[:, None]
    steps = jnp.arange(micro, dtype=jnp.int32)[None, None, :, None]
    all_images, all_captions = count * images, count * captions
    image_row = (steps * count + image_device[:, :, None, None]) * images + jnp.arange(images)
    text_row = (steps * count + text_device[:, :, None, None]) * captions + jnp.arange(captions)
    image_row, text_row = image_row.reshape(-1), text_row.reshape(-1)
    held_images = held[:, :group_count].reshape(-1, width)
    held_texts = held[:, group_count:].reshape(-1, width)
    image_pick = jnp.arange(micro * all_images)[:, None] == image_row[None, :]
    text_pick = jnp.arange(micro * all_captions)[:, None] == text_row[None, :]
    images_low = dot(image_pick.astype(LOW), held_images, 1, 0).astype(LOW)
    texts_low = dot(text_pick.astype(LOW), held_texts, 1, 0).astype(LOW)

    sharpness_factor = jnp.exp(sharpness_exponent[0])
    cosine = dot(images_low, texts_low, 1, 1)
    image_at = jnp.arange(micro * all_images)
    text_at = jnp.arange(micro * all_captions)
    together = (image_at // all_images)[:, None] == (text_at // all_captions)[None, :]
    matched = pairing.reshape(-1)[None, :] == (image_at % all_images)[:, None]
    signs = jnp.where(matched, 1.0, -1.0)
    logits = sharpness_factor * cosine + match_score_offset[0]
    objective = jnp.sum(jnp.where(together, jax.nn.softplus(-signs * logits), 0.0))
    grad_logits = jnp.where(together, -signs * jax.nn.sigmoid(-signs * logits), 0.0)
    sharpness_grad = jnp.sum(grad_logits * cosine) * sharpness_factor
    offset_grad = jnp.sum(grad_logits)
    grad_cosine = (sharpness_factor * grad_logits).astype(LOW)
    own_images = jnp.pad(image_row[:group_count], (0, caption_slots - group_count), constant_values=-1)
    own_captions = text_row[: 2 * own_texts]
    gap = jnp.full((caption_half - own_texts,), -1, jnp.int32)
    own_captions = jnp.concatenate((own_captions[:own_texts], gap, own_captions[own_texts:], gap))
    pick_images = (own_images[:, None] == image_at[None, :]).astype(LOW)
    pick_texts = (own_captions[:, None] == text_at[None, :]).astype(LOW)
    from_texts = dot(dot(pick_images, grad_cosine, 1, 0).astype(LOW), texts_low, 1, 0)
    from_images = dot(dot(pick_texts, grad_cosine, 1, 1).astype(LOW), images_low, 1, 0)
    grad_unit = jnp.where(on_images, from_texts, from_images)

    grad_raw = length_inverse * (grad_unit - unit * jnp.sum(grad_unit * unit, axis=-1, keepdims=True))
    grad_raw = grad_raw.astype(LOW)
    grad_head = dot(head_in, grad_raw, 0, 0).astype(LOW)
    grad_head_in = dot(grad_raw, head_matrix, 1, 1)
    grad_pooled = grad_head_in[:group_count].astype(LOW)
    pooled_wide = jnp.broadcast_to(grad_pooled[:, None], (group_count, seq_len, width))
    pooled_wide = pooled_wide.reshape(total_rows, width)
    grad_values = probs_wide * pooled_wide
    pooled_map = jnp.where(spread[None], grad_pooled[:, :, None], 0.0).astype(LOW)
    grad_probs = lax.dot_general(
        values.reshape(group_count, seq_len, width),
        pooled_map,
        (((2,), (1,)), ((0,), (0,))),
        preferred_element_type=F32,
    )
    delta = jnp.sum(grad_probs * pool_full, axis=1, keepdims=True)
    grad_scores = (pool_full * (grad_probs - delta)).astype(LOW).reshape(total_rows, 128)
    grad_keys = dot(grad_scores, probe_map, 1, 1) * SCALE
    grad_probe = jnp.sum(jnp.where(spread, dot(keys, grad_scores, 0, 0), 0.0), axis=1) * SCALE
    grad_pairs = jnp.concatenate((grad_keys.astype(LOW), grad_values.astype(LOW)), axis=1)
    grad_keyval = dot(normed_c, grad_pairs, 0, 0).astype(LOW)
    pool_side = dot(grad_pairs, pool_keyval, 1, 1)
    text_side = jnp.pad(grad_head_in[:, None], ((0, 0), (text_len - 1, 0), (0, 0)))
    grad_normed_c = jnp.where(on_images, pool_side, text_side.reshape(total_rows, width))
    grad_gain_c = jnp.sum(grad_normed_c * hat_c, axis=0)
    grad_shift_c = jnp.sum(grad_normed_c, axis=0)
    grad_hidden = normalize_back(grad_normed_c * gain_c, hat_c, inverse_c)

    grad_low = grad_hidden.astype(LOW)
    grad_shrink = dot(active, grad_low, 0, 0).astype(LOW)
    grad_up = (dot(grad_low, shrink, 1, 1) * gelu_slope(upward)).astype(LOW)
    grad_expand = dot(normed_b, grad_up, 0, 0).astype(LOW)
    grad_normed_b = dot(grad_up, expand, 1, 1)
    grad_gain_b = jnp.sum(grad_normed_b * hat_b, axis=0)
    grad_shift_b = jnp.sum(grad_normed_b, axis=0)
    grad_middle = grad_hidden + normalize_back(grad_normed_b * gain_b, hat_b, inverse_b)
    grad_branch = grad_middle.astype(LOW)
    grad_merge = dot(mixed, grad_branch, 0, 0).astype(LOW)
    grad_mixed = dot(grad_branch, merge, 1, 1).astype(LOW)
    grad_triples = attend_back(side_word, triples, grad_mixed, seq_len, text_len)
    grad_triple = dot(normed_a, grad_triples, 0, 0).astype(LOW)
    grad_normed_a = dot(grad_triples, triple, 1, 1)
    grad_gain_a = jnp.sum(grad_normed_a * hat_a, axis=0)
    grad_shift_a = jnp.sum(grad_normed_a, axis=0)
    grad_inputs = grad_middle + normalize_back(grad_normed_a * gain_a, hat_a, inverse_a)

    def rows_of(grad):
        return [
            item.reshape(count, row_shards, width)
            for item in jnp.split(grad, grad.shape[1] // width, axis=1)
        ]

    shrink_rows = grad_shrink.reshape(count, 4 * row_shards, width)
    grad_lines = jnp.stack(
        (grad_gain_a, grad_shift_a, grad_gain_b, grad_shift_b, grad_gain_c, grad_shift_c, grad_probe)
    )
    grad_lines = jnp.transpose(grad_lines.reshape(7, count, row_shards), (1, 0, 2))
    grad_lines = grad_lines.reshape(count, 1, 7 * row_shards).astype(LOW)
    grad_lines = jnp.pad(grad_lines, ((0, 0), (0, VEC_ROWS - 1), (0, width - 7 * row_shards)))
    whole = jnp.concatenate(
        rows_of(grad_triple)
        + rows_of(grad_merge)
        + rows_of(grad_expand)
        + [shrink_rows]
        + rows_of(grad_keyval)
        + rows_of(grad_head)
        + [grad_lines],
        axis=1,
    )
    summed = []
    for chain, order in enumerate(links.orders):
        stop = (chain + 1) * chain_rows + (VEC_ROWS if chain == 2 else 0)
        keep, send = pack_chain(links, device, order, whole[:, chain * chain_rows : stop])
        summed.append(scatter_chain(links, order, keep, send))
    summed = jnp.concatenate(summed, axis=1)
    crossed = links.swap(summed[1].astype(LOW), half).astype(F32)
    visual_sum = jnp.where(on_images, summed[0], crossed)
    textual_sum = jnp.where(on_images, crossed, summed[0])

    def outputs_of(total, names):
        def cols(first, many):
            return jnp.concatenate(
                [total[(first + k) * row_shards : (first + k + 1) * row_shards] for k in range(many)],
                axis=1,
            )

        line = total[BLOCKS * row_shards]
        vec = [line[k * row_shards : (k + 1) * row_shards] for k in range(7)]
        layer = (
            vec[0],
            vec[1],
            cols(0, 3),
            cols(3, 1),
            vec[2],
            vec[3],
            cols(4, 4),
            total[8 * row_shards : 12 * row_shards],
        )
        if names == 0:
            return layer + (vec[4], vec[5], vec[6], cols(12, 2), cols(14, 1))
        return layer + (vec[4], vec[5], cols(14, 1))

    returned = links.swap(grad_inputs[own_rows:].astype(LOW), half).astype(F32)
    kept = grad_inputs[:own_rows]
    patches_grad = jnp.where(on_images, kept, returned).reshape(tile_embeds.shape)
    captions_grad = jnp.where(on_images, returned[:text_rows], kept[:text_rows])
    own_group = group_count // 2
    image_embedding = jnp.where(on_images, unit[:own_group], their_unit[own_group:group_count])
    text_embedding = jnp.where(
        on_images, their_unit[caption_half : caption_half + own_texts], unit[:own_texts]
    )
    return (
        image_embedding.reshape(micro, images, width),
        text_embedding.reshape(micro, captions, width),
        objective / (micro * all_images),
        patches_grad,
        captions_grad.reshape(sentence_embeds.shape),
        *outputs_of(visual_sum, 0),
        *outputs_of(textual_sum, 1),
        jnp.reshape(sharpness_grad, (1,)),
        jnp.reshape(offset_grad, (1,)),
    )


def solution(mesh):
    row, matrix, batch, rest = P(AXES), P(AXES, None), P(None, AXES, None, None), P()
    layer = (row, row, matrix, matrix, row, row, matrix, matrix)
    visual = layer + (row, row, row, matrix, matrix)
    textual = layer + (row, row, matrix)
    in_specs = (batch, batch, rest) + visual + textual + (rest, rest)
    embed = P(None, AXES, None)
    out_specs = (embed, embed, rest, batch, batch) + visual + textual + (rest, rest)
    return jax.shard_map(body, mesh=mesh, in_specs=in_specs, out_specs=out_specs, check_vma=False)
```

profile of v0, /device:TPU:0, one launch (start us, length us, event | category | flops | bytes accessed | tf_op | source)
XLA Modules:
  0.0 671.6 jit_solution(7615394674091067394)
XLA Ops:
  0.7 4.2 concatenate.145
  4.9 4.8 concatenate.142
  28.0 4.1 collective-permute-start.1
  39.2 35.8 %collective-permute-done.1 = bf16[368,768]{1,0:T(8,128)(2,1)} collective-permute-done((bf16[368,768]{1,0:T(8,128)(2,1)}, bf16[368,768]{1,0:T(8,128)(2,1)}, u32[]{:S(2)}, u32[]{:S(2)}) %collective-permute-start.1) | collective-permute-done | bytes 565280 | tf_op jit(solution)/shard_map/ppermute | solution.py:161
  78.7 6.4 collective-permute-done.7
  90.5 14.1 %collective-permute-done.8 = bf16[2,2,120,768]{3,2,1,0:T(8,128)(2,1)S(1)} collective-permute-done((bf16[2,2,120,768]{3,2,1,0:T(8,128)(2,1)S(1)}, bf16[2,2,120,768]{3,2,1,0:T(8,128)(2,1)S(1)}, u32[]{:S(2)}, u32[]{:S(2)}) %collective-permute-start.8) | collective-permute-done | bytes 737312 | tf_op jit(solution)/shard_map/ppermute | solution.py:161
  105.4 3.7 collective-permute-done.12
  116.5 13.1 %collective-permute-done.13 = bf16[2,2,120,768]{3,2,1,0:T(8,128)(2,1)S(1)} collective-permute-done((bf16[2,2,120,768]{3,2,1,0:T(8,128)(2,1)S(1)}, bf16[2,2,120,768]{3,2,1,0:T(8,128)(2,1)S(1)}, u32[]{:S(2)}, u32[]{:S(2)}) %collective-permute-start.13) | collective-permute-done | bytes 737312 | tf_op jit(solution)/shard_map/ppermute | solution.py:161
  137.0 21.7 %collective-permute-done.9 = bf16[4,2,120,768]{3,2,1,0:T(8,128)(2,1)S(1)} collective-permute-done((bf16[4,2,120,768]{3,2,1,0:T(8,128)(2,1)S(1)}, bf16[4,2,120,768]{3,2,1,0:T(8,128)(2,1)S(1)}, u32[]{:S(2)}, u32[]{:S(2)}) %collective-permute-start.9) | collective-permute-done | bytes 1474592 | tf_op jit(solution)/shard_map/ppermute | solution.py:161
  176.6 6.1 gather_fusion.4
  182.8 5.9 copy_select_fusion.1
  190.0 6.1 gather_fusion.5
  199.4 3.3 select_bitcast_fusion.7
  210.9 6.4 gather_fusion.1
  217.3 3.5 broadcast_select_fusion
  226.3 4.3 fusion.8
  231.5 6.2 convolution_convert_fusion.q_ref.k_ref.v_ref
  237.7 26.5 %attend.1 = bf16[1024,768]{1,0:T(8,128)(2,1)} custom-call(s32[1]{0:T(128)} %bitcast.2.side_ref, bf16[1024,2304]{1,0:T(8,128)(2,1)} %convolution_convert_fusion.q_ref.k_ref.v_ref, bf16[1024,2304]{1,0:T(8,128)(2,1)} %convolution_convert_fusion.q_ref.k_ref.v_ref, bf16[1024,2304]{1,0:T(8,128)(2,1)} %convolution_convert_fusion.q_ref.k_ref.v_ref), custom_call_target="tpu_custom_call" | custom-call | flops 805306368 | bytes 6291456 | tf_op jit(solution)/shard_map/attend/pallas_call | solution.py:109
  270.2 9.7 %fusion.53 = f32[1024,3072]{1,0:T(8,128)} fusion(bf16[768,768]{1,0:T(8,128)(2,1)S(1)} %bitcast.264, bf16[768,768]{1,0:T(8,128)(2,1)S(1)} %bitcast.266, bf16[768,768]{1,0:T(8,128)(2,1)S(1)} %bitcast.262, bf16[768,768]{1,0:T(8,128)(2,1)S(1)} %bitcast.268, f32[1024,768]{1,0:T(8,128)S(1)} %get-tuple-element.248, f32[768]{0:T(1024)S(1)} %add.351, ...), kind=kOutput, calls=%fused_computation.176 | convolution fusion | flops 4854644736 | bytes 20461568 | tf_op jit(solution)/shard_map/dot_general | solution.py:24
  279.8 10.6 %fusion.122 = (f32[1024]{0:T(1024)S(1)}, f32[1024,768]{1,0:T(8,128)S(1)}) fusion(f32[1024,768]{1,0:T(8,128)S(1)} %get-tuple-element.248, bf16[3072,768]{1,0:T(8,128)(2,1)S(1)} %bitcast.238, f32[1024,3072]{1,0:T(8,128)} %fusion.53), kind=kOutput, calls=%fused_computation.453 | convolution fusion | flops 4861721600 | bytes 23597056 | tf_op jit(solution)/shard_map/dot_general | solution.py:24
  300.8 3.4 collective-permute-start.17
  360.4 4.1 convolution_convert_fusion.5
  364.9 3.4 multiply_reduce_fusion
  369.5 13.0 %fusion.7 = bf16[1024,3072]{1,0:T(8,128)(2,1)S(1)} fusion(f32[1024,3072]{1,0:T(8,128)} %fusion.53, bf16[3072,768]{1,0:T(8,128)(2,1)S(1)} %bitcast.241, f32[1024,768]{1,0:T(8,128)S(1)} %subtract_multiply_fusion), kind=kOutput, calls=%fused_computation.21 | convolution fusion | flops 4892393472 | bytes 26738688 | tf_op jit(solution)/shard_map/dot_general | solution.py:24
  382.6 12.0 %convolution_convert_fusion.1 = bf16[3072,768]{1,0:T(8,128)(2,1)} fusion(f32[1024,768]{1,0:T(8,128)S(1)} %subtract_multiply_fusion, f32[1024,3072]{1,0:T(8,128)} %fusion.53), kind=kOutput, calls=%fused_computation.45 | convolution fusion | flops 4863295488 | bytes 20447232 | tf_op jit(solution)/shard_map/dot_general | solution.py:24
  394.7 5.8 multiply_reduce_fusion.1
  400.6 8.3 %convolution_convert_fusion.2 = bf16[768,3072]{1,0:T(8,128)(2,1)} fusion(bf16[1024,3072]{1,0:T(8,128)(2,1)S(1)} %fusion.7, f32[1024,768]{1,0:T(8,128)S(1)} %copy-done.10, f32[768]{0:T(1024)S(1)} %copy-done.115, f32[768]{0:T(1024)S(1)} %copy-done.100, f32[1024]{0:T(1024)S(1)} %copy-done.102, f32[1024]{0:T(1024)S(1)} %copy-done.92), kind=kOutput, calls=%fused_computation.46 | convolution fusion | flops 4838129664 | bytes 14170112 | tf_op jit(solution)/shard_map/dot_general | solution.py:24
  417.3 4.3 fusion.115
  421.8 36.7 %attend_back.1 = bf16[1024,2304]{1,0:T(8,128)(2,1)} custom-call(s32[1]{0:T(128)} %bitcast.2.side_ref, bf16[1024,2304]{1,0:T(8,128)(2,1)} %convolution_convert_fusion.q_ref.k_ref.v_ref, bf16[1024,2304]{1,0:T(8,128)(2,1)} %convolution_convert_fusion.q_ref.k_ref.v_ref, bf16[1024,2304]{1,0:T(8,128)(2,1)} %convolution_convert_fusion.q_ref.k_ref.v_ref, ...), custom_call_target="tpu_custom_call" | custom-call | flops 2013265920 | bytes 11010048 | tf_op jit(solution)/shard_map/attend_back/pallas_call | solution.py:131
  458.6 7.0 %convolution_convert_fusion.3 = bf16[768,2304]{1,0:T(8,128)(2,1)S(1)} fusion(bf16[1024,2304]{1,0:T(8,128)(2,1)} %attend_back.1, f32[768]{0:T(1024)S(1)} %copy-done.113, f32[768]{0:T(1024)S(1)} %copy-done.96, f32[1024]{0:T(1024)S(1)} %copy-done.98, f32[1024]{0:T(1024)S(1)} %copy-done.88, bf16[512,768]{1,0:T(8,128)(2,1)S(1)} %copy-done.25, ...), kind=kOutput, calls=%fused_computation.47 | convolution fusion | flops 3632726016 | bytes 9844736 | tf_op jit(solution)/shard_map/dot_general | solution.py:24
  470.0 6.0 fusion.21
  476.4 5.2 constant_dynamic-update-slice_fusion.63
  486.8 3.5 gather_fusion.9
  496.7 4.5 select_bitcast_fusion.1
  507.4 5.1 gather_fusion.7
  512.5 3.9 broadcast_select_fusion.5
  520.1 3.7 gather_fusion.11
  526.7 5.0 gather_fusion.8
  531.7 3.5 gather_fusion.10
  535.2 5.0 gather_fusion.6
  559.2 20.9 %collective-permute-done.28 = bf16[4,2,120,768]{3,2,1,0:T(8,128)(2,1)S(1)} collective-permute-done((bf16[4,2,120,768]{3,2,1,0:T(8,128)(2,1)S(1)}, bf16[4,2,120,768]{3,2,1,0:T(8,128)(2,1)S(1)}, u32[]{:S(2)}, u32[]{:S(2)}) %collective-permute-start.28) | collective-permute-done | bytes 1474592 | tf_op jit(solution)/shard_map/ppermute | solution.py:161
  585.0 15.6 %collective-permute-done.24 = bf16[4,2,120,768]{3,2,1,0:T(8,128)(2,1)S(1)} collective-permute-done((bf16[4,2,120,768]{3,2,1,0:T(8,128)(2,1)S(1)}, bf16[4,2,120,768]{3,2,1,0:T(8,128)(2,1)S(1)}, u32[]{:S(2)}, u32[]{:S(2)}) %collective-permute-start.24) | collective-permute-done | bytes 1474592 | tf_op jit(solution)/shard_map/ppermute | solution.py:161
  618.2 4.1 collective-permute-done.25
  624.7 4.7 collective-permute-done.33
  630.9 3.9 collective-permute-done.26
  634.9 6.1 collective-permute-done.34
  641.3 4.0 collective-permute-start.35
  648.9 12.3 %collective-permute-done.35 = bf16[368,768]{1,0:T(8,128)(2,1)S(1)} collective-permute-done((bf16[368,768]{1,0:T(8,128)(2,1)S(1)}, bf16[368,768]{1,0:T(8,128)(2,1)S(1)}, u32[]{:S(2)}, u32[]{:S(2)}) %collective-permute-start.35) | collective-permute-done | bytes 565280 | tf_op jit(solution)/shard_map/ppermute | solution.py:161
  (606 shorter events, 251.7 us)
Async XLA Ops:
  28.0 47.0 %collective-permute-start.1 = (bf16[368,768]{1,0:T(8,128)(2,1)}, bf16[368,768]{1,0:T(8,128)(2,1)}, u32[]{:S(2)}, u32[]{:S(2)}) collective-permute-start(bf16[368,768]{1,0:T(8,128)(2,1)} %get-tuple-element.234), channel_id=1, source_target_pairs={{0,16},{1,17},{2,18},{3,19},{4,20},{5,21},{6,22},{7,23},{8,24},{9,... | collective-permute-start | bytes 1695752 | tf_op jit(solution)/shard_map/ppermute | solution.py:161
  32.5 98.8 %copy-start.4 = (bf16[512,768]{1,0:T(8,128)(2,1)}, bf16[512,768]{1,0:T(8,128)(2,1)S(1)}, u32[]{:S(2)}) copy-start(bf16[512,768]{1,0:T(8,128)(2,1)S(1)} %get-tuple-element.198) | copy-start | bytes 2359300
  32.5 83.7 %collective-permute-start = (bf16[512,768]{1,0:T(8,128)(2,1)S(1)}, bf16[512,768]{1,0:T(8,128)(2,1)S(1)}, u32[]{:S(2)}, u32[]{:S(2)}) collective-permute-start(bf16[512,768]{1,0:T(8,128)(2,1)S(1)} %get-tuple-element.199), channel_id=1, source_target_pairs={{0,16},{1,17},{2,18},{3,19},{4,20},{5,21},{6,22},{7,23},{8,24},{9,... | collective-permute-start | bytes 2359304 | tf_op jit(solution)/shard_map/ppermute | solution.py:161
  76.1 9.0 %collective-permute-start.7 = (bf16[1,2,120,768]{3,2,1,0:T(8,128)(2,1)S(1)}, bf16[1,2,120,768]{3,2,1,0:T(8,128)(2,1)S(1)}, u32[]{:S(2)}, u32[]{:S(2)}) collective-permute-start(bf16[1,2,120,768]{3,2,1,0:T(8,128)(2,1)S(1)} %maximum_bitcast_fusion.1), channel_id=1, source_target_pairs={{0,1},{1,0},{2,3},{3,2},{4,5},{5,4},{6,7},{7,6},{8,9},{9,8},{10,11... | collective-permute-start | bytes 1105928 | tf_op jit(solution)/shard_map/ppermute | solution.py:161
  78.0 219.9 %copy-start.103 = (pred[768]{0:T(1024)(128)(4,1)}, pred[768]{0:T(1024)(128)(4,1)S(1)}, u32[]{:S(2)}) copy-start(pred[768]{0:T(1024)(128)(4,1)S(1)} %fusion.92) | copy-start | bytes 2308
  78.0 219.9 %copy-start.81 = (s32[768]{0:T(1024)}, s32[768]{0:T(1024)S(1)}, u32[]{:S(2)}) copy-start(s32[768]{0:T(1024)S(1)} %get-tuple-element.270) | copy-start | bytes 9220
  78.0 219.9 %copy-start.83 = (s32[768]{0:T(1024)}, s32[768]{0:T(1024)S(1)}, u32[]{:S(2)}) copy-start(s32[768]{0:T(1024)S(1)} %get-tuple-element.271) | copy-start | bytes 9220
  85.2 19.4 %collective-permute-start.8 = (bf16[2,2,120,768]{3,2,1,0:T(8,128)(2,1)S(1)}, bf16[2,2,120,768]{3,2,1,0:T(8,128)(2,1)S(1)}, u32[]{:S(2)}, u32[]{:S(2)}) collective-permute-start(bf16[2,2,120,768]{3,2,1,0:T(8,128)(2,1)S(1)} %pad_maximum_fusion.33), channel_id=1, source_target_pairs={{0,4},{1,5},{2,6},{3,7},{4,0},{5,1},{6,2},{7,3},{8,12},{9,13},{10,... | collective-permute-start | bytes 2211848 | tf_op jit(solution)/shard_map/ppermute | solution.py:161
  87.2 21.9 %collective-permute-start.12 = (bf16[1,2,120,768]{3,2,1,0:T(8,128)(2,1)S(1)}, bf16[1,2,120,768]{3,2,1,0:T(8,128)(2,1)S(1)}, u32[]{:S(2)}, u32[]{:S(2)}) collective-permute-start(bf16[1,2,120,768]{3,2,1,0:T(8,128)(2,1)S(1)} %maximum_bitcast_fusion.2), channel_id=1, source_target_pairs={{0,4},{1,5},{2,6},{3,7},{4,0},{5,1},{6,2},{7,3},{8,12},{9,13},{10,... | collective-permute-start | bytes 1105928 | tf_op jit(solution)/shard_map/ppermute | solution.py:161
  89.0 24.8 %collective-permute-start.2 = (bf16[1,2,128,768]{3,2,1,0:T(8,128)(2,1)S(1)}, bf16[1,2,128,768]{3,2,1,0:T(8,128)(2,1)S(1)}, u32[]{:S(2)}, u32[]{:S(2)}) collective-permute-start(bf16[1,2,128,768]{3,2,1,0:T(8,128)(2,1)S(1)} %maximum_bitcast_fusion), channel_id=1, source_target_pairs={{0,8},{1,9},{2,10},{3,11},{4,12},{5,13},{6,14},{7,15},{8,0},{9,1},... | collective-permute-start | bytes 1179656 | tf_op jit(solution)/shard_map/ppermute | solution.py:161
  104.7 29.8 %collective-permute-start.10 = (bf16[4,2,120,768]{3,2,1,0:T(8,128)(2,1)S(1)}, bf16[4,2,120,768]{3,2,1,0:T(8,128)(2,1)S(1)}, u32[]{:S(2)}, u32[]{:S(2)}) collective-permute-start(bf16[4,2,120,768]{3,2,1,0:T(8,128)(2,1)S(1)} %pad_maximum_fusion.21), channel_id=1, source_target_pairs={{0,2},{1,3},{2,0},{3,1},{4,6},{5,7},{6,4},{7,5},{8,10},{9,11},{10,... | collective-permute-start | bytes 4423688 | tf_op jit(solution)/shard_map/ppermute | solution.py:161
  109.2 20.4 %collective-permute-start.13 = (bf16[2,2,120,768]{3,2,1,0:T(8,128)(2,1)S(1)}, bf16[2,2,120,768]{3,2,1,0:T(8,128)(2,1)S(1)}, u32[]{:S(2)}, u32[]{:S(2)}) collective-permute-start(bf16[2,2,120,768]{3,2,1,0:T(8,128)(2,1)S(1)} %pad_maximum_fusion.34), channel_id=1, source_target_pairs={{0,8},{1,9},{2,10},{3,11},{4,12},{5,13},{6,14},{7,15},{8,0},{9,1},... | collective-permute-start | bytes 2211848 | tf_op jit(solution)/shard_map/ppermute | solution.py:161
  113.0 45.7 %collective-permute-start.9 = (bf16[4,2,120,768]{3,2,1,0:T(8,128)(2,1)S(1)}, bf16[4,2,120,768]{3,2,1,0:T(8,128)(2,1)S(1)}, u32[]{:S(2)}, u32[]{:S(2)}) collective-permute-start(bf16[4,2,120,768]{3,2,1,0:T(8,128)(2,1)S(1)} %pad_maximum_fusion.21), channel_id=1, source_target_pairs={{0,8},{1,9},{2,10},{3,11},{4,12},{5,13},{6,14},{7,15},{8,0},{9,1},... | collective-permute-start | bytes 4423688 | tf_op jit(solution)/shard_map/ppermute | solution.py:161
  113.9 20.5 %collective-permute-start.3 = (bf16[2,2,128,768]{3,2,1,0:T(8,128)(2,1)S(1)}, bf16[2,2,128,768]{3,2,1,0:T(8,128)(2,1)S(1)}, u32[]{:S(2)}, u32[]{:S(2)}) collective-permute-start(bf16[2,2,128,768]{3,2,1,0:T(8,128)(2,1)S(1)} %pad_maximum_fusion.32), channel_id=1, source_target_pairs={{0,1},{1,0},{2,3},{3,2},{4,5},{5,4},{6,7},{7,6},{8,9},{9,8},{10,11... | collective-permute-start | bytes 2359304 | tf_op jit(solution)/shard_map/ppermute | solution.py:161
  116.5 114.1 %copy-start.87 = (f32[1024]{0:T(1024)}, f32[1024]{0:T(1024)S(1)}, u32[]{:S(2)}) copy-start(f32[1024]{0:T(1024)S(1)} %broadcast_multiply_fusion.9) | copy-start | bytes 12292
  129.7 34.5 %collective-permute-start.14 = (bf16[4,2,120,768]{3,2,1,0:T(8,128)(2,1)S(1)}, bf16[4,2,120,768]{3,2,1,0:T(8,128)(2,1)S(1)}, u32[]{:S(2)}, u32[]{:S(2)}) collective-permute-start(bf16[4,2,120,768]{3,2,1,0:T(8,128)(2,1)S(1)} %pad_maximum_fusion.22), channel_id=1, source_target_pairs={{0,1},{1,0},{2,3},{3,2},{4,5},{5,4},{6,7},{7,6},{8,9},{9,8},{10,11... | collective-permute-start | bytes 4423688 | tf_op jit(solution)/shard_map/ppermute | solution.py:161
  131.9 35.4 %collective-permute-start.15 = (bf16[4,2,120,768]{3,2,1,0:T(8,128)(2,1)S(1)}, bf16[4,2,120,768]{3,2,1,0:T(8,128)(2,1)S(1)}, u32[]{:S(2)}, u32[]{:S(2)}) collective-permute-start(bf16[4,2,120,768]{3,2,1,0:T(8,128)(2,1)S(1)} %pad_maximum_fusion.22), channel_id=1, source_target_pairs={{0,2},{1,3},{2,0},{3,1},{4,6},{5,7},{6,4},{7,5},{8,10},{9,11},{10,... | collective-permute-start | bytes 4423688 | tf_op jit(solution)/shard_map/ppermute | solution.py:161
  134.5 39.6 %collective-permute-start.5 = (bf16[4,2,128,768]{3,2,1,0:T(8,128)(2,1)S(1)}, bf16[4,2,128,768]{3,2,1,0:T(8,128)(2,1)S(1)}, u32[]{:S(2)}, u32[]{:S(2)}) collective-permute-start(bf16[4,2,128,768]{3,2,1,0:T(8,128)(2,1)S(1)} %pad_maximum_fusion.18), channel_id=1, source_target_pairs={{0,2},{1,3},{2,0},{3,1},{4,6},{5,7},{6,4},{7,5},{8,10},{9,11},{10,... | collective-permute-start | bytes 4718600 | tf_op jit(solution)/shard_map/ppermute | solution.py:161
  134.6 36.9 %collective-permute-start.4 = (bf16[4,2,128,768]{3,2,1,0:T(8,128)(2,1)S(1)}, bf16[4,2,128,768]{3,2,1,0:T(8,128)(2,1)}, u32[]{:S(2)}, u32[]{:S(2)}) collective-permute-start(bf16[4,2,128,768]{3,2,1,0:T(8,128)(2,1)S(1)} %pad_maximum_fusion.18), channel_id=1, source_target_pairs={{0,4},{1,5},{2,6},{3,7},{4,0},{5,1},{6,2},{7,3},{8,12},{9,13},{10,... | collective-permute-start | bytes 4718600 | tf_op jit(solution)/shard_map/ppermute | solution.py:161
  136.2 94.4 %copy-start.97 = (f32[1024]{0:T(1024)}, f32[1024]{0:T(1024)S(1)}, u32[]{:S(2)}) copy-start(f32[1024]{0:T(1024)S(1)} %add_rsqrt_fusion.2) | copy-start | bytes 12292
  158.7 16.8 %collective-permute-start.11 = (bf16[4,2,120,768]{3,2,1,0:T(8,128)(2,1)S(1)}, bf16[4,2,120,768]{3,2,1,0:T(8,128)(2,1)S(1)}, u32[]{:S(2)}, u32[]{:S(2)}) collective-permute-start(bf16[4,2,120,768]{3,2,1,0:T(8,128)(2,1)S(1)} %collective-permute-done.9), channel_id=1, source_target_pairs={{0,2},{1,3},{2,0},{3,1},{4,6},{5,7},{6,4},{7,5},{8,10},{9,11},{10,... | collective-permute-start | bytes 4423688 | tf_op jit(solution)/shard_map/ppermute | solution.py:161
  164.2 24.4 %collective-permute-start.16 = (bf16[4,2,120,768]{3,2,1,0:T(8,128)(2,1)S(1)}, bf16[4,2,120,768]{3,2,1,0:T(8,128)(2,1)S(1)}, u32[]{:S(2)}, u32[]{:S(2)}) collective-permute-start(bf16[4,2,120,768]{3,2,1,0:T(8,128)(2,1)S(1)} %collective-permute-done.14), channel_id=1, source_target_pairs={{0,2},{1,3},{2,0},{3,1},{4,6},{5,7},{6,4},{7,5},{8,10},{9,11},{10,... | collective-permute-start | bytes 4423688 | tf_op jit(solution)/shard_map/ppermute | solution.py:161
  171.5 36.7 %collective-permute-start.6 = (bf16[4,2,128,768]{3,2,1,0:T(8,128)(2,1)}, bf16[4,2,128,768]{3,2,1,0:T(8,128)(2,1)}, u32[]{:S(2)}, u32[]{:S(2)}) collective-permute-start(bf16[4,2,128,768]{3,2,1,0:T(8,128)(2,1)} %collective-permute-done.4), channel_id=1, source_target_pairs={{0,2},{1,3},{2,0},{3,1},{4,6},{5,7},{6,4},{7,5},{8,10},{9,11},{10,... | collective-permute-start | bytes 4718600 | tf_op jit(solution)/shard_map/ppermute | solution.py:161
  225.6 70.3 %copy-start.109 = (bf16[768]{0:T(1024)(128)(2,1)}, bf16[768]{0:T(1024)(128)(2,1)S(1)}, u32[]{:S(2)}) copy-start(bf16[768]{0:T(1024)(128)(2,1)S(1)} %broadcast_in_dim.155) | copy-start | bytes 4612
  225.7 42.3 %copy-start.99 = (f32[768]{0:T(1024)}, f32[768]{0:T(1024)S(1)}, u32[]{:S(2)}) copy-start(f32[768]{0:T(1024)S(1)} %mul.336) | copy-start | bytes 9220
  225.9 65.1 %copy-start.89 = (f32[768]{0:T(1024)}, f32[768]{0:T(1024)S(1)}, u32[]{:S(2)}) copy-start(f32[768]{0:T(1024)S(1)} %mul.348) | copy-start | bytes 9220
  226.0 42.0 %copy-start.114 = (f32[768]{0:T(1024)}, f32[768]{0:T(1024)S(1)}, u32[]{:S(2)}) copy-start(f32[768]{0:T(1024)S(1)} %add.351) | copy-start | bytes 9220
  300.8 5.8 collective-permute-start.17
  307.9 4.5 collective-permute-start.18
  313.9 15.1 %collective-permute-start.19 = (bf16[2,16,768]{2,1,0:T(8,128)(2,1)}, bf16[2,16,768]{2,1,0:T(8,128)(2,1)}, u32[]{:S(2)}, u32[]{:S(2)}) collective-permute-start(bf16[2,16,768]{2,1,0:T(8,128)(2,1)} %pad_maximum_fusion.42), channel_id=1, source_target_pairs={{0,4},{1,5},{2,6},{3,7},{4,0},{5,1},{6,2},{7,3},{8,12},{9,13},{10,... | collective-permute-start | bytes 147464 | tf_op jit(solution)/shard_map/ppermute | solution.py:161
  329.8 4.7 collective-permute-start.20
  335.4 1.5 collective-permute-start.21
  421.8 36.8 %copy-start.7 = (bf16[512,768]{1,0:T(8,128)(2,1)S(1)}, bf16[512,768]{1,0:T(8,128)(2,1)}, u32[]{:S(2)}) copy-start(bf16[512,768]{1,0:T(8,128)(2,1)} %copy-done.4) | copy-start | bytes 2359300
  421.8 36.8 %copy-start.25 = (bf16[512,768]{1,0:T(8,128)(2,1)S(1)}, bf16[512,768]{1,0:T(8,128)(2,1)}, u32[]{:S(2)}) copy-start(bf16[512,768]{1,0:T(8,128)(2,1)} %copy-done.22) | copy-start | bytes 2359300
  492.4 51.4 %collective-permute-start.27 = (bf16[8,2,120,768]{3,2,1,0:T(8,128)(2,1)}, bf16[8,2,120,768]{3,2,1,0:T(8,128)(2,1)}, u32[]{:S(2)}, u32[]{:S(2)}) collective-permute-start(bf16[8,2,120,768]{3,2,1,0:T(8,128)(2,1)} %broadcast_select_fusion.3), channel_id=1, source_target_pairs={{0,2},{1,3},{2,0},{3,1},{4,6},{5,7},{6,4},{7,5},{8,10},{9,11},{10,... | collective-permute-start | bytes 8847368 | tf_op jit(solution)/shard_map/ppermute | solution.py:161
  516.5 30.1 %collective-permute-start.23 = (bf16[8,2,120,768]{3,2,1,0:T(8,128)(2,1)}, bf16[8,2,120,768]{3,2,1,0:T(8,128)(2,1)}, u32[]{:S(2)}, u32[]{:S(2)}) collective-permute-start(bf16[8,2,120,768]{3,2,1,0:T(8,128)(2,1)} %broadcast_select_fusion.5), channel_id=1, source_target_pairs={{0,2},{1,3},{2,0},{3,1},{4,6},{5,7},{6,4},{7,5},{8,10},{9,11},{10,... | collective-permute-start | bytes 8847368 | tf_op jit(solution)/shard_map/ppermute | solution.py:161
  525.9 24.7 %collective-permute-start.31 = (bf16[8,2,128,768]{3,2,1,0:T(8,128)(2,1)}, bf16[8,2,128,768]{3,2,1,0:T(8,128)(2,1)}, u32[]{:S(2)}, u32[]{:S(2)}) collective-permute-start(bf16[8,2,128,768]{3,2,1,0:T(8,128)(2,1)} %broadcast_select_fusion.1), channel_id=1, source_target_pairs={{0,2},{1,3},{2,0},{3,1},{4,6},{5,7},{6,4},{7,5},{8,10},{9,11},{10,... | collective-permute-start | bytes 9437192 | tf_op jit(solution)/shard_map/ppermute | solution.py:161
  545.4 34.6 %collective-permute-start.28 = (bf16[4,2,120,768]{3,2,1,0:T(8,128)(2,1)S(1)}, bf16[4,2,120,768]{3,2,1,0:T(8,128)(2,1)S(1)}, u32[]{:S(2)}, u32[]{:S(2)}) collective-permute-start(bf16[4,2,120,768]{3,2,1,0:T(8,128)(2,1)S(1)} %add_convert_fusion.3), channel_id=1, source_target_pairs={{0,1},{1,0},{2,3},{3,2},{4,5},{5,4},{6,7},{7,6},{8,9},{9,8},{10,11... | collective-permute-start | bytes 4423688 | tf_op jit(solution)/shard_map/ppermute | solution.py:161
  548.5 52.1 %collective-permute-start.24 = (bf16[4,2,120,768]{3,2,1,0:T(8,128)(2,1)S(1)}, bf16[4,2,120,768]{3,2,1,0:T(8,128)(2,1)S(1)}, u32[]{:S(2)}, u32[]{:S(2)}) collective-permute-start(bf16[4,2,120,768]{3,2,1,0:T(8,128)(2,1)S(1)} %add_convert_fusion.4), channel_id=1, source_target_pairs={{0,8},{1,9},{2,10},{3,11},{4,12},{5,13},{6,14},{7,15},{8,0},{9,1},... | collective-permute-start | bytes 4423688 | tf_op jit(solution)/shard_map/ppermute | solution.py:161
  552.4 51.7 %collective-permute-start.32 = (bf16[4,2,128,768]{3,2,1,0:T(8,128)(2,1)S(1)}, bf16[4,2,128,768]{3,2,1,0:T(8,128)(2,1)S(1)}, u32[]{:S(2)}, u32[]{:S(2)}) collective-permute-start(bf16[4,2,128,768]{3,2,1,0:T(8,128)(2,1)S(1)} %add_convert_fusion), channel_id=1, source_target_pairs={{0,4},{1,5},{2,6},{3,7},{4,0},{5,1},{6,2},{7,3},{8,12},{9,13},{10,... | collective-permute-start | bytes 4718600 | tf_op jit(solution)/shard_map/ppermute | solution.py:161
  556.1 55.4 %collective-permute-start.22 = (bf16[512,768]{1,0:T(8,128)(2,1)}, bf16[512,768]{1,0:T(8,128)(2,1)}, u32[]{:S(2)}, u32[]{:S(2)}) collective-permute-start(bf16[512,768]{1,0:T(8,128)(2,1)} %slice.918), channel_id=1, source_target_pairs={{0,16},{1,17},{2,18},{3,19},{4,20},{5,21},{6,22},{7,23},{8,24},{9,... | collective-permute-start | bytes 2359304 | tf_op jit(solution)/shard_map/ppermute | solution.py:161
  583.0 32.9 %collective-permute-start.29 = (bf16[2,2,120,768]{3,2,1,0:T(8,128)(2,1)}, bf16[2,2,120,768]{3,2,1,0:T(8,128)(2,1)}, u32[]{:S(2)}, u32[]{:S(2)}) collective-permute-start(bf16[2,2,120,768]{3,2,1,0:T(8,128)(2,1)} %slice.919), channel_id=1, source_target_pairs={{0,8},{1,9},{2,10},{3,11},{4,12},{5,13},{6,14},{7,15},{8,0},{9,1},... | collective-permute-start | bytes 2211848 | tf_op jit(solution)/shard_map/ppermute | solution.py:161
  603.5 18.8 %collective-permute-start.25 = (bf16[2,2,120,768]{3,2,1,0:T(8,128)(2,1)}, bf16[2,2,120,768]{3,2,1,0:T(8,128)(2,1)}, u32[]{:S(2)}, u32[]{:S(2)}) collective-permute-start(bf16[2,2,120,768]{3,2,1,0:T(8,128)(2,1)} %slice.920), channel_id=1, source_target_pairs={{0,4},{1,5},{2,6},{3,7},{4,0},{5,1},{6,2},{7,3},{8,12},{9,13},{10,... | collective-permute-start | bytes 2211848 | tf_op jit(solution)/shard_map/ppermute | solution.py:161
  608.6 20.7 %collective-permute-start.33 = (bf16[2,2,128,768]{3,2,1,0:T(8,128)(2,1)}, bf16[2,2,128,768]{3,2,1,0:T(8,128)(2,1)}, u32[]{:S(2)}, u32[]{:S(2)}) collective-permute-start(bf16[2,2,128,768]{3,2,1,0:T(8,128)(2,1)} %slice.917), channel_id=1, source_target_pairs={{0,1},{1,0},{2,3},{3,2},{4,5},{5,4},{6,7},{7,6},{8,9},{9,8},{10,11... | collective-permute-start | bytes 2359304 | tf_op jit(solution)/shard_map/ppermute | solution.py:161
  617.7 13.1 %collective-permute-start.30 = (bf16[1,2,120,768]{3,2,1,0:T(8,128)(2,1)S(1)}, bf16[1,2,120,768]{3,2,1,0:T(8,128)(2,1)S(1)}, u32[]{:S(2)}, u32[]{:S(2)}) collective-permute-start(bf16[1,2,120,768]{3,2,1,0:T(8,128)(2,1)S(1)} %slice.922), channel_id=1, source_target_pairs={{0,4},{1,5},{2,6},{3,7},{4,0},{5,1},{6,2},{7,3},{8,12},{9,13},{10,... | collective-permute-start | bytes 1105928 | tf_op jit(solution)/shard_map/ppermute | solution.py:161
  623.7 11.1 %collective-permute-start.26 = (bf16[1,2,120,768]{3,2,1,0:T(8,128)(2,1)S(1)}, bf16[1,2,120,768]{3,2,1,0:T(8,128)(2,1)S(1)}, u32[]{:S(2)}, u32[]{:S(2)}) collective-permute-start(bf16[1,2,120,768]{3,2,1,0:T(8,128)(2,1)S(1)} %slice.923), channel_id=1, source_target_pairs={{0,1},{1,0},{2,3},{3,2},{4,5},{5,4},{6,7},{7,6},{8,9},{9,8},{10,11... | collective-permute-start | bytes 1105928 | tf_op jit(solution)/shard_map/ppermute | solution.py:161
  630.7 10.3 %collective-permute-start.34 = (bf16[1,2,128,768]{3,2,1,0:T(8,128)(2,1)S(1)}, bf16[1,2,128,768]{3,2,1,0:T(8,128)(2,1)S(1)}, u32[]{:S(2)}, u32[]{:S(2)}) collective-permute-start(bf16[1,2,128,768]{3,2,1,0:T(8,128)(2,1)S(1)} %slice.921), channel_id=1, source_target_pairs={{0,8},{1,9},{2,10},{3,11},{4,12},{5,13},{6,14},{7,15},{8,0},{9,1},... | collective-permute-start | bytes 1179656 | tf_op jit(solution)/shard_map/ppermute | solution.py:161
  641.3 19.9 %collective-permute-start.35 = (bf16[368,768]{1,0:T(8,128)(2,1)S(1)}, bf16[368,768]{1,0:T(8,128)(2,1)S(1)}, u32[]{:S(2)}, u32[]{:S(2)}) collective-permute-start(bf16[368,768]{1,0:T(8,128)(2,1)S(1)} %fusion.64), channel_id=1, source_target_pairs={{0,16},{1,17},{2,18},{3,19},{4,20},{5,21},{6,22},{7,23},{8,24},{9,... | collective-permute-start | bytes 1695752 | tf_op jit(solution)/shard_map/ppermute | solution.py:161
  (127 other events, 944.3 us)
where the time goes:
time: 682 us; the launch traced here: 672 us
  waiting for transfers between devices  175 us (26%)
  local copies, waits for them, and re-layouts  161 us (24%)
  matrix products  116 us (17%)
  other arithmetic  105 us (15%)
  Pallas kernels  63.2 us (9%)
  starting transfers between devices  43.4 us (6%)
  between operations  8.27 us (1%)
    ppermute x36, waiting for transfers between devices, swap(): lax.ppermute(value, AXES, [(place, place ^ mask) for place in range(self....  175 us
    dot_general x27, matrix products, dot(): lax.dot_general(left, right, (((left_dim,), (right_dim,)), ((), ())), pre...  113 us
    unnamed x333, local copies, waits for them, and re-layouts  61.1 us
    ppermute x36, starting transfers between devices, swap(): lax.ppermute(value, AXES, [(place, place ^ mask) for place in range(self....  43.4 us
    pallas_call x1, Pallas kernels, attend_back(): pl.pallas_call(functools.partial(attend_back_kernel, group, width), out_s...  36.7 us
    pallas_call x1, Pallas kernels, attend(): pl.pallas_call(functools.partial(attend_kernel, group), out_shape=jax.Sha...  26.5 us
    gather x3, local copies, waits for them, and re-layouts, unpack_chain(): whole = jnp.take(jnp.concatenate(pieces, axis=0), slots, axis=0)  18.6 us
    another operation x6, other arithmetic, pack_chain(): both = jnp.stack((mine, theirs), axis=1)  15.5 us
  transfers between devices with their start and end apart: 36, of which 19 were waited for; matrix products, arithmetic and copies ran while one was open for 23% of the time, Pallas kernels for 0%

commit v1 on v0

v1 whole, which is shorter than its diff:
```python
import functools

import jax
import jax.numpy as jnp
import numpy as np
from jax import lax
from jax.experimental import pallas as pl
from jax.experimental.pallas import tpu as pltpu
from jax.sharding import PartitionSpec as P

HD = 64
AXES = ("dp", "fsdp")
GELU_COEF = 0.7978845608028654
GELU_CUBE = 0.044715
F32 = jnp.float32
LOW = jnp.bfloat16
SCALE = HD ** (-0.5)

LANES = 128
CHAINS = 3
GATHER_GROUPS = (
    (("triple", 3), ("merge", 1), ("line", 0)),
    (("expand", 4), ("keyval", 2), ("head", 1), ("shrink", 4)),
)
SCATTER_GROUPS = (
    (("head", 1), ("keyval", 2), ("shrink", 4)),
    (("expand", 4), ("merge", 1)),
    (("triple", 3), ("line", 0)),
)
IMAGE_ROWS = 8


def dot(left, right, left_dim, right_dim):
    return lax.dot_general(
        left, right, (((left_dim,), (right_dim,)), ((), ())), preferred_element_type=F32
    )


def normalize_rows(values):
    centred = values - jnp.mean(values, axis=-1, keepdims=True)
    inverse = lax.rsqrt(jnp.mean(centred * centred, axis=-1, keepdims=True) + 1e-06)
    return (centred * inverse, inverse)


def normalize_back(grad_hat, hat_rows, inverse):
    first = jnp.mean(grad_hat, axis=-1, keepdims=True)
    second = jnp.mean(grad_hat * hat_rows, axis=-1, keepdims=True)
    return inverse * (grad_hat - first - hat_rows * second)


def gelu_tanh(values):
    return (
        0.5 * values * (1.0 + jnp.tanh(GELU_COEF * (values + GELU_CUBE * values * values * values)))
    )


def gelu_slope(values):
    tanh_val = jnp.tanh(GELU_COEF * (values + GELU_CUBE * values * values * values))
    return 0.5 * (1.0 + tanh_val) + 0.5 * values * (1.0 - tanh_val * tanh_val) * GELU_COEF * (
        1.0 + 3.0 * GELU_CUBE * values * values
    )


def pair_bias(side_ref, seq_len, group):
    key = lax.broadcasted_iota(jnp.int32, (seq_len, seq_len), 0)
    query = lax.broadcasted_iota(jnp.int32, (seq_len, seq_len), 1)
    seen = jnp.logical_and(key // group == query // group, query >= key)
    seen = jnp.logical_or(seen, side_ref[0] == 0)
    return jnp.where(seen, 0.0, -1e30)

def head_lanes(shape):
    lane = lax.broadcasted_iota(jnp.int32, shape, 1)
    return (lane < HD, lane >= HD)

def head_probs(key, query_part, bias):
    scores = dot(key, query_part, 1, 1) + bias
    row_exp = jnp.exp(scores - jnp.max(scores, axis=0, keepdims=True))
    return row_exp * (1.0 / jnp.sum(row_exp, axis=0, keepdims=True))

def attend_kernel(group, side_ref, q_ref, k_ref, v_ref, out_ref, bias_ref):
    @pl.when(pl.program_id(0) == 0)
    def _():
        bias_ref[...] = pair_bias(side_ref, q_ref.shape[0], group)
    bias = bias_ref[...]
    pairs = q_ref.shape[1] // (2 * HD)
    def scores_of(pair):
        lanes = slice(pair * 2 * HD, (pair + 1) * 2 * HD)
        query, key = q_ref[:, lanes] * jnp.asarray(SCALE, LOW), k_ref[:, lanes]
        zero = jnp.zeros_like(query)
        return [dot(key, jnp.where(mine, query, zero), 1, 1) for mine in head_lanes(query.shape)]
    def finish(pair, scores):
        lanes = slice(pair * 2 * HD, (pair + 1) * 2 * HD)
        value_t = v_ref[:, lanes].T
        parts = []
        for head in range(2):
            masked = scores[head] + bias
            row_exp = jnp.exp(masked - jnp.max(masked, axis=0, keepdims=True))
            inverse = 1.0 / jnp.sum(row_exp, axis=0, keepdims=True)
            part = dot(value_t[head * HD : (head + 1) * HD], row_exp.astype(LOW), 1, 0)
            parts.append(part * inverse)
        out_ref[:, lanes] = jnp.concatenate(parts, axis=0).T.astype(LOW)
    for pair in range(pairs):
        finish(pair, scores_of(pair))

def attend_back_kernel(group, width, side_ref, q_ref, k_ref, v_ref, grad_ref, out_ref, bias_ref):
    @pl.when(pl.program_id(0) == 0)
    def _():
        bias_ref[...] = pair_bias(side_ref, q_ref.shape[0], group)
    bias = bias_ref[...]
    for pair in range(width // (2 * HD)):
        lanes = slice(pair * 2 * HD, (pair + 1) * 2 * HD)
        query, key, value = q_ref[:, lanes] * jnp.asarray(SCALE, LOW), k_ref[:, lanes], v_ref[:, lanes]
        grad = grad_ref[:, lanes]
        key_t = key.T
        zero = jnp.zeros_like(query)
        sides = head_lanes(query.shape)
        grad_q, grad_k, grad_v = [], [], []
        for head, mine in enumerate(sides):
            probs = head_probs(key, jnp.where(mine, query, zero), bias)
            grad_probs = dot(value, jnp.where(mine, grad, zero), 1, 1)
            delta = jnp.sum(grad_probs * probs, axis=0, keepdims=True)
            grad_scores = (probs * (grad_probs - delta)).astype(LOW)
            grad_q.append(dot(key_t[head * HD : (head + 1) * HD], grad_scores, 1, 0))
            grad_k.append(dot(grad_scores, query, 1, 0))
            grad_v.append(dot(probs.astype(LOW), grad, 1, 0))
        parts = (
            jnp.concatenate(grad_q, axis=0).T * SCALE,
            jnp.where(sides[0], grad_k[0], grad_k[1]),
            jnp.where(sides[0], grad_v[0], grad_v[1]),
        )
        for place, part in enumerate(parts):
            start = place * width + pair * 2 * HD
            out_ref[:, start : start + 2 * HD] = part.astype(LOW)

def triple_specs(seq_len, width):
    return [pl.BlockSpec((seq_len, width), lambda b, s, place=place: (b, place)) for place in range(3)]


def attend(side, triples, seq_len, group):
    rows, wide = triples.shape
    width = wide // 3
    return pl.pallas_call(
        functools.partial(attend_kernel, group),
        out_shape=jax.ShapeDtypeStruct((rows, width), LOW),
        grid_spec=pltpu.PrefetchScalarGridSpec(
            num_scalar_prefetch=1,
            grid=(rows // seq_len,),
            in_specs=triple_specs(seq_len, width),
            out_specs=pl.BlockSpec((seq_len, width), lambda b, s: (b, 0)),
            scratch_shapes=[pltpu.VMEM((seq_len, seq_len), F32)],
        ),
        cost_estimate=pl.CostEstimate(
            flops=4 * rows * seq_len * width,
            bytes_accessed=8 * rows * width,
            transcendentals=rows * seq_len * width // HD,
        ),
        name="attend",
    )(side, triples, triples, triples)


def attend_back(side, triples, grad_mixed, first, seq_len, group):
    rows, wide = triples.shape
    width = wide // 3
    return pl.pallas_call(
        functools.partial(attend_back_kernel, group, width),
        out_shape=jax.ShapeDtypeStruct((rows, wide), LOW),
        grid_spec=pltpu.PrefetchScalarGridSpec(
            num_scalar_prefetch=1,
            grid=(rows // seq_len,),
            in_specs=triple_specs(seq_len, width)
            + [pl.BlockSpec((seq_len, width), lambda b, s: (b + first, 0))],
            out_specs=pl.BlockSpec((seq_len, wide), lambda b, s: (b, 0)),
            scratch_shapes=[pltpu.VMEM((seq_len, seq_len), F32)],
        ),
        cost_estimate=pl.CostEstimate(
            flops=10 * rows * seq_len * width,
            bytes_accessed=14 * rows * width,
            transcendentals=rows * seq_len * width // HD,
        ),
        name="attend_back",
    )(side, triples, triples, triples, grad_mixed)


class Segment:
    def __init__(self, name, quarter, weight_col, chain, chain_col, cols):
        self.name, self.quarter, self.weight_col = name, quarter, weight_col
        self.chain, self.chain_col, self.cols = chain, chain_col, cols


class Group:
    def __init__(self, parts, width):
        self.names = [name for name, _ in parts]
        self.cols = {name: max(many * width, LANES) for name, many in parts}
        total = sum(self.cols.values())
        tiles = total // LANES
        cuts = [tiles * chain // CHAINS * LANES for chain in range(CHAINS + 1)]
        self.total = total
        self.bounds = list(zip(cuts[:-1], cuts[1:]))
        self.chain_cols = [stop - start for start, stop in self.bounds]
        self.segments, self.places = [], []
        at = 0
        for name, _ in parts:
            quarters = range(4) if name == "shrink" else (None,)
            cols = self.cols[name] // len(quarters)
            for quarter in quarters:
                self.places.append((name, quarter, at, cols))
                for chain, (start, stop) in enumerate(self.bounds):
                    low, high = max(at, start), min(at + cols, stop)
                    if low < high:
                        self.segments.append(
                            Segment(name, quarter, low - at, chain, low - start, high - low)
                        )
                at += cols

    def shape(self, name, count, rows):
        if name == "shrink":
            return (count, 4, rows, self.cols[name] // 4)
        return (count, rows, self.cols[name])


def window(ref, lead, quarter, col, cols):
    lead = lead if quarter is None else lead + (quarter,)
    return ref.at[lead + (slice(None), pl.ds(col, cols))]


def wait_whole(refs, sems):
    for place, ref in enumerate(refs):
        pltpu.make_async_copy(ref, ref, sems.at[place]).wait()


def block_call(kernel, operands, outs, name):
    anywhere = pl.BlockSpec(memory_space=pl.ANY)
    size = sum(2 * out.size * out.dtype.itemsize for out in outs)
    return pl.pallas_call(
        kernel,
        out_shape=outs,
        grid_spec=pltpu.PrefetchScalarGridSpec(
            num_scalar_prefetch=1,
            grid=(1,),
            in_specs=[anywhere] * (len(operands) - 1),
            out_specs=[pl.BlockSpec(memory_space=pltpu.VMEM)] * len(outs),
            scratch_shapes=[pltpu.SemaphoreType.DMA((len(outs),))],
        ),
        cost_estimate=pl.CostEstimate(flops=0, bytes_accessed=size, transcendentals=0),
        name=name,
    )(*operands)


def collect_kernel(groups, towers, side_ref, *refs):
    tower_refs = (refs[: len(towers[0])], refs[len(towers[0]) : len(towers[0]) + len(towers[1])])
    outs, sems = refs[len(towers[0]) + len(towers[1]) : -1], refs[-1]

    def fill(kept):
        for index, group in enumerate(groups):
            base = index * (CHAINS + 1)
            sources = dict(zip(towers[kept], tower_refs[kept]))
            for part in group.segments:
                if part.name in sources:
                    source = sources[part.name]
                    rows = outs[base].shape[0]
                    first = 0 if part.quarter is None else part.quarter * rows
                    pltpu.make_async_copy(
                        source.at[pl.ds(first, rows), pl.ds(part.weight_col, part.cols)],
                        outs[base + part.chain].at[:, pl.ds(part.chain_col, part.cols)],
                        sems.at[base + part.chain],
                    ).start()
            sources = dict(zip(towers[1 - kept], tower_refs[1 - kept]))
            for name, quarter, at, cols in group.places:
                if name in sources:
                    source = sources[name]
                    rows = outs[base].shape[0]
                    first = 0 if quarter is None else quarter * rows
                    pltpu.make_async_copy(
                        source.at[pl.ds(first, rows), :],
                        outs[base + CHAINS].at[:, pl.ds(at, cols)],
                        sems.at[base + CHAINS],
                    ).start()

    pl.when(side_ref[0] == 0)(lambda: fill(0))
    pl.when(side_ref[0] != 0)(lambda: fill(1))
    wait_whole(outs, sems)


def collect(side_word, groups, visual, textual, rows):
    outs = []
    for group in groups:
        outs += [jax.ShapeDtypeStruct((rows, cols), LOW) for cols in group.chain_cols]
        outs.append(jax.ShapeDtypeStruct((rows, group.total), LOW))
    if rows % 8 == 0:
        towers = (tuple(visual), tuple(textual))
        operands = (side_word,) + tuple(visual.values()) + tuple(textual.values())
        kernel = functools.partial(collect_kernel, groups, towers)
        flat = block_call(kernel, operands, outs, "collect")
    else:
        flat = []
        for group in groups:
            blocks = []
            for tower in (visual, textual):
                parts = []
                for name, quarter, _, cols in group.places:
                    first = 0 if quarter is None else quarter * rows
                    parts.append(tower[name][first : first + rows])
                blocks.append(jnp.concatenate(parts, axis=1))
            on_images = side_word[0] == 0
            mine = jnp.where(on_images, blocks[0], blocks[1])
            flat += [mine[:, start:stop] for start, stop in group.bounds]
            flat.append(jnp.where(on_images, blocks[1], blocks[0]))
    size = CHAINS + 1
    return [flat[k * size : (k + 1) * size] for k in range(len(groups))]


def spread_kernel(group, sizes, table_ref, *refs):
    pieces = refs[: sum(len(each) for each in sizes)]
    outs, sems = refs[len(pieces) : -1], refs[-1]
    place = {name: k for k, name in enumerate(group.names)}
    base, at = 0, 0
    for chain, each in enumerate(sizes):
        parts = [part for part in group.segments if part.chain == chain]
        for size in each:
            piece = pieces[at]
            at += 1

            def step(slot, carry, piece=piece, base=base, parts=parts):
                for j in range(2):
                    owner = table_ref[base + 2 * slot + j]
                    for part in parts:
                        target = place[part.name]
                        pltpu.make_async_copy(
                            window(piece, (slot, j), None, part.chain_col, part.cols),
                            window(outs[target], (owner,), part.quarter, part.weight_col, part.cols),
                            sems.at[target],
                        ).start()
                return carry

            lax.fori_loop(0, size, step, 0)
            base += 2 * size
    wait_whole(outs, sems)


def pack_kernel(group, slots, table_ref, *refs):
    grads, outs, sems = refs[: len(group.names)], refs[len(group.names) : -1], refs[-1]
    place = {name: k for k, name in enumerate(group.names)}
    for chain in range(CHAINS):
        parts = [part for part in group.segments if part.chain == chain]
        for which in range(2):
            base = (2 * chain + which) * 2 * slots
            target = 2 * chain + which

            def step(slot, carry, base=base, parts=parts, target=target):
                for j in range(2):
                    owner = table_ref[base + 2 * slot + j]
                    for part in parts:
                        source = grads[place[part.name]]
                        pltpu.make_async_copy(
                            window(source, (owner,), part.quarter, part.weight_col, part.cols),
                            window(outs[target], (slot, j), None, part.chain_col, part.cols),
                            sems.at[target],
                        ).start()
                return carry

            lax.fori_loop(0, slots, step, 0)
    wait_whole(outs, sems)


class Links:
    def __init__(self, count, device):
        self.count = count
        self.half = count // 2
        self.core = 2
        self.device = device
        self.low, self.side = device % self.half, device // self.half
        bits = [1 << place for place in range(self.half.bit_length() - 1)]
        outer = [bit for bit in bits if bit != self.core]
        third = max(1, len(outer) // 3)
        self.orders = [outer[place:] + outer[:place] for place in (0, third, 2 * third)]

    def swap(self, value, mask):
        return lax.ppermute(value, AXES, [(place, place ^ mask) for place in range(self.count)])

    def owners(self, masks):
        low = jnp.array(masks, jnp.int32) ^ self.low
        sides = jnp.stack((self.side, 1 - self.side)).astype(jnp.int32)
        return low[:, None] + sides[None, :] * self.half


def chain_masks(order):
    masks = [0]
    for bit in order:
        masks = masks + [mask ^ bit for mask in masks]
    return masks


def gather_chain(links, order, start):
    held = start[None]
    for bit in order[:-1]:
        held = jnp.concatenate((held, links.swap(held, bit)), axis=0)
    far = links.swap(held, order[-1])
    pieces = [held, far, links.swap(held, links.core), links.swap(far, links.core)]
    masks = chain_masks(order)
    return pieces, masks + [mask ^ links.core for mask in masks]


def gather_pieces(links, group, kept, arrived):
    return [
        gather_chain(links, order, jnp.stack((kept[chain], arrived[:, start:stop])))
        for chain, (order, (start, stop)) in enumerate(zip(links.orders, group.bounds))
    ]


def place_pieces(links, group, chains, rows):
    pieces = [got for got, _ in chains]
    sizes = [[piece.shape[0] for piece in got] for got in pieces]
    tables = [links.owners(masks) for _, masks in chains]
    shapes = [group.shape(name, links.count, rows) for name in group.names]
    if rows % 8 == 0:
        operands = (jnp.stack(tables).reshape(-1),) + tuple(p for got in pieces for p in got)
        outs = [jax.ShapeDtypeStruct(shape, LOW) for shape in shapes]
        kernel = functools.partial(spread_kernel, group, sizes)
        whole = block_call(kernel, operands, outs, "spread")
    else:
        columns = []
        for got, table in zip(pieces, tables):
            order = jnp.argsort(table.reshape(-1))
            every = jnp.concatenate(got, axis=0)
            columns.append(jnp.take(every.reshape((-1,) + every.shape[2:]), order, axis=0))
        every = jnp.concatenate(columns, axis=2)
        whole, at = [], 0
        for name in group.names:
            cols = group.cols[name]
            block = every[:, :, at : at + cols]
            if name == "shrink":
                block = block.reshape(links.count, rows, 4, cols // 4).transpose(0, 2, 1, 3)
            whole.append(block)
            at += cols
    result = {}
    for name, block in zip(group.names, whole):
        result[name] = block if name == "line" else block.reshape(-1, block.shape[-1])
    return result


class ChainSum:
    def __init__(self, links, order, keep, send):
        self.links, self.bits, self.terms = links, list(order[::-1]), [keep]
        self.pending = links.swap(send, links.core)

    def total(self, rows):
        return sum(term[rows].astype(F32) for term in self.terms)

    def prepare(self):
        self.terms.append(self.pending)
        near = self.pending.shape[0] // 2
        self.send = self.total(slice(near, 2 * near)).astype(LOW)
        self.terms = [term[:near] for term in self.terms]

    def launch(self):
        self.pending = self.links.swap(self.send, self.bits.pop(0))

    def result(self):
        self.terms.append(self.pending)
        return self.total(0)


class GroupSum:
    def __init__(self, links, flat):
        self.links = links
        self.chains = [
            ChainSum(links, order, flat[2 * chain], flat[2 * chain + 1])
            for chain, order in enumerate(links.orders)
        ]
        self.crossed = None

    def relay(self, value):
        if self.crossed is not None:
            return value
        if self.chains[0].bits:
            for chain in self.chains:
                chain.prepare()
            value, sends = lax.optimization_barrier((value, [chain.send for chain in self.chains]))
            for chain, send in zip(self.chains, sends):
                chain.send = send
                chain.launch()
            return value
        summed = [chain.result() for chain in self.chains]
        self.kept = jnp.concatenate([each[0] for each in summed], axis=1)
        send = jnp.concatenate([each[1].astype(LOW) for each in summed], axis=1)
        value, send = lax.optimization_barrier((value, send))
        self.crossed = self.links.swap(send, self.links.half)
        return value

    def finish(self):
        while self.crossed is None:
            self.relay(())
        return self.kept, self.crossed.astype(F32)


def pack_group(links, group, grads, rows):
    blocks = [grads[name].reshape(group.shape(name, links.count, rows)) for name in group.names]
    masks = [chain_masks(order) for order in links.orders]
    slots = len(masks[0])
    tables = [
        jnp.stack((links.owners(each), links.owners([mask ^ links.core for mask in each])))
        for each in masks
    ]
    if rows % 8 == 0:
        outs = []
        for cols in group.chain_cols:
            outs += [jax.ShapeDtypeStruct((slots, 2, rows, cols), LOW)] * 2
        kernel = functools.partial(pack_kernel, group, slots)
        flat = block_call(kernel, (jnp.stack(tables).reshape(-1),) + tuple(blocks), outs, "pack")
    else:
        whole = []
        for name, block in zip(group.names, blocks):
            if name == "shrink":
                block = block.transpose(0, 2, 1, 3).reshape(links.count, rows, -1)
            whole.append(block)
        whole = jnp.concatenate(whole, axis=2)
        flat = []
        for (start, stop), table in zip(group.bounds, tables):
            for which in range(2):
                taken = jnp.take(whole[:, :, start:stop], table[which].reshape(-1), axis=0)
                flat.append(taken.reshape((slots, 2) + taken.shape[1:]))
    return flat


def line_place(index, rows):
    per = LANES // rows
    return index // per, index % per * rows


def line_block(vectors, rows):
    block = jnp.zeros((rows, LANES), LOW)
    for index, vector in enumerate(vectors):
        row, lane = line_place(index, rows)
        spot = ((row, rows - row - 1), (lane, LANES - lane - rows))
        block = block + jnp.pad(vector.reshape(1, rows), spot)
    return block


def body(*args):
    tile_embeds, sentence_embeds, pairing = args[:3]
    visual_shards, textual_shards = args[3:16], args[16:27]
    sharpness_exponent, match_score_offset = args[27:]
    device = lax.axis_index(AXES)
    links = Links(lax.axis_size(AXES), device)
    count, half, low, side = links.count, links.half, links.low, links.side
    on_images = side == 0
    side_word = jnp.reshape(side, (1,)).astype(jnp.int32)
    micro, images, seq_len, width = tile_embeds.shape
    captions, text_len = sentence_embeds.shape[1:3]
    own_rows = micro * images * seq_len
    text_rows = micro * captions * text_len
    row_shards = visual_shards[2].shape[0]
    gather_groups = [Group(parts, width) for parts in GATHER_GROUPS]
    scatter_groups = [Group(parts, width) for parts in SCATTER_GROUPS]

    (v_gain_a, v_shift_a, v_triple, v_merge, v_gain_b, v_shift_b, v_expand, v_shrink) = (
        visual_shards[:8]
    )
    pool_gain, pool_shift, probe, keyval, pool_out = visual_shards[8:]
    (t_gain_a, t_shift_a, t_triple, t_merge, t_gain_b, t_shift_b, t_expand, t_shrink) = (
        textual_shards[:8]
    )
    final_gain, final_shift, readout = textual_shards[8:]
    visual_line = line_block(
        (v_gain_a, v_shift_a, v_gain_b, v_shift_b, pool_gain, pool_shift, probe), row_shards
    )
    textual_line = line_block(
        (t_gain_a, t_shift_a, t_gain_b, t_shift_b, final_gain, final_shift), row_shards
    )
    visual = dict(
        triple=v_triple,
        merge=v_merge,
        line=visual_line,
        expand=v_expand,
        keyval=keyval,
        head=pool_out,
        shrink=v_shrink,
    )
    textual = dict(
        triple=t_triple,
        merge=t_merge,
        line=textual_line,
        expand=t_expand,
        keyval=jnp.zeros_like(keyval),
        head=readout,
        shrink=t_shrink,
    )
    weights = {}
    collected = collect(side_word, gather_groups, visual, textual, row_shards)
    first = links.swap(collected[0][CHAINS], half)
    patch_rows = tile_embeds.reshape(own_rows, width)
    token_rows = jnp.pad(
        sentence_embeds.reshape(text_rows, width), ((0, own_rows - text_rows), (0, 0))
    )
    kept_rows = jnp.where(on_images, patch_rows, token_rows)
    moved_rows = jnp.where(on_images, token_rows, patch_rows)
    first, later = lax.optimization_barrier((first, collected[1][CHAINS]))
    later = links.swap(later, half)
    pieces = gather_pieces(links, gather_groups[0], collected[0][:CHAINS], first)
    across = [got[1] for got, _ in pieces]
    across, moved_rows, later = lax.optimization_barrier((across, moved_rows, later))
    for (got, _), far in zip(pieces, across):
        got[1] = far
    moved_rows = links.swap(moved_rows, half)
    weights.update(place_pieces(links, gather_groups[0], pieces, row_shards))
    pieces = gather_pieces(links, gather_groups[1], collected[1][:CHAINS], later)
    weights.update(place_pieces(links, gather_groups[1], pieces, row_shards))

    triple, merge, expand = weights["triple"], weights["merge"], weights["expand"]
    pool_keyval, head_matrix, shrink = weights["keyval"], weights["head"], weights["shrink"]
    per = LANES // row_shards
    line_rows = -(-7 // per)
    lines = weights["line"][:, :line_rows, : per * row_shards]
    lines = jnp.transpose(lines.reshape(count, line_rows, per, row_shards), (1, 2, 0, 3))
    vectors = lines.reshape(line_rows * per, width).astype(F32)
    gain_a, shift_a, gain_b, shift_b, gain_c, shift_c, probe_line = [vectors[k] for k in range(7)]

    shares = []
    for share in (kept_rows, moved_rows):
        share = share.astype(F32)
        hat_a, inverse_a = normalize_rows(share)
        normed_a = (hat_a * gain_a + shift_a).astype(LOW)
        triples = dot(normed_a, triple, 1, 0).astype(LOW)
        mixed = attend(side_word, triples, seq_len, text_len)
        shares.append((share, hat_a, inverse_a, normed_a, triples, mixed))
    inputs = jnp.concatenate([share[0] for share in shares], axis=0)
    mixed = jnp.concatenate([share[5] for share in shares], axis=0)
    middle = inputs + dot(mixed, merge, 1, 0)
    hat_b, inverse_b = normalize_rows(middle)
    normed_b = (hat_b * gain_b + shift_b).astype(LOW)
    upward = dot(normed_b, expand, 1, 0)
    active, slope = gelu_tanh(upward).astype(LOW), gelu_slope(upward).astype(LOW)
    active, slope = lax.optimization_barrier((active, slope))
    hidden = middle + dot(active, shrink, 1, 0)

    total_rows = 2 * own_rows
    group_count = total_rows // seq_len
    caption_slots = total_rows // text_len
    heads = width // HD
    hat_c, inverse_c = normalize_rows(hidden)
    normed_c = (hat_c * gain_c + shift_c).astype(LOW)
    pairs = dot(normed_c, pool_keyval, 1, 0).astype(LOW)
    keys, values = pairs[:, :width], pairs[:, width:]
    lane = lax.broadcasted_iota(jnp.int32, (width, 128), 0) // HD
    spread = lane == lax.broadcasted_iota(jnp.int32, (width, 128), 1)
    probe_map = jnp.where(spread, probe_line[:, None], 0.0).astype(LOW)
    spread_low = spread.astype(LOW)
    scores = (dot(keys, probe_map, 1, 0) * SCALE).reshape(group_count, seq_len, 128)
    row_exp = jnp.exp(scores - jnp.max(scores, axis=1, keepdims=True))
    pool_full = row_exp / jnp.sum(row_exp, axis=1, keepdims=True)
    pool_probs = pool_full.astype(LOW).reshape(total_rows, 128)
    probs_wide = dot(pool_probs, spread_low, 1, 1)
    pooled = jnp.sum((probs_wide * values).reshape(group_count, seq_len, width), axis=1)
    pooled = jnp.pad(pooled.astype(LOW), ((0, caption_slots - group_count), (0, 0)))
    last_rows = normed_c.reshape(caption_slots, text_len, width)[:, -1]
    head_in = jnp.where(on_images, pooled, last_rows)
    raw = dot(head_in, head_matrix, 1, 0)
    length_inverse = lax.rsqrt(jnp.sum(raw * raw, axis=-1, keepdims=True) + 1e-06)
    unit = raw * length_inverse

    their_unit = links.swap(unit, half)
    caption_half = caption_slots // 2
    own_texts = micro * captions
    image_units = jnp.where(on_images, unit, their_unit)[:IMAGE_ROWS]
    text_units = jnp.where(on_images, their_unit, unit)
    held = jnp.concatenate((image_units, text_units), axis=0).astype(LOW)[None]
    exchange = links.orders[0] + [links.core]
    for bit in exchange:
        held = jnp.concatenate((held, links.swap(held, bit)), axis=0)
    slot_rows = IMAGE_ROWS + caption_slots
    row = np.arange(slot_rows)
    is_image, text_row = row < group_count, row - IMAGE_ROWS
    in_half = text_row % caption_half
    is_text = (text_row >= 0) & (in_half < own_texts)
    place = np.where(is_image, row % (micro * images), in_half)
    pack = np.where(is_image, images, captions)
    row_side = np.where(is_image, row // (micro * images), 1 - text_row // caption_half)
    row_micro, row_item = np.where(is_image | is_text, place // pack, 0), place % pack
    slot_device = jnp.array(chain_masks(exchange), jnp.int32) ^ low
    row_device = slot_device[:, None] + jnp.array(row_side * half, jnp.int32)[None, :]
    all_images, all_captions = count * images, count * captions
    number = row_device * jnp.array(pack, jnp.int32)[None, :] + jnp.array(row_item, jnp.int32)
    number = jnp.where(jnp.array(is_image | is_text), number, 0)
    wanted = jnp.take(
        pairing.reshape(-1),
        jnp.where(jnp.array(is_text), number + jnp.array(row_micro * all_captions, jnp.int32), 0),
    )
    named = jnp.where(jnp.array(is_text), wanted, number)
    named = named + jnp.array(row_micro * all_images, jnp.int32)

    sharpness_factor = jnp.exp(sharpness_exponent[0])
    kind = np.where(is_image, 1, np.where(is_text, 2, 0)) + 4 * row_micro
    slots = slot_device.shape[0]

    def pair_terms(left, right, left_rows, right_rows, left_slots):
        left_kind = jnp.array(np.tile(kind[left_rows], left_slots))
        right_kind = jnp.array(np.tile(kind[right_rows], slots))
        together = (left_kind[:, None] + right_kind[None, :]) % 8 == 3
        together = jnp.logical_and(together, (left_kind[:, None] // 4) == (right_kind[None, :] // 4))
        matched = named[:left_slots, left_rows].reshape(-1)[:, None] == (
            named[:, right_rows].reshape(-1)[None, :]
        )
        signs = jnp.where(matched, 1.0, -1.0)
        cosine = dot(left, right, 1, 1)
        logits = sharpness_factor * cosine + match_score_offset[0]
        terms = jnp.where(together, jax.nn.softplus(-signs * logits), 0.0)
        grad_logits = jnp.where(together, -signs * jax.nn.sigmoid(-signs * logits), 0.0)
        return cosine, grad_logits, terms

    every_row, image_part, text_part = slice(None), slice(0, IMAGE_ROWS), slice(IMAGE_ROWS, None)
    flat = held.reshape(-1, width)
    _, grad_logits, _ = pair_terms(held[0], flat, every_row, every_row, 1)
    grad_cosine = (sharpness_factor * grad_logits).astype(LOW)
    own_grad = dot(grad_cosine, flat, 1, 0)
    from_texts = jnp.pad(own_grad[:IMAGE_ROWS], ((0, caption_slots - IMAGE_ROWS), (0, 0)))
    grad_unit = jnp.where(on_images, from_texts, own_grad[IMAGE_ROWS:])
    cosine, grad_logits, terms = pair_terms(
        held[:, image_part].reshape(-1, width),
        held[:, text_part].reshape(-1, width),
        image_part,
        text_part,
        slots,
    )
    objective = jnp.sum(terms)
    sharpness_grad = jnp.sum(grad_logits * cosine) * sharpness_factor
    offset_grad = jnp.sum(grad_logits)

    grad_raw = length_inverse * (grad_unit - unit * jnp.sum(grad_unit * unit, axis=-1, keepdims=True))
    grad_raw = grad_raw.astype(LOW)
    grad_head = dot(head_in, grad_raw, 0, 0).astype(LOW)
    grad_head_in = dot(grad_raw, head_matrix, 1, 1)
    grad_pooled = grad_head_in[:group_count].astype(LOW)
    pooled_wide = jnp.broadcast_to(grad_pooled[:, None], (group_count, seq_len, width))
    pooled_wide = pooled_wide.reshape(total_rows, width)
    grad_values = probs_wide * pooled_wide
    pooled_map = jnp.where(spread[None], grad_pooled[:, :, None], 0.0).astype(LOW)
    grad_probs = lax.dot_general(
        values.reshape(group_count, seq_len, width),
        pooled_map,
        (((2,), (1,)), ((0,), (0,))),
        preferred_element_type=F32,
    )
    delta = jnp.sum(grad_probs * pool_full, axis=1, keepdims=True)
    grad_scores = (pool_full * (grad_probs - delta)).astype(LOW).reshape(total_rows, 128)
    grad_keys = dot(grad_scores, probe_map, 1, 1) * SCALE
    grad_probe = jnp.sum(jnp.where(spread, dot(keys, grad_scores, 0, 0), 0.0), axis=1) * SCALE
    grad_pairs = jnp.concatenate((grad_keys.astype(LOW), grad_values.astype(LOW)), axis=1)
    grad_keyval = dot(normed_c, grad_pairs, 0, 0).astype(LOW)
    pool_side = dot(grad_pairs, pool_keyval, 1, 1)
    text_side = jnp.pad(grad_head_in[:, None], ((0, 0), (text_len - 1, 0), (0, 0)))
    grad_normed_c = jnp.where(on_images, pool_side, text_side.reshape(total_rows, width))
    grad_gain_c = jnp.sum(grad_normed_c * hat_c, axis=0)
    grad_shift_c = jnp.sum(grad_normed_c, axis=0)
    grad_hidden = normalize_back(grad_normed_c * gain_c, hat_c, inverse_c)

    grad_low = grad_hidden.astype(LOW)
    grad_shrink = dot(active, grad_low, 0, 0).astype(LOW)
    grads = dict(shrink=grad_shrink, keyval=grad_keyval, head=grad_head)
    packed = [pack_group(links, scatter_groups[0], grads, row_shards)]
    grad_up = (dot(grad_low, shrink, 1, 1) * slope.astype(F32)).astype(LOW)
    grad_up, packed = lax.optimization_barrier((grad_up, packed))
    sums = [GroupSum(links, packed[0])]
    grad_normed_b = dot(grad_up, expand, 1, 1)
    grad_gain_b = jnp.sum(grad_normed_b * hat_b, axis=0)
    grad_shift_b = jnp.sum(grad_normed_b, axis=0)
    grad_middle = grad_hidden + normalize_back(grad_normed_b * gain_b, hat_b, inverse_b)
    grad_branch, grad_up = sums[0].relay((grad_middle.astype(LOW), grad_up))
    grad_expand = dot(normed_b, grad_up, 0, 0).astype(LOW)
    grad_merge = dot(mixed, grad_branch, 0, 0).astype(LOW)
    grad_mixed = dot(grad_branch, merge, 1, 1).astype(LOW)
    grads = dict(merge=grad_merge, expand=grad_expand)
    packed = pack_group(links, scatter_groups[1], grads, row_shards)
    grad_mixed, packed = lax.optimization_barrier((grad_mixed, packed))
    sums.append(GroupSum(links, packed))
    grad_mixed = sums[0].relay(grad_mixed)

    def inputs_back(index, grad_triples):
        _, hat_a, inverse_a, _, _, _ = shares[index]
        grad_normed_a = dot(grad_triples, triple, 1, 1)
        grad_gain = jnp.sum(grad_normed_a * hat_a, axis=0)
        grad_shift = jnp.sum(grad_normed_a, axis=0)
        own = grad_middle[index * own_rows : (index + 1) * own_rows]
        return grad_gain, grad_shift, own + normalize_back(grad_normed_a * gain_a, hat_a, inverse_a)

    blocks = own_rows // seq_len
    moved_back = attend_back(side_word, shares[1][4], grad_mixed, blocks, seq_len, text_len)
    moved_back = sums[0].relay(moved_back)
    moved_back = sums[1].relay(moved_back)
    moved_gain, moved_shift, moved_grad = inputs_back(1, moved_back)
    moved_grad = moved_grad.astype(LOW)
    grad_mixed, moved_grad = lax.optimization_barrier((grad_mixed, moved_grad))
    returned = links.swap(moved_grad, half).astype(F32)
    kept_back = attend_back(side_word, shares[0][4], grad_mixed, 0, seq_len, text_len)
    kept_back = sums[1].relay(kept_back)
    kept_gain, kept_shift, kept = inputs_back(0, kept_back)
    grad_gain_a, grad_shift_a = kept_gain + moved_gain, kept_shift + moved_shift
    grad_triple = dot(shares[1][3], moved_back, 0, 0) + dot(shares[0][3], kept_back, 0, 0)
    grad_triple = sums[1].relay(grad_triple.astype(LOW))
    grad_triple = sums[0].relay(grad_triple)

    grad_lines = jnp.stack(
        (grad_gain_a, grad_shift_a, grad_gain_b, grad_shift_b, grad_gain_c, grad_shift_c, grad_probe)
    )
    grad_lines = jnp.pad(grad_lines, ((0, line_rows * per - 7), (0, 0)))
    grad_lines = jnp.transpose(
        grad_lines.reshape(line_rows, per, count, row_shards), (2, 0, 1, 3)
    ).reshape(count, line_rows, per * row_shards)
    grad_lines = jnp.pad(
        grad_lines.astype(LOW),
        ((0, 0), (0, row_shards - line_rows), (0, LANES - per * row_shards)),
    )
    grads = dict(triple=grad_triple, line=grad_lines)
    sums.append(GroupSum(links, pack_group(links, scatter_groups[2], grads, row_shards)))
    visual_sums, textual_sums = {}, {}
    for group, partial in zip(scatter_groups, sums):
        own_sum, crossed = partial.finish()
        for target, mine in ((visual_sums, on_images), (textual_sums, jnp.logical_not(on_images))):
            for name, quarter, at, cols in group.places:
                piece = jnp.where(mine, own_sum[:, at : at + cols], crossed[:, at : at + cols])
                target.setdefault(name, []).append(piece)

    def outputs_of(sums, names):
        line = sums["line"][0]
        vec = []
        for index in range(7):
            spot_row, lane = line_place(index, row_shards)
            vec.append(line[spot_row, lane : lane + row_shards])
        layer = (vec[0], vec[1], sums["triple"][0], sums["merge"][0], vec[2], vec[3])
        layer += (sums["expand"][0], jnp.concatenate(sums["shrink"], axis=0), vec[4], vec[5])
        if names == 0:
            return layer + (vec[6], sums["keyval"][0], sums["head"][0])
        return layer + (sums["head"][0],)

    patches_grad = jnp.where(on_images, kept, returned).reshape(tile_embeds.shape)
    captions_grad = jnp.where(on_images, returned[:text_rows], kept[:text_rows])
    own_group = group_count // 2
    image_embedding = jnp.where(on_images, unit[:own_group], their_unit[own_group:group_count])
    text_embedding = jnp.where(
        on_images, their_unit[caption_half : caption_half + own_texts], unit[:own_texts]
    )
    return (
        image_embedding.reshape(micro, images, width),
        text_embedding.reshape(micro, captions, width),
        objective / (micro * all_images),
        patches_grad,
        captions_grad.reshape(sentence_embeds.shape),
        *outputs_of(visual_sums, 0),
        *outputs_of(textual_sums, 1),
        jnp.reshape(sharpness_grad, (1,)),
        jnp.reshape(offset_grad, (1,)),
    )


def solution(mesh):
    row, matrix, batch, rest = P(AXES), P(AXES, None), P(None, AXES, None, None), P()
    layer = (row, row, matrix, matrix, row, row, matrix, matrix)
    visual = layer + (row, row, row, matrix, matrix)
    textual = layer + (row, row, matrix)
    in_specs = (batch, batch, rest) + visual + textual + (rest, rest)
    embed = P(None, AXES, None)
    out_specs = (embed, embed, rest, batch, batch) + visual + textual + (rest, rest)
    return jax.shard_map(body, mesh=mesh, in_specs=in_specs, out_specs=out_specs, check_vma=False)
```

time: 682 us -> 525 us (0.77)
  local copies, waits for them, and re-layouts: 161 us -> 41.3 us
  waiting for transfers between devices: 175 us -> 95.8 us
  starting transfers between devices: 43.4 us -> 65.8 us
  Pallas kernels: 63.2 us -> 81.2 us
  matrix products: 116 us -> 127 us
  other arithmetic: 105 us -> 95.7 us
    ppermute x36 -> x78, waiting for transfers between devices: 175 us -> 95.8 us  [swap(): lax.ppermute(value, AXES, [(place, place ^ mask) for place in range(self....]
    unnamed x333 -> x302, local copies, waits for them, and re-layouts: 61.1 us -> 16.1 us
    gather x12 -> x2, local copies, waits for them, and re-layouts: 46.5 us -> 2.89 us  [body(): jnp.take(pairing.reshape(-1), jnp.where(jnp.array(is_text), number + jnp....]
    convert_element_type x5 -> x36, other arithmetic: 6.87 us -> 45.6 us  [the longest x27 34.6 us: prepare(): self.send = self.total(slice(near, 2 * near)).astype(LOW)]
    pallas_call x0 -> x6, Pallas kernels: none -> 37.1 us  [block_call(): pl.pallas_call(kernel, out_shape=outs, grid_spec=pltpu.PrefetchScalarGrid...]
    select_n x21 -> x9, other arithmetic: 30.1 us -> 5.65 us  [the longest x7 3.73 us: body(): piece = jnp.where(mine, own_sum[:, at:at + cols], crossed[:, at:at + cols])]
    ppermute x36 -> x78, starting transfers between devices: 43.4 us -> 65.8 us  [swap(): lax.ppermute(value, AXES, [(place, place ^ mask) for place in range(self....]
    concatenate x10 -> x0, local copies, waits for them, and re-layouts: 15.1 us -> none  [the longest x2 8.96 us: tower_block(): line = jnp.concatenate(vectors)]
  transfers between devices with their start and end apart: 36 -> 78, of which waited for: 19 -> 26; matrix products, arithmetic and copies ran while one was open for 23% -> 29% of each run, Pallas kernels for 0% -> 12%
where the time goes in v1:
time: 525 us; the launch traced here: 515 us
  matrix products  127 us (24%)
  waiting for transfers between devices  95.8 us (18%)
  other arithmetic  95.7 us (18%)
  Pallas kernels  81.2 us (15%)
  starting transfers between devices  65.8 us (13%)
  local copies, waits for them, and re-layouts  41.3 us (8%)
  between operations  8.61 us (2%)
    dot_general x27, matrix products, dot(): lax.dot_general(left, right, (((left_dim,), (right_dim,)), ((), ())), pre...  127 us
    ppermute x78, waiting for transfers between devices, swap(): lax.ppermute(value, AXES, [(place, place ^ mask) for place in range(self....  95.8 us
    ppermute x78, starting transfers between devices, swap(): lax.ppermute(value, AXES, [(place, place ^ mask) for place in range(self....  65.8 us
    pallas_call x6, Pallas kernels, block_call(): pl.pallas_call(kernel, out_shape=outs, grid_spec=pltpu.PrefetchScalarGrid...  37.1 us
    convert_element_type x27, other arithmetic, prepare(): self.send = self.total(slice(near, 2 * near)).astype(LOW)  34.6 us
    pallas_call x2, Pallas kernels, attend_back(): pl.pallas_call(functools.partial(attend_back_kernel, group, width), out_s...  24.9 us
    pallas_call x2, Pallas kernels, attend(): pl.pallas_call(functools.partial(attend_kernel, group), out_shape=jax.Sha...  19.2 us
    unnamed x302, local copies, waits for them, and re-layouts  16.1 us
  transfers between devices with their start and end apart: 78, of which 26 were waited for; matrix products, arithmetic and copies ran while one was open for 29% of the time, Pallas kernels for 12%

profile of v1, /device:TPU:0, one launch (start us, length us, event | category | flops | bytes accessed | tf_op | source)
XLA Modules:
  0.0 515.5 jit_solution(4865670534121693703)
XLA Ops:
  5.2 4.1 collective-permute-start
  16.4 2.8 gather_fusion
  34.1 9.6 %collective-permute-done.5 = bf16[2,2,24,1024]{3,2,1,0:T(8,128)(2,1)S(1)} collective-permute-done((bf16[2,2,24,1024]{3,2,1,0:T(8,128)(2,1)S(1)}, bf16[2,2,24,1024]{3,2,1,0:T(8,128)(2,1)S(1)}, u32[]{:S(2)}, u32[]{:S(2)}) %collective-permute-start.5) | collective-permute-done | bytes 196640 | tf_op jit(solution)/shard_map/ppermute | solution.py:378
  53.8 3.7 collective-permute-done.3.refs_1_
  63.0 5.2 %collective-permute-done.28 = bf16[1,2,24,2816]{3,2,1,0:T(8,128)(2,1)S(1)} collective-permute-done((bf16[1,2,24,2816]{3,2,1,0:T(8,128)(2,1)S(1)}, bf16[1,2,24,2816]{3,2,1,0:T(8,128)(2,1)S(1)}, u32[]{:S(2)}, u32[]{:S(2)}) %collective-permute-start.28) | collective-permute-done | bytes 270368 | tf_op jit(solution)/shard_map/ppermute | solution.py:378
  70.2 4.5 collective-permute-done.23
  79.9 5.5 %spread.2 = (bf16[32,24,2304]{2,1,0:T(8,128)(2,1)}, bf16[32,24,768]{2,1,0:T(8,128)(2,1)}, bf16[32,24,128]{2,1,0:T(8,128)(2,1)}) custom-call(s32[96]{0:T(128)} %reshape.1931.table_ref, bf16[4,2,24,1024]{3,2,1,0:T(8,128)(2,1)} %pad_maximum_fusion.15.refs_0_, bf16[4,2,24,1024]{3,2,1,0:T(8,128)(2,1)} %collective-permute-done.3.refs_1_, ...), custom_call_target="tpu_custom_call" | custom-call | bytes 9830400 | tf_op jit(solution)/shard_map/spread/pallas_call | solution.py:234
  86.7 5.5 %convolution_convert_fusion.3.q_ref.k_ref.v_ref = bf16[512,2304]{1,0:T(8,128)(2,1)} fusion(bf16[768,2304]{1,0:T(8,128)(2,1)} %bitcast.307, bf16[512,768]{1,0:T(8,128)(2,1)S(1)} %get-tuple-element.378, f32[768]{0:T(1024)S(1)} %get-tuple-element.367, f32[768]{0:T(1024)S(1)} %get-tuple-element.368, f32[512]{0:T(512)S(1)} %copy-done.97, ...), kind=kOutput, calls=%fused_computation.16 | convolution fusion | flops 1815478272 | bytes 6694912 | tf_op jit(solution)/shard_map/dot_general | solution.py:34
  92.2 9.7 %attend.2 = bf16[512,768]{1,0:T(8,128)(2,1)} custom-call(s32[1]{0:T(128)} %bitcast.2.side_ref, bf16[512,2304]{1,0:T(8,128)(2,1)} %convolution_convert_fusion.3.q_ref.k_ref.v_ref, bf16[512,2304]{1,0:T(8,128)(2,1)} %convolution_convert_fusion.3.q_ref.k_ref.v_ref, bf16[512,2304]{1,0:T(8,128)(2,1)} %convolution_convert_fusion.3.q_ref.k_ref.v_ref), custom_call_target="tpu_custom_call" | custom-call | flops 402653184 | bytes 3145728 | tf_op jit(solution)/shard_map/attend/pallas_call | solution.py:142
  101.9 12.2 %collective-permute-done.11 = bf16[512,768]{1,0:T(8,128)(2,1)S(1)} collective-permute-done((bf16[512,768]{1,0:T(8,128)(2,1)}, bf16[512,768]{1,0:T(8,128)(2,1)S(1)}, u32[]{:S(2)}, u32[]{:S(2)}) %collective-permute-start.11) | collective-permute-done | bytes 786464 | tf_op jit(solution)/shard_map/ppermute | solution.py:378
  123.4 3.6 convolution_convert_fusion.2.q_ref.k_ref.v_ref
  127.0 9.5 %attend.3 = bf16[512,768]{1,0:T(8,128)(2,1)} custom-call(s32[1]{0:T(128)} %bitcast.2.side_ref, bf16[512,2304]{1,0:T(8,128)(2,1)} %convolution_convert_fusion.2.q_ref.k_ref.v_ref, bf16[512,2304]{1,0:T(8,128)(2,1)} %convolution_convert_fusion.2.q_ref.k_ref.v_ref, bf16[512,2304]{1,0:T(8,128)(2,1)} %convolution_convert_fusion.2.q_ref.k_ref.v_ref), custom_call_target="tpu_custom_call" | custom-call | flops 402653184 | bytes 3145728 | tf_op jit(solution)/shard_map/attend/pallas_call | solution.py:142
  137.0 5.0 collective-permute-done.30.refs_9_
  142.1 2.7 collective-permute-done.25.refs_5_
  144.7 2.9 collective-permute-done.20.refs_1_
  147.6 4.2 fusion.135
  152.4 10.4 %spread.3 = (bf16[32,24,3072]{2,1,0:T(8,128)(2,1)}, bf16[32,24,1536]{2,1,0:T(8,128)(2,1)}, bf16[32,24,768]{2,1,0:T(8,128)(2,1)}, bf16[32,4,24,768]{3,2,1,0:T(8,128)(2,1)}) custom-call(s32[96]{0:T(128)} %reshape.1931.table_ref, bf16[4,2,24,2816]{3,2,1,0:T(8,128)(2,1)} %pad_maximum_fusion.6.refs_0_, bf16[4,2,24,2816]{3,2,1,0:T(8,128)(2,1)} %collective-permute-done.20.refs_1_, ...), custom_call_target="tpu_custom_call" | custom-call | bytes 25952256 | tf_op jit(solution)/shard_map/spread/pallas_call | solution.py:234
  162.9 17.4 %fusion.6 = (bf16[1024,3072]{1,0:T(8,128)(2,1)}, bf16[1024,3072]{1,0:T(8,128)(2,1)S(1)}) fusion(bf16[768,3072]{1,0:T(8,128)(2,1)} %bitcast.301, f32[1024,768]{1,0:T(8,128)S(1)} %get-tuple-element.428, f32[768]{0:T(1024)S(1)} %get-tuple-element.365, f32[768]{0:T(1024)S(1)} %get-tuple-element.366, f32[1024]{0:T(1024)S(1)} %add_rsqrt_fusion.1, ...), kind=kOutput, calls=%fused_computation.9 | convolution fusion | flops 4898684928 | bytes 20461568 | tf_op jit(solution)/shard_map/dot_general | solution.py:34
  180.3 9.4 %fusion.136 = (f32[1024]{0:T(1024)S(1)}, f32[1024,768]{1,0:T(8,128)S(1)}) fusion(f32[1024,768]{1,0:T(8,128)} %copy-done.2, bf16[1024,3072]{1,0:T(8,128)(2,1)S(1)} %get-tuple-element.144, bf16[3072,768]{1,0:T(8,128)(2,1)S(1)} %bitcast.303), kind=kOutput, calls=%fused_computation.416 | convolution fusion | flops 4833410048 | bytes 17305600 | tf_op jit(solution)/shard_map/dot_general | solution.py:34
  192.2 2.8 convolution_convert_fusion.4
  200.6 5.8 %collective-permute-done.33 = f32[16,768]{1,0:T(8,128)S(1)} collective-permute-done((f32[16,768]{1,0:T(8,128)S(1)}, f32[16,768]{1,0:T(8,128)S(1)}, u32[]{:S(2)}, u32[]{:S(2)}) %collective-permute-start.33) | collective-permute-done | bytes 49184 | tf_op jit(solution)/shard_map/ppermute | solution.py:378
  241.6 4.6 convolution_convert_fusion.5
  247.9 3.4 multiply_reduce_fusion
  252.5 11.5 %convolution_convert_fusion.1 = bf16[3072,768]{1,0:T(8,128)(2,1)} fusion(bf16[1024,3072]{1,0:T(8,128)(2,1)} %copy-done.143, f32[1024,768]{1,0:T(8,128)S(1)} %subtract_multiply_fusion), kind=kOutput, calls=%fused_computation.14 | convolution fusion | flops 4834983936 | bytes 14155776 | tf_op jit(solution)/shard_map/dot_general | solution.py:34
  264.0 7.1 %multiply_convert_fusion = bf16[1024,3072]{1,0:T(8,128)(2,1)} fusion(bf16[1024,3072]{1,0:T(8,128)(2,1)S(1)} %bitcast.316, bf16[3072,768]{1,0:T(8,128)(2,1)S(1)} %bitcast.306, f32[1024,768]{1,0:T(8,128)S(1)} %subtract_multiply_fusion), kind=kOutput, calls=%fused_computation.10 | convolution fusion | flops 4842061824 | bytes 20447232 | tf_op jit(solution)/shard_map/dot_general | solution.py:34
  271.1 7.7 %pack.3 = (bf16[8,2,24,1792]{3,2,1,0:T(8,128)(2,1)}, bf16[8,2,24,1792]{3,2,1,0:T(8,128)(2,1)}, bf16[8,2,24,1792]{3,2,1,0:T(8,128)(2,1)}, bf16[8,2,24,1792]{3,2,1...) custom-call(s32[96]{0:T(128)} %reshape.1951.table_ref, ...), custom_call_target="tpu_custom_call" | custom-call | bytes 16515072 | tf_op jit(solution)/shard_map/pack/pallas_call | solution.py:234
  279.0 10.4 %multiply_reduce_fusion.1 = (bf16[768]{0:T(1024)(128)(2,1)S(1)}, f32[1024]{0:T(1024)S(1)}, f32[1024]{0:T(1024)S(1)}, bf16[768]{0:T(1024)(128)(2,1)S(1)}, f32[1024,768]{1,0:T(8,128)}) fusion(f32[1024,768]{1,0:T(8,128)S(1)} %copy-done.3, f32[1024]{0:T(1024)S(1)} %copy-done.88, f32[1024]{0:T(1024)S(1)} %copy-done.75, f32[768]{0:T(1024)S(1)} %copy-done.86, ...), kind=kOutput, calls=%fused_computation.26 | convolution fusion | flops 4838912000 | bytes 17324032 | tf_op jit(solution)/shard_map/dot_general | solution.py:34
  293.9 4.9 fusion.133
  298.8 2.8 add_convert_fusion.7
  305.9 10.0 %convolution_convert_fusion = bf16[768,3072]{1,0:T(8,128)(2,1)} fusion(bf16[1024,3072]{1,0:T(8,128)(2,1)} %multiply_convert_fusion, f32[1024,768]{1,0:T(8,128)S(1)} %copy-done.3, f32[768]{0:T(1024)S(1)} %copy-done.116, f32[768]{0:T(1024)S(1)} %copy-done.86, f32[1024]{0:T(1024)S(1)} %copy-done.88, f32[1024]{0:T(1024)S(1)} %copy-done.75), kind=kOutput, calls=%fused_computation.13 | convolution fusion | flops 4838129664 | bytes 14170112 | tf_op jit(solution)/shard_map/dot_general | solution.py:34
  320.1 6.2 %pack.4 = (bf16[8,2,24,1280]{3,2,1,0:T(8,128)(2,1)}, bf16[8,2,24,1280]{3,2,1,0:T(8,128)(2,1)}, bf16[8,2,24,1280]{3,2,1,0:T(8,128)(2,1)}, bf16[8,2,24,1280]{3,2,1...) custom-call(s32[96]{0:T(128)} %reshape.1951.table_ref, ...), custom_call_target="tpu_custom_call" | custom-call | bytes 11796480 | tf_op jit(solution)/shard_map/pack/pallas_call | solution.py:234
  326.3 2.6 convolution_convert_fusion.6.grad_ref
  331.0 2.6 collective-permute-done.41
  337.7 8.0 %collective-permute-done.43 = bf16[4,2,24,1792]{3,2,1,0:T(8,128)(2,1)S(1)} collective-permute-done((bf16[4,2,24,1792]{3,2,1,0:T(8,128)(2,1)S(1)}, bf16[4,2,24,1792]{3,2,1,0:T(8,128)(2,1)S(1)}, u32[]{:S(2)}, u32[]{:S(2)}) %collective-permute-start.43) | collective-permute-done | bytes 688160 | tf_op jit(solution)/shard_map/ppermute | solution.py:378
  351.2 12.4 %attend_back.2 = bf16[512,2304]{1,0:T(8,128)(2,1)} custom-call(s32[1]{0:T(128)} %bitcast.2.side_ref, bf16[512,2304]{1,0:T(8,128)(2,1)} %convolution_convert_fusion.2.q_ref.k_ref.v_ref, bf16[512,2304]{1,0:T(8,128)(2,1)} %convolution_convert_fusion.2.q_ref.k_ref.v_ref, bf16[512,2304]{1,0:T(8,128)(2,1)} %convolution_convert_fusion.2.q_ref.k_ref.v_ref, ...), custom_call_target="tpu_custom_call" | custom-call | flops 1006632960 | bytes 5505024 | tf_op jit(solution)/shard_map/attend_back/pallas_call | solution.py:164
  379.4 4.4 multiply_reduce_fusion.8
  383.8 5.1 fusion.130
  390.4 12.5 %attend_back.3 = bf16[512,2304]{1,0:T(8,128)(2,1)} custom-call(s32[1]{0:T(128)} %bitcast.2.side_ref, bf16[512,2304]{1,0:T(8,128)(2,1)} %convolution_convert_fusion.3.q_ref.k_ref.v_ref, bf16[512,2304]{1,0:T(8,128)(2,1)} %convolution_convert_fusion.3.q_ref.k_ref.v_ref, bf16[512,2304]{1,0:T(8,128)(2,1)} %convolution_convert_fusion.3.q_ref.k_ref.v_ref, ...), custom_call_target="tpu_custom_call" | custom-call | flops 1006632960 | bytes 5505024 | tf_op jit(solution)/shard_map/attend_back/pallas_call | solution.py:164
  417.4 3.0 multiply_reduce_fusion.9
  427.7 7.7 %add_convert_fusion = bf16[768,2304]{1,0:T(8,128)(2,1)} fusion(f32[768,2304]{1,0:T(8,128)} %fusion.130, bf16[512,2304]{1,0:T(8,128)(2,1)} %attend_back.3, bf16[512,768]{1,0:T(8,128)(2,1)S(1)} %copy-done.1, f32[768]{0:T(1024)} %copy-done.113, f32[768]{0:T(1024)S(1)} %copy-done.79, f32[512]{0:T(512)} %add_rsqrt_fusion.3, f32[512]{0:T(512)} %copy-done.80), kind=kOutput, calls=%fused_computation.12 | convolution fusion | flops 1817837568 | bytes 13772800 | tf_op jit(solution)/shard_map/dot_general | solution.py:34
  437.3 8.0 %collective-permute-done.55 = bf16[2,2,24,1280]{3,2,1,0:T(8,128)(2,1)S(1)} collective-permute-done((bf16[2,2,24,1280]{3,2,1,0:T(8,128)(2,1)}, bf16[2,2,24,1280]{3,2,1,0:T(8,128)(2,1)S(1)}, u32[]{:S(2)}, u32[]{:S(2)}) %collective-permute-start.55) | collective-permute-done | bytes 245792 | tf_op jit(solution)/shard_map/ppermute | solution.py:378
  453.6 4.9 pack.5
  458.8 3.3 broadcast_select_fusion
  476.0 3.3 collective-permute-done.76
  480.9 3.1 collective-permute-done.64
  484.1 5.3 %collective-permute-done.63 = bf16[4,2,24,896]{3,2,1,0:T(8,128)(2,1)S(1)} collective-permute-done((bf16[4,2,24,896]{3,2,1,0:T(8,128)(2,1)S(1)}, bf16[4,2,24,896]{3,2,1,0:T(8,128)(2,1)S(1)}, u32[]{:S(2)}, u32[]{:S(2)}) %collective-permute-start.63) | collective-permute-done | bytes 344096 | tf_op jit(solution)/shard_map/ppermute | solution.py:378
  504.4 3.5 collective-permute-start.72
  507.9 2.8 collective-permute-done.72
  (678 shorter events, 209.4 us)
Async XLA Ops:
  5.2 19.2 %collective-permute-start = (bf16[24,3200]{1,0:T(8,128)(2,1)}, bf16[24,3200]{1,0:T(8,128)(2,1)S(1)}, u32[]{:S(2)}, u32[]{:S(2)}) collective-permute-start(bf16[24,3200]{1,0:T(8,128)(2,1)} %get-tuple-element.126), channel_id=1, source_target_pairs={{0,16},{1,17},{2,18},{3,19},{4,20},{5,21},{6,22},{7,23},{8,24},{9,... | collective-permute-start | bytes 460808 | tf_op jit(solution)/shard_map/ppermute | solution.py:378
  29.3 23.9 %collective-permute-start.10 = (bf16[24,8448]{1,0:T(8,128)(2,1)}, bf16[24,8448]{1,0:T(8,128)(2,1)S(1)}, u32[]{:S(2)}, u32[]{:S(2)}) collective-permute-start(bf16[24,8448]{1,0:T(8,128)(2,1)} %get-tuple-element.131), channel_id=1, source_target_pairs={{0,16},{1,17},{2,18},{3,19},{4,20},{5,21},{6,22},{7,23},{8,24},{9,... | collective-permute-start | bytes 1216520 | tf_op jit(solution)/shard_map/ppermute | solution.py:378
  29.7 15.3 %collective-permute-start.2 = (bf16[2,2,24,1024]{3,2,1,0:T(8,128)(2,1)S(1)}, bf16[2,2,24,1024]{3,2,1,0:T(8,128)(2,1)S(1)}, u32[]{:S(2)}, u32[]{:S(2)}) collective-permute-start(bf16[2,2,24,1024]{3,2,1,0:T(8,128)(2,1)S(1)} %pad_maximum_fusion.26), channel_id=1, source_target_pairs={{0,4},{1,5},{2,6},{3,7},{4,0},{5,1},{6,2},{7,3},{8,12},{9,13},{10,... | collective-permute-start | bytes 589832 | tf_op jit(solution)/shard_map/ppermute | solution.py:378
  30.8 12.9 %collective-permute-start.5 = (bf16[2,2,24,1024]{3,2,1,0:T(8,128)(2,1)S(1)}, bf16[2,2,24,1024]{3,2,1,0:T(8,128)(2,1)S(1)}, u32[]{:S(2)}, u32[]{:S(2)}) collective-permute-start(bf16[2,2,24,1024]{3,2,1,0:T(8,128)(2,1)S(1)} %pad_maximum_fusion.27), channel_id=1, source_target_pairs={{0,8},{1,9},{2,10},{3,11},{4,12},{5,13},{6,14},{7,15},{8,0},{9,1},... | collective-permute-start | bytes 589832 | tf_op jit(solution)/shard_map/ppermute | solution.py:378
  33.9 14.4 %collective-permute-start.8 = (bf16[2,2,24,1152]{3,2,1,0:T(8,128)(2,1)S(1)}, bf16[2,2,24,1152]{3,2,1,0:T(8,128)(2,1)S(1)}, u32[]{:S(2)}, u32[]{:S(2)}) collective-permute-start(bf16[2,2,24,1152]{3,2,1,0:T(8,128)(2,1)S(1)} %pad_maximum_fusion.25), channel_id=1, source_target_pairs={{0,1},{1,0},{2,3},{3,2},{4,5},{5,4},{6,7},{7,6},{8,9},{9,8},{10,11... | collective-permute-start | bytes 663560 | tf_op jit(solution)/shard_map/ppermute | solution.py:378
  45.8 11.8 %collective-permute-start.3 = (bf16[4,2,24,1024]{3,2,1,0:T(8,128)(2,1)}, bf16[4,2,24,1024]{3,2,1,0:T(8,128)(2,1)}, u32[]{:S(2)}, u32[]{:S(2)}) collective-permute-start(bf16[4,2,24,1024]{3,2,1,0:T(8,128)(2,1)} %pad_maximum_fusion.15.refs_0_), channel_id=1, source_target_pairs={{0,8},{1,9},{2,10},{3,11},{4,12},{5,13},{6,14},{7,15},{8,0},{9,1},... | collective-permute-start | bytes 1179656 | tf_op jit(solution)/shard_map/ppermute | solution.py:378
  53.2 16.4 %collective-permute-start.14 = (bf16[4,2,24,1024]{3,2,1,0:T(8,128)(2,1)}, bf16[4,2,24,1024]{3,2,1,0:T(8,128)(2,1)S(1)}, u32[]{:S(2)}, u32[]{:S(2)}) collective-permute-start(bf16[4,2,24,1024]{3,2,1,0:T(8,128)(2,1)} %pad_maximum_fusion.16.refs_4_), channel_id=1, source_target_pairs={{0,2},{1,3},{2,0},{3,1},{4,6},{5,7},{6,4},{7,5},{8,10},{9,11},{10,... | collective-permute-start | bytes 1179656 | tf_op jit(solution)/shard_map/ppermute | solution.py:378
  53.2 23.2 %collective-permute-start.12 = (bf16[4,2,24,1024]{3,2,1,0:T(8,128)(2,1)}, bf16[4,2,24,1024]{3,2,1,0:T(8,128)(2,1)S(1)}, u32[]{:S(2)}, u32[]{:S(2)}) collective-permute-start(bf16[4,2,24,1024]{3,2,1,0:T(8,128)(2,1)} %pad_maximum_fusion.15.refs_0_), channel_id=1, source_target_pairs={{0,2},{1,3},{2,0},{3,1},{4,6},{5,7},{6,4},{7,5},{8,10},{9,11},{10,... | collective-permute-start | bytes 1179656 | tf_op jit(solution)/shard_map/ppermute | solution.py:378
  53.8 22.9 %collective-permute-start.16 = (bf16[4,2,24,1152]{3,2,1,0:T(8,128)(2,1)S(1)}, bf16[4,2,24,1152]{3,2,1,0:T(8,128)(2,1)S(1)}, u32[]{:S(2)}, u32[]{:S(2)}) collective-permute-start(bf16[4,2,24,1152]{3,2,1,0:T(8,128)(2,1)S(1)} %pad_maximum_fusion.14.refs_8_), channel_id=1, source_target_pairs={{0,2},{1,3},{2,0},{3,1},{4,6},{5,7},{6,4},{7,5},{8,10},{9,11},{10,... | collective-permute-start | bytes 1327112 | tf_op jit(solution)/shard_map/ppermute | solution.py:378
  59.2 10.5 %collective-permute-start.18 = (bf16[1,2,24,2816]{3,2,1,0:T(8,128)(2,1)S(1)}, bf16[1,2,24,2816]{3,2,1,0:T(8,128)(2,1)S(1)}, u32[]{:S(2)}, u32[]{:S(2)}) collective-permute-start(bf16[1,2,24,2816]{3,2,1,0:T(8,128)(2,1)S(1)} %maximum_bitcast_fusion), channel_id=1, source_target_pairs={{0,1},{1,0},{2,3},{3,2},{4,5},{5,4},{6,7},{7,6},{8,9},{9,8},{10,11... | collective-permute-start | bytes 811016 | tf_op jit(solution)/shard_map/ppermute | solution.py:378
  76.4 37.7 %collective-permute-start.11 = (bf16[512,768]{1,0:T(8,128)(2,1)}, bf16[512,768]{1,0:T(8,128)(2,1)S(1)}, u32[]{:S(2)}, u32[]{:S(2)}) collective-permute-start(bf16[512,768]{1,0:T(8,128)(2,1)} %pad_select_fusion), channel_id=1, source_target_pairs={{0,16},{1,17},{2,18},{3,19},{4,20},{5,21},{6,22},{7,23},{8,24},{9,... | collective-permute-start | bytes 2359304 | tf_op jit(solution)/shard_map/ppermute | solution.py:378
  76.8 42.5 %collective-permute-start.19 = (bf16[2,2,24,2816]{3,2,1,0:T(8,128)(2,1)}, bf16[2,2,24,2816]{3,2,1,0:T(8,128)(2,1)}, u32[]{:S(2)}, u32[]{:S(2)}) collective-permute-start(bf16[2,2,24,2816]{3,2,1,0:T(8,128)(2,1)} %pad_maximum_fusion.11), channel_id=1, source_target_pairs={{0,4},{1,5},{2,6},{3,7},{4,0},{5,1},{6,2},{7,3},{8,12},{9,13},{10,... | collective-permute-start | bytes 1622024 | tf_op jit(solution)/shard_map/ppermute | solution.py:378
  77.3 39.0 %collective-permute-start.24 = (bf16[2,2,24,2816]{3,2,1,0:T(8,128)(2,1)}, bf16[2,2,24,2816]{3,2,1,0:T(8,128)(2,1)}, u32[]{:S(2)}, u32[]{:S(2)}) collective-permute-start(bf16[2,2,24,2816]{3,2,1,0:T(8,128)(2,1)} %pad_maximum_fusion.12), channel_id=1, source_target_pairs={{0,8},{1,9},{2,10},{3,11},{4,12},{5,13},{6,14},{7,15},{8,0},{9,1},... | collective-permute-start | bytes 1622024 | tf_op jit(solution)/shard_map/ppermute | solution.py:378
  79.1 35.2 %collective-permute-start.29 = (bf16[2,2,24,2816]{3,2,1,0:T(8,128)(2,1)}, bf16[2,2,24,2816]{3,2,1,0:T(8,128)(2,1)}, u32[]{:S(2)}, u32[]{:S(2)}) collective-permute-start(bf16[2,2,24,2816]{3,2,1,0:T(8,128)(2,1)} %pad_maximum_fusion.13), channel_id=1, source_target_pairs={{0,1},{1,0},{2,3},{3,2},{4,5},{5,4},{6,7},{7,6},{8,9},{9,8},{10,11... | collective-permute-start | bytes 1622024 | tf_op jit(solution)/shard_map/ppermute | solution.py:378
  115.6 20.9 %collective-permute-start.31 = (bf16[4,2,24,2816]{3,2,1,0:T(8,128)(2,1)S(1)}, bf16[4,2,24,2816]{3,2,1,0:T(8,128)(2,1)}, u32[]{:S(2)}, u32[]{:S(2)}) collective-permute-start(bf16[4,2,24,2816]{3,2,1,0:T(8,128)(2,1)S(1)} %pad_maximum_fusion.8.refs_8_), channel_id=1, source_target_pairs={{0,2},{1,3},{2,0},{3,1},{4,6},{5,7},{6,4},{7,5},{8,10},{9,11},{10,... | collective-permute-start | bytes 3244040 | tf_op jit(solution)/shard_map/ppermute | solution.py:378
  115.8 26.3 %collective-permute-start.30 = (bf16[4,2,24,2816]{3,2,1,0:T(8,128)(2,1)S(1)}, bf16[4,2,24,2816]{3,2,1,0:T(8,128)(2,1)}, u32[]{:S(2)}, u32[]{:S(2)}) collective-permute-start(bf16[4,2,24,2816]{3,2,1,0:T(8,128)(2,1)S(1)} %pad_maximum_fusion.8.refs_8_), channel_id=1, source_target_pairs={{0,4},{1,5},{2,6},{3,7},{4,0},{5,1},{6,2},{7,3},{8,12},{9,13},{10,... | collective-permute-start | bytes 3244040 | tf_op jit(solution)/shard_map/ppermute | solution.py:378
  118.5 26.2 %collective-permute-start.25 = (bf16[4,2,24,2816]{3,2,1,0:T(8,128)(2,1)}, bf16[4,2,24,2816]{3,2,1,0:T(8,128)(2,1)}, u32[]{:S(2)}, u32[]{:S(2)}) collective-permute-start(bf16[4,2,24,2816]{3,2,1,0:T(8,128)(2,1)} %pad_maximum_fusion.7.refs_4_), channel_id=1, source_target_pairs={{0,1},{1,0},{2,3},{3,2},{4,5},{5,4},{6,7},{7,6},{8,9},{9,8},{10,11... | collective-permute-start | bytes 3244040 | tf_op jit(solution)/shard_map/ppermute | solution.py:378
  121.7 25.9 %collective-permute-start.20 = (bf16[4,2,24,2816]{3,2,1,0:T(8,128)(2,1)}, bf16[4,2,24,2816]{3,2,1,0:T(8,128)(2,1)}, u32[]{:S(2)}, u32[]{:S(2)}) collective-permute-start(bf16[4,2,24,2816]{3,2,1,0:T(8,128)(2,1)} %pad_maximum_fusion.6.refs_0_), channel_id=1, source_target_pairs={{0,8},{1,9},{2,10},{3,11},{4,12},{5,13},{6,14},{7,15},{8,0},{9,1},... | collective-permute-start | bytes 3244040 | tf_op jit(solution)/shard_map/ppermute | solution.py:378
  136.5 15.8 %collective-permute-start.26 = (bf16[4,2,24,2816]{3,2,1,0:T(8,128)(2,1)}, bf16[4,2,24,2816]{3,2,1,0:T(8,128)(2,1)}, u32[]{:S(2)}, u32[]{:S(2)}) collective-permute-start(bf16[4,2,24,2816]{3,2,1,0:T(8,128)(2,1)} %pad_maximum_fusion.7.refs_4_), channel_id=1, source_target_pairs={{0,2},{1,3},{2,0},{3,1},{4,6},{5,7},{6,4},{7,5},{8,10},{9,11},{10,... | collective-permute-start | bytes 3244040 | tf_op jit(solution)/shard_map/ppermute | solution.py:378
  136.5 15.8 %collective-permute-start.21 = (bf16[4,2,24,2816]{3,2,1,0:T(8,128)(2,1)}, bf16[4,2,24,2816]{3,2,1,0:T(8,128)(2,1)}, u32[]{:S(2)}, u32[]{:S(2)}) collective-permute-start(bf16[4,2,24,2816]{3,2,1,0:T(8,128)(2,1)} %pad_maximum_fusion.6.refs_0_), channel_id=1, source_target_pairs={{0,2},{1,3},{2,0},{3,1},{4,6},{5,7},{6,4},{7,5},{8,10},{9,11},{10,... | collective-permute-start | bytes 3244040 | tf_op jit(solution)/shard_map/ppermute | solution.py:378
  142.1 10.3 %collective-permute-start.32 = (bf16[4,2,24,2816]{3,2,1,0:T(8,128)(2,1)}, bf16[4,2,24,2816]{3,2,1,0:T(8,128)(2,1)}, u32[]{:S(2)}, u32[]{:S(2)}) collective-permute-start(bf16[4,2,24,2816]{3,2,1,0:T(8,128)(2,1)} %collective-permute-done.30.refs_9_), channel_id=1, source_target_pairs={{0,2},{1,3},{2,0},{3,1},{4,6},{5,7},{6,4},{7,5},{8,10},{9,11},{10,... | collective-permute-start | bytes 3244040 | tf_op jit(solution)/shard_map/ppermute | solution.py:378
  289.9 11.7 %collective-permute-start.39 = (bf16[8,2,24,1792]{3,2,1,0:T(8,128)(2,1)}, bf16[8,2,24,1792]{3,2,1,0:T(8,128)(2,1)}, u32[]{:S(2)}, u32[]{:S(2)}) collective-permute-start(bf16[8,2,24,1792]{3,2,1,0:T(8,128)(2,1)} %get-tuple-element.159), channel_id=1, source_target_pairs={{0,2},{1,3},{2,0},{3,1},{4,6},{5,7},{6,4},{7,5},{8,10},{9,11},{10,... | collective-permute-start | bytes 4128776 | tf_op jit(solution)/shard_map/ppermute | solution.py:378
  292.7 11.1 %collective-permute-start.40 = (bf16[8,2,24,1792]{3,2,1,0:T(8,128)(2,1)}, bf16[8,2,24,1792]{3,2,1,0:T(8,128)(2,1)}, u32[]{:S(2)}, u32[]{:S(2)}) collective-permute-start(bf16[8,2,24,1792]{3,2,1,0:T(8,128)(2,1)} %get-tuple-element.161), channel_id=1, source_target_pairs={{0,2},{1,3},{2,0},{3,1},{4,6},{5,7},{6,4},{7,5},{8,10},{9,11},{10,... | collective-permute-start | bytes 4128776 | tf_op jit(solution)/shard_map/ppermute | solution.py:378
  315.9 17.7 %collective-permute-start.41 = (bf16[4,2,24,1792]{3,2,1,0:T(8,128)(2,1)}, bf16[4,2,24,1792]{3,2,1,0:T(8,128)(2,1)}, u32[]{:S(2)}, u32[]{:S(2)}) collective-permute-start(bf16[4,2,24,1792]{3,2,1,0:T(8,128)(2,1)} %add_convert_fusion.7), channel_id=1, source_target_pairs={{0,8},{1,9},{2,10},{3,11},{4,12},{5,13},{6,14},{7,15},{8,0},{9,1},... | collective-permute-start | bytes 2064392 | tf_op jit(solution)/shard_map/ppermute | solution.py:378
  316.7 19.0 %collective-permute-start.42 = (bf16[4,2,24,1792]{3,2,1,0:T(8,128)(2,1)}, bf16[4,2,24,1792]{3,2,1,0:T(8,128)(2,1)}, u32[]{:S(2)}, u32[]{:S(2)}) collective-permute-start(bf16[4,2,24,1792]{3,2,1,0:T(8,128)(2,1)} %add_convert_fusion.6), channel_id=1, source_target_pairs={{0,1},{1,0},{2,3},{3,2},{4,5},{5,4},{6,7},{7,6},{8,9},{9,8},{10,11... | collective-permute-start | bytes 2064392 | tf_op jit(solution)/shard_map/ppermute | solution.py:378
  328.9 16.8 %collective-permute-start.43 = (bf16[4,2,24,1792]{3,2,1,0:T(8,128)(2,1)S(1)}, bf16[4,2,24,1792]{3,2,1,0:T(8,128)(2,1)S(1)}, u32[]{:S(2)}, u32[]{:S(2)}) collective-permute-start(bf16[4,2,24,1792]{3,2,1,0:T(8,128)(2,1)S(1)} %copy-done.41), channel_id=1, source_target_pairs={{0,4},{1,5},{2,6},{3,7},{4,0},{5,1},{6,2},{7,3},{8,12},{9,13},{10,... | collective-permute-start | bytes 2064392 | tf_op jit(solution)/shard_map/ppermute | solution.py:378
  330.4 33.2 %collective-permute-start.47 = (bf16[8,2,24,1280]{3,2,1,0:T(8,128)(2,1)}, bf16[8,2,24,1280]{3,2,1,0:T(8,128)(2,1)}, u32[]{:S(2)}, u32[]{:S(2)}) collective-permute-start(bf16[8,2,24,1280]{3,2,1,0:T(8,128)(2,1)} %get-tuple-element.180), channel_id=1, source_target_pairs={{0,2},{1,3},{2,0},{3,1},{4,6},{5,7},{6,4},{7,5},{8,10},{9,11},{10,... | collective-permute-start | bytes 2949128 | tf_op jit(solution)/shard_map/ppermute | solution.py:378
  330.4 36.5 %collective-permute-start.48 = (bf16[8,2,24,1280]{3,2,1,0:T(8,128)(2,1)}, bf16[8,2,24,1280]{3,2,1,0:T(8,128)(2,1)}, u32[]{:S(2)}, u32[]{:S(2)}) collective-permute-start(bf16[8,2,24,1280]{3,2,1,0:T(8,128)(2,1)} %get-tuple-element.182), channel_id=1, source_target_pairs={{0,2},{1,3},{2,0},{3,1},{4,6},{5,7},{6,4},{7,5},{8,10},{9,11},{10,... | collective-permute-start | bytes 2949128 | tf_op jit(solution)/shard_map/ppermute | solution.py:378
  333.6 35.4 %collective-permute-start.49 = (bf16[8,2,24,1280]{3,2,1,0:T(8,128)(2,1)}, bf16[8,2,24,1280]{3,2,1,0:T(8,128)(2,1)}, u32[]{:S(2)}, u32[]{:S(2)}) collective-permute-start(bf16[8,2,24,1280]{3,2,1,0:T(8,128)(2,1)} %get-tuple-element.184), channel_id=1, source_target_pairs={{0,2},{1,3},{2,0},{3,1},{4,6},{5,7},{6,4},{7,5},{8,10},{9,11},{10,... | collective-permute-start | bytes 2949128 | tf_op jit(solution)/shard_map/ppermute | solution.py:378
  348.4 22.7 %collective-permute-start.44 = (bf16[2,2,24,1792]{3,2,1,0:T(8,128)(2,1)}, bf16[2,2,24,1792]{3,2,1,0:T(8,128)(2,1)}, u32[]{:S(2)}, u32[]{:S(2)}) collective-permute-start(bf16[2,2,24,1792]{3,2,1,0:T(8,128)(2,1)} %add_convert_fusion.14), channel_id=1, source_target_pairs={{0,4},{1,5},{2,6},{3,7},{4,0},{5,1},{6,2},{7,3},{8,12},{9,13},{10,... | collective-permute-start | bytes 1032200 | tf_op jit(solution)/shard_map/ppermute | solution.py:378
  349.9 22.4 %collective-permute-start.45 = (bf16[2,2,24,1792]{3,2,1,0:T(8,128)(2,1)}, bf16[2,2,24,1792]{3,2,1,0:T(8,128)(2,1)S(1)}, u32[]{:S(2)}, u32[]{:S(2)}) collective-permute-start(bf16[2,2,24,1792]{3,2,1,0:T(8,128)(2,1)} %add_convert_fusion.13), channel_id=1, source_target_pairs={{0,8},{1,9},{2,10},{3,11},{4,12},{5,13},{6,14},{7,15},{8,0},{9,1},... | collective-permute-start | bytes 1032200 | tf_op jit(solution)/shard_map/ppermute | solution.py:378
  374.8 28.1 %collective-permute-start.57 = (bf16[1,2,24,1792]{3,2,1,0:T(8,128)(2,1)S(1)}, bf16[1,2,24,1792]{3,2,1,0:T(8,128)(2,1)S(1)}, u32[]{:S(2)}, u32[]{:S(2)}) collective-permute-start(bf16[1,2,24,1792]{3,2,1,0:T(8,128)(2,1)S(1)} %add_convert_fusion.23), channel_id=1, source_target_pairs={{0,1},{1,0},{2,3},{3,2},{4,5},{5,4},{6,7},{7,6},{8,9},{9,8},{10,11... | collective-permute-start | bytes 516104 | tf_op jit(solution)/shard_map/ppermute | solution.py:378
  375.7 30.7 %collective-permute-start.58 = (bf16[1,2,24,1792]{3,2,1,0:T(8,128)(2,1)S(1)}, bf16[1,2,24,1792]{3,2,1,0:T(8,128)(2,1)S(1)}, u32[]{:S(2)}, u32[]{:S(2)}) collective-permute-start(bf16[1,2,24,1792]{3,2,1,0:T(8,128)(2,1)S(1)} %add_convert_fusion.22), channel_id=1, source_target_pairs={{0,4},{1,5},{2,6},{3,7},{4,0},{5,1},{6,2},{7,3},{8,12},{9,13},{10,... | collective-permute-start | bytes 516104 | tf_op jit(solution)/shard_map/ppermute | solution.py:378
  376.2 32.4 %collective-permute-start.59 = (bf16[1,2,24,1792]{3,2,1,0:T(8,128)(2,1)S(1)}, bf16[1,2,24,1792]{3,2,1,0:T(8,128)(2,1)S(1)}, u32[]{:S(2)}, u32[]{:S(2)}) collective-permute-start(bf16[1,2,24,1792]{3,2,1,0:T(8,128)(2,1)S(1)} %add_convert_fusion.21), channel_id=1, source_target_pairs={{0,8},{1,9},{2,10},{3,11},{4,12},{5,13},{6,14},{7,15},{8,0},{9,1},... | collective-permute-start | bytes 516104 | tf_op jit(solution)/shard_map/ppermute | solution.py:378
  377.0 33.6 %collective-permute-start.50 = (bf16[4,2,24,1280]{3,2,1,0:T(8,128)(2,1)}, bf16[4,2,24,1280]{3,2,1,0:T(8,128)(2,1)}, u32[]{:S(2)}, u32[]{:S(2)}) collective-permute-start(bf16[4,2,24,1280]{3,2,1,0:T(8,128)(2,1)} %add_convert_fusion.10), channel_id=1, source_target_pairs={{0,8},{1,9},{2,10},{3,11},{4,12},{5,13},{6,14},{7,15},{8,0},{9,1},... | collective-permute-start | bytes 1474568 | tf_op jit(solution)/shard_map/ppermute | solution.py:378
  378.3 34.5 %collective-permute-start.51 = (bf16[4,2,24,1280]{3,2,1,0:T(8,128)(2,1)}, bf16[4,2,24,1280]{3,2,1,0:T(8,128)(2,1)}, u32[]{:S(2)}, u32[]{:S(2)}) collective-permute-start(bf16[4,2,24,1280]{3,2,1,0:T(8,128)(2,1)} %add_convert_fusion.9), channel_id=1, source_target_pairs={{0,1},{1,0},{2,3},{3,2},{4,5},{5,4},{6,7},{7,6},{8,9},{9,8},{10,11... | collective-permute-start | bytes 1474568 | tf_op jit(solution)/shard_map/ppermute | solution.py:378
  402.9 11.9 %collective-permute-start.52 = (bf16[4,2,24,1280]{3,2,1,0:T(8,128)(2,1)}, bf16[4,2,24,1280]{3,2,1,0:T(8,128)(2,1)S(1)}, u32[]{:S(2)}, u32[]{:S(2)}) collective-permute-start(bf16[4,2,24,1280]{3,2,1,0:T(8,128)(2,1)} %add_convert_fusion.8), channel_id=1, source_target_pairs={{0,4},{1,5},{2,6},{3,7},{4,0},{5,1},{6,2},{7,3},{8,12},{9,13},{10,... | collective-permute-start | bytes 1474568 | tf_op jit(solution)/shard_map/ppermute | solution.py:378
  406.5 52.1 %collective-permute-start.53 = (bf16[512,768]{1,0:T(8,128)(2,1)}, bf16[512,768]{1,0:T(8,128)(2,1)S(1)}, u32[]{:S(2)}, u32[]{:S(2)}) collective-permute-start(bf16[512,768]{1,0:T(8,128)(2,1)} %fusion.9), channel_id=1, source_target_pairs={{0,16},{1,17},{2,18},{3,19},{4,20},{5,21},{6,22},{7,23},{8,24},{9,... | collective-permute-start | bytes 2359304 | tf_op jit(solution)/shard_map/ppermute | solution.py:378
  425.0 10.5 %collective-permute-start.54 = (bf16[2,2,24,1280]{3,2,1,0:T(8,128)(2,1)}, bf16[2,2,24,1280]{3,2,1,0:T(8,128)(2,1)S(1)}, u32[]{:S(2)}, u32[]{:S(2)}) collective-permute-start(bf16[2,2,24,1280]{3,2,1,0:T(8,128)(2,1)} %add_convert_fusion.19), channel_id=1, source_target_pairs={{0,4},{1,5},{2,6},{3,7},{4,0},{5,1},{6,2},{7,3},{8,12},{9,13},{10,... | collective-permute-start | bytes 737288 | tf_op jit(solution)/shard_map/ppermute | solution.py:378
  425.5 19.8 %collective-permute-start.55 = (bf16[2,2,24,1280]{3,2,1,0:T(8,128)(2,1)}, bf16[2,2,24,1280]{3,2,1,0:T(8,128)(2,1)S(1)}, u32[]{:S(2)}, u32[]{:S(2)}) collective-permute-start(bf16[2,2,24,1280]{3,2,1,0:T(8,128)(2,1)} %add_convert_fusion.18), channel_id=1, source_target_pairs={{0,8},{1,9},{2,10},{3,11},{4,12},{5,13},{6,14},{7,15},{8,0},{9,1},... | collective-permute-start | bytes 737288 | tf_op jit(solution)/shard_map/ppermute | solution.py:378
  426.7 20.9 %collective-permute-start.56 = (bf16[2,2,24,1280]{3,2,1,0:T(8,128)(2,1)}, bf16[2,2,24,1280]{3,2,1,0:T(8,128)(2,1)S(1)}, u32[]{:S(2)}, u32[]{:S(2)}) collective-permute-start(bf16[2,2,24,1280]{3,2,1,0:T(8,128)(2,1)} %add_convert_fusion.17), channel_id=1, source_target_pairs={{0,1},{1,0},{2,3},{3,2},{4,5},{5,4},{6,7},{7,6},{8,9},{9,8},{10,11... | collective-permute-start | bytes 737288 | tf_op jit(solution)/shard_map/ppermute | solution.py:378
  450.1 13.1 %collective-permute-start.73 = (bf16[1,2,24,1280]{3,2,1,0:T(8,128)(2,1)}, bf16[1,2,24,1280]{3,2,1,0:T(8,128)(2,1)}, u32[]{:S(2)}, u32[]{:S(2)}) collective-permute-start(bf16[1,2,24,1280]{3,2,1,0:T(8,128)(2,1)} %add_convert_fusion.26), channel_id=1, source_target_pairs={{0,8},{1,9},{2,10},{3,11},{4,12},{5,13},{6,14},{7,15},{8,0},{9,1},... | collective-permute-start | bytes 368648 | tf_op jit(solution)/shard_map/ppermute | solution.py:378
  450.1 14.9 %collective-permute-start.74 = (bf16[1,2,24,1280]{3,2,1,0:T(8,128)(2,1)}, bf16[1,2,24,1280]{3,2,1,0:T(8,128)(2,1)}, u32[]{:S(2)}, u32[]{:S(2)}) collective-permute-start(bf16[1,2,24,1280]{3,2,1,0:T(8,128)(2,1)} %add_convert_fusion.28), channel_id=1, source_target_pairs={{0,1},{1,0},{2,3},{3,2},{4,5},{5,4},{6,7},{7,6},{8,9},{9,8},{10,11... | collective-permute-start | bytes 368648 | tf_op jit(solution)/shard_map/ppermute | solution.py:378
  451.0 15.3 %collective-permute-start.75 = (bf16[1,2,24,1280]{3,2,1,0:T(8,128)(2,1)}, bf16[1,2,24,1280]{3,2,1,0:T(8,128)(2,1)}, u32[]{:S(2)}, u32[]{:S(2)}) collective-permute-start(bf16[1,2,24,1280]{3,2,1,0:T(8,128)(2,1)} %add_convert_fusion.27), channel_id=1, source_target_pairs={{0,4},{1,5},{2,6},{3,7},{4,0},{5,1},{6,2},{7,3},{8,12},{9,13},{10,... | collective-permute-start | bytes 368648 | tf_op jit(solution)/shard_map/ppermute | solution.py:378
  451.6 17.0 %collective-permute-start.77 = (bf16[24,5376]{1,0:T(8,128)(2,1)}, bf16[24,5376]{1,0:T(8,128)(2,1)}, u32[]{:S(2)}, u32[]{:S(2)}) collective-permute-start(bf16[24,5376]{1,0:T(8,128)(2,1)} %pad_maximum_fusion.22), channel_id=1, source_target_pairs={{0,16},{1,17},{2,18},{3,19},{4,20},{5,21},{6,22},{7,23},{8,24},{9,... | collective-permute-start | bytes 774152 | tf_op jit(solution)/shard_map/ppermute | solution.py:378
  458.5 11.8 %collective-permute-start.61 = (bf16[8,2,24,768]{3,2,1,0:T(8,128)(2,1)}, bf16[8,2,24,768]{3,2,1,0:T(8,128)(2,1)S(1)}, u32[]{:S(2)}, u32[]{:S(2)}) collective-permute-start(bf16[8,2,24,768]{3,2,1,0:T(8,128)(2,1)} %get-tuple-element.203), channel_id=1, source_target_pairs={{0,2},{1,3},{2,0},{3,1},{4,6},{5,7},{6,4},{7,5},{8,10},{9,11},{10,... | collective-permute-start | bytes 1769480 | tf_op jit(solution)/shard_map/ppermute | solution.py:378
  467.6 11.7 %collective-permute-start.76 = (bf16[24,3840]{1,0:T(8,128)(2,1)S(1)}, bf16[24,3840]{1,0:T(8,128)(2,1)S(1)}, u32[]{:S(2)}, u32[]{:S(2)}) collective-permute-start(bf16[24,3840]{1,0:T(8,128)(2,1)S(1)} %pad_maximum_fusion.28), channel_id=1, source_target_pairs={{0,16},{1,17},{2,18},{3,19},{4,20},{5,21},{6,22},{7,23},{8,24},{9,... | collective-permute-start | bytes 552968 | tf_op jit(solution)/shard_map/ppermute | solution.py:378
  470.7 13.3 %collective-permute-start.64 = (bf16[4,2,24,768]{3,2,1,0:T(8,128)(2,1)S(1)}, bf16[4,2,24,768]{3,2,1,0:T(8,128)(2,1)S(1)}, u32[]{:S(2)}, u32[]{:S(2)}) collective-permute-start(bf16[4,2,24,768]{3,2,1,0:T(8,128)(2,1)S(1)} %add_convert_fusion.16), channel_id=1, source_target_pairs={{0,8},{1,9},{2,10},{3,11},{4,12},{5,13},{6,14},{7,15},{8,0},{9,1},... | collective-permute-start | bytes 884744 | tf_op jit(solution)/shard_map/ppermute | solution.py:378
  (179 other events, 1876.7 us)

commit v2 on v1

--- a/solution.py
+++ b/solution.py
@@ -48,17 +48,13 @@
     return inverse * (grad_hat - first - hat_rows * second)
 
 
-def gelu_tanh(values):
-    return (
-        0.5 * values * (1.0 + jnp.tanh(GELU_COEF * (values + GELU_CUBE * values * values * values)))
-    )
-
-
-def gelu_slope(values):
-    tanh_val = jnp.tanh(GELU_COEF * (values + GELU_CUBE * values * values * values))
-    return 0.5 * (1.0 + tanh_val) + 0.5 * values * (1.0 - tanh_val * tanh_val) * GELU_COEF * (
-        1.0 + 3.0 * GELU_CUBE * values * values
-    )
+def gelu_parts(values):
+    square = values * values
+    inner = values * (GELU_COEF + (GELU_COEF * GELU_CUBE) * square)
+    share = 0.5 + 0.5 * jnp.tanh(inner)
+    active = values * share
+    rise = 2.0 * GELU_COEF + (6.0 * GELU_COEF * GELU_CUBE) * square
+    return active, share + active * (1.0 - share) * rise
 
 
 def pair_bias(side_ref, seq_len, group):
@@ -390,21 +386,24 @@
     return masks
 
 
-def gather_chain(links, order, start):
-    held = start[None]
-    for bit in order[:-1]:
-        held = jnp.concatenate((held, links.swap(held, bit)), axis=0)
-    far = links.swap(held, order[-1])
-    pieces = [held, far, links.swap(held, links.core), links.swap(far, links.core)]
-    masks = chain_masks(order)
-    return pieces, masks + [mask ^ links.core for mask in masks]
-
-
-def gather_pieces(links, group, kept, arrived):
-    return [
-        gather_chain(links, order, jnp.stack((kept[chain], arrived[:, start:stop])))
-        for chain, (order, (start, stop)) in enumerate(zip(links.orders, group.bounds))
-    ]
+def gather_near(links, group, kept, arrived):
+    chains = []
+    for chain, (order, (start, stop)) in enumerate(zip(links.orders, group.bounds)):
+        held = jnp.stack((kept[chain], arrived[:, start:stop]))[None]
+        for bit in order[:-1]:
+            held = jnp.concatenate((held, links.swap(held, bit)), axis=0)
+        chains.append(held)
+    return chains
+
+
+def gather_far(links, near):
+    chains = []
+    for order, held in zip(links.orders, near):
+        far = links.swap(held, order[-1])
+        pieces = [held, far, links.swap(held, links.core), links.swap(far, links.core)]
+        masks = chain_masks(order)
+        chains.append((pieces, masks + [mask ^ links.core for mask in masks]))
+    return chains
 
 
 def place_pieces(links, group, chains, rows):
@@ -438,51 +437,81 @@
     return result
 
 
-class ChainSum:
-    def __init__(self, links, order, keep, send):
-        self.links, self.bits, self.terms = links, list(order[::-1]), [keep]
-        self.pending = links.swap(send, links.core)
-
-    def total(self, rows):
-        return sum(term[rows].astype(F32) for term in self.terms)
-
-    def prepare(self):
-        self.terms.append(self.pending)
-        near = self.pending.shape[0] // 2
-        self.send = self.total(slice(near, 2 * near)).astype(LOW)
-        self.terms = [term[:near] for term in self.terms]
-
-    def launch(self):
-        self.pending = self.links.swap(self.send, self.bits.pop(0))
-
-    def result(self):
-        self.terms.append(self.pending)
-        return self.total(0)
+def far_kernel(counts, *refs):
+    outs, at = refs[sum(counts) :], 0
+    for out, many in zip(outs, counts):
+        out[...] = sum(ref[...].astype(F32) for ref in refs[at : at + many]).astype(LOW)
+        at += many
+
+
+def own_kernel(counts, *refs):
+    own, send = refs[sum(counts) :]
+    at, col = 0, 0
+    for many in counts:
+        total = sum(ref[0].astype(F32) for ref in refs[at : at + many])
+        cols = slice(col, col + total.shape[-1])
+        own[:, cols] = total[0]
+        send[:, cols] = total[1].astype(LOW)
+        at, col = at + many, cols.stop
+
+
+def sum_call(kernel, chains, slots, index, outs, name):
+    terms = [term for chain in chains for term in chain]
+    specs = [
+        pl.BlockSpec((slots,) + term.shape[1:], lambda step: (index, 0, 0, 0)) for term in terms
+    ]
+    size = sum(2 * slots * term[0].size for term in terms) + sum(2 * out.size for out in outs)
+    return pl.pallas_call(
+        functools.partial(kernel, [len(chain) for chain in chains]),
+        out_shape=outs,
+        grid=(1,),
+        in_specs=specs,
+        out_specs=[pl.BlockSpec(out.shape, lambda step, n=len(out.shape): (0,) * n) for out in outs],
+        cost_estimate=pl.CostEstimate(flops=size, bytes_accessed=size, transcendentals=0),
+        name=name,
+    )(*terms)
 
 
 class GroupSum:
     def __init__(self, links, flat):
-        self.links = links
-        self.chains = [
-            ChainSum(links, order, flat[2 * chain], flat[2 * chain + 1])
-            for chain, order in enumerate(links.orders)
-        ]
-        self.crossed = None
+        self.links, self.crossed = links, None
+        self.bits = [list(order[::-1]) for order in links.orders]
+        self.chains = [[keep] for keep in flat[::2]]
+        self.pending = [links.swap(send, links.core) for send in flat[1::2]]
+        self.slots = flat[0].shape[0]
 
     def relay(self, value):
         if self.crossed is not None:
             return value
-        if self.chains[0].bits:
-            for chain in self.chains:
-                chain.prepare()
-            value, sends = lax.optimization_barrier((value, [chain.send for chain in self.chains]))
-            for chain, send in zip(self.chains, sends):
-                chain.send = send
-                chain.launch()
+        for chain, arrived in zip(self.chains, self.pending):
+            chain.append(arrived)
+        rows = self.chains[0][0].shape[2]
+        if self.slots > 1:
+            self.slots //= 2
+            near = self.slots
+            if rows % 8 == 0:
+                outs = [
+                    jax.ShapeDtypeStruct((near,) + chain[0].shape[1:], LOW) for chain in self.chains
+                ]
+                sends = sum_call(far_kernel, self.chains, near, 1, outs, "far_sum")
+            else:
+                sends = [
+                    sum(term[near : 2 * near].astype(F32) for term in chain).astype(LOW)
+                    for chain in self.chains
+                ]
+            value, sends = lax.optimization_barrier((value, sends))
+            self.pending = [
+                self.links.swap(send, bits.pop(0)) for send, bits in zip(sends, self.bits)
+            ]
             return value
-        summed = [chain.result() for chain in self.chains]
-        self.kept = jnp.concatenate([each[0] for each in summed], axis=1)
-        send = jnp.concatenate([each[1].astype(LOW) for each in summed], axis=1)
+        cols = sum(chain[0].shape[3] for chain in self.chains)
+        if rows % 8 == 0:
+            outs = [jax.ShapeDtypeStruct((rows, cols), kind) for kind in (F32, LOW)]
+            self.kept, send = sum_call(own_kernel, self.chains, 1, 0, outs, "own_sum")
+        else:
+            summed = [sum(term[0].astype(F32) for term in chain) for chain in self.chains]
+            self.kept = jnp.concatenate([each[0] for each in summed], axis=1)
+            send = jnp.concatenate([each[1].astype(LOW) for each in summed], axis=1)
         value, send = lax.optimization_barrier((value, send))
         self.crossed = self.links.swap(send, self.links.half)
         return value
@@ -594,20 +623,20 @@
     )
     kept_rows = jnp.where(on_images, patch_rows, token_rows)
     moved_rows = jnp.where(on_images, token_rows, patch_rows)
-    first, later = lax.optimization_barrier((first, collected[1][CHAINS]))
+    first, moved_rows = lax.optimization_barrier((first, moved_rows))
+    moved_rows = links.swap(moved_rows, half)
+    near = gather_near(links, gather_groups[0], collected[0][:CHAINS], first)
+    near, later = lax.optimization_barrier((near, collected[1][CHAINS]))
     later = links.swap(later, half)
-    pieces = gather_pieces(links, gather_groups[0], collected[0][:CHAINS], first)
+    pieces = gather_far(links, near)
     across = [got[1] for got, _ in pieces]
-    across, moved_rows, later = lax.optimization_barrier((across, moved_rows, later))
+    across, later = lax.optimization_barrier((across, later))
     for (got, _), far in zip(pieces, across):
         got[1] = far
-    moved_rows = links.swap(moved_rows, half)
     weights.update(place_pieces(links, gather_groups[0], pieces, row_shards))
-    pieces = gather_pieces(links, gather_groups[1], collected[1][:CHAINS], later)
-    weights.update(place_pieces(links, gather_groups[1], pieces, row_shards))
-
-    triple, merge, expand = weights["triple"], weights["merge"], weights["expand"]
-    pool_keyval, head_matrix, shrink = weights["keyval"], weights["head"], weights["shrink"]
+    near = gather_near(links, gather_groups[1], collected[1][:CHAINS], later)
+
+    triple, merge = weights["triple"], weights["merge"]
     per = LANES // row_shards
     line_rows = -(-7 // per)
     lines = weights["line"][:, :line_rows, : per * row_shards]
@@ -617,20 +646,28 @@
 
     shares = []
     for share in (kept_rows, moved_rows):
+        if shares:
+            share, _ = lax.optimization_barrier((share, shares[0][5]))
         share = share.astype(F32)
         hat_a, inverse_a = normalize_rows(share)
         normed_a = (hat_a * gain_a + shift_a).astype(LOW)
         triples = dot(normed_a, triple, 1, 0).astype(LOW)
+        if not shares:
+            triples, near = lax.optimization_barrier((triples, near))
+            pieces = gather_far(links, near)
         mixed = attend(side_word, triples, seq_len, text_len)
         shares.append((share, hat_a, inverse_a, normed_a, triples, mixed))
+    weights.update(place_pieces(links, gather_groups[1], pieces, row_shards))
+    expand, shrink = weights["expand"], weights["shrink"]
+    pool_keyval, head_matrix = weights["keyval"], weights["head"]
     inputs = jnp.concatenate([share[0] for share in shares], axis=0)
     mixed = jnp.concatenate([share[5] for share in shares], axis=0)
     middle = inputs + dot(mixed, merge, 1, 0)
     hat_b, inverse_b = normalize_rows(middle)
     normed_b = (hat_b * gain_b + shift_b).astype(LOW)
     upward = dot(normed_b, expand, 1, 0)
-    active, slope = gelu_tanh(upward).astype(LOW), gelu_slope(upward).astype(LOW)
-    active, slope = lax.optimization_barrier((active, slope))
+    active, slope = gelu_parts(upward)
+    active, slope = lax.optimization_barrier((active.astype(LOW), slope.astype(LOW)))
     hidden = middle + dot(active, shrink, 1, 0)
 
     total_rows = 2 * own_rows
@@ -766,13 +803,13 @@
     grad_middle = grad_hidden + normalize_back(grad_normed_b * gain_b, hat_b, inverse_b)
     grad_branch, grad_up = sums[0].relay((grad_middle.astype(LOW), grad_up))
     grad_expand = dot(normed_b, grad_up, 0, 0).astype(LOW)
+    grad_branch, grad_expand = sums[0].relay((grad_branch, grad_expand))
     grad_merge = dot(mixed, grad_branch, 0, 0).astype(LOW)
     grad_mixed = dot(grad_branch, merge, 1, 1).astype(LOW)
     grads = dict(merge=grad_merge, expand=grad_expand)
     packed = pack_group(links, scatter_groups[1], grads, row_shards)
     grad_mixed, packed = lax.optimization_barrier((grad_mixed, packed))
     sums.append(GroupSum(links, packed))
-    grad_mixed = sums[0].relay(grad_mixed)
 
     def inputs_back(index, grad_triples):
         _, hat_a, inverse_a, _, _, _ = shares[index]
@@ -795,8 +832,7 @@
     kept_gain, kept_shift, kept = inputs_back(0, kept_back)
     grad_gain_a, grad_shift_a = kept_gain + moved_gain, kept_shift + moved_shift
     grad_triple = dot(shares[1][3], moved_back, 0, 0) + dot(shares[0][3], kept_back, 0, 0)
-    grad_triple = sums[1].relay(grad_triple.astype(LOW))
-    grad_triple = sums[0].relay(grad_triple)
+    grad_triple = grad_triple.astype(LOW)
 
     grad_lines = jnp.stack(
         (grad_gain_a, grad_shift_a, grad_gain_b, grad_shift_b, grad_gain_c, grad_shift_c, grad_probe)
@@ -810,7 +846,14 @@
         ((0, 0), (0, row_shards - line_rows), (0, LANES - per * row_shards)),
     )
     grads = dict(triple=grad_triple, line=grad_lines)
-    sums.append(GroupSum(links, pack_group(links, scatter_groups[2], grads, row_shards)))
+    packed = pack_group(links, scatter_groups[2], grads, row_shards)
+    sums.append(GroupSum(links, packed))
+    first, second, third = sums
+    first.pending, second.pending = third.relay((first.pending, second.pending))
+    third.pending = first.relay(third.pending)
+    third.pending = second.relay(third.pending)
+    second.pending = third.relay(second.pending)
+    third.pending = second.relay(third.pending)
     visual_sums, textual_sums = {}, {}
     for group, partial in zip(scatter_groups, sums):
         own_sum, crossed = partial.finish()

time: 525 us -> 504 us (0.960)
  other arithmetic: 95.7 us -> 40.8 us
  Pallas kernels: 81.2 us -> 112 us
  waiting for transfers between devices: 95.8 us -> 89 us
  matrix products: 127 us -> 133 us
    convert_element_type x27 -> x0, other arithmetic: 34.6 us -> none  [prepare(): self.send = self.total(slice(near, 2 * near)).astype(LOW)]
    pallas_call x0 -> x12, Pallas kernels: none -> 31.4 us  [sum_call(): pl.pallas_call(functools.partial(kernel, [len(chain) for chain in chains]...]
    add x9 -> x0, other arithmetic: 7.41 us -> none  [total(): return sum((term[rows].astype(F32) for term in self.terms))]
    ppermute x78, waiting for transfers between devices: 95.8 us -> 89 us  [swap(): lax.ppermute(value, AXES, [(place, place ^ mask) for place in range(self....]
    dot_general x27, matrix products: 127 us -> 132 us  [dot(): lax.dot_general(left, right, (((left_dim,), (right_dim,)), ((), ())), pre...]
    concatenate x15 -> x12, other arithmetic: 11 us -> 7.58 us  [gather_near(): held = jnp.concatenate((held, links.swap(held, bit)), axis=0)]
    unnamed x302 -> x328, local copies, waits for them, and re-layouts: 16.1 us -> 18.5 us
  transfers between devices with their start and end apart: 78 -> 78, of which waited for: 26 -> 24; matrix products, arithmetic and copies ran while one was open for 29% -> 24% of each run, Pallas kernels for 12% -> 15%
where the time goes in v2:
time: 504 us; the launch traced here: 495 us
  matrix products  133 us (26%)
  Pallas kernels  112 us (22%)
  waiting for transfers between devices  89 us (18%)
  starting transfers between devices  69.5 us (14%)
  local copies, waits for them, and re-layouts  41.9 us (8%)
  other arithmetic  40.8 us (8%)
  between operations  8.23 us (2%)
    dot_general x27, matrix products, dot(): lax.dot_general(left, right, (((left_dim,), (right_dim,)), ((), ())), pre...  132 us
    ppermute x78, waiting for transfers between devices, swap(): lax.ppermute(value, AXES, [(place, place ^ mask) for place in range(self....  89 us
    ppermute x78, starting transfers between devices, swap(): lax.ppermute(value, AXES, [(place, place ^ mask) for place in range(self....  69.5 us
    pallas_call x6, Pallas kernels, block_call(): pl.pallas_call(kernel, out_shape=outs, grid_spec=pltpu.PrefetchScalarGrid...  36.7 us
    pallas_call x12, Pallas kernels, sum_call(): pl.pallas_call(functools.partial(kernel, [len(chain) for chain in chains]...  31.4 us
    pallas_call x2, Pallas kernels, attend_back(): pl.pallas_call(functools.partial(attend_back_kernel, group, width), out_s...  25 us
    pallas_call x2, Pallas kernels, attend(): pl.pallas_call(functools.partial(attend_kernel, group), out_shape=jax.Sha...  19.2 us
    unnamed x328, local copies, waits for them, and re-layouts  18.5 us
  transfers between devices with their start and end apart: 78, of which 24 were waited for; matrix products, arithmetic and copies ran while one was open for 24% of the time, Pallas kernels for 15%

profile of v2, /device:TPU:0, one launch (start us, length us, event | category | flops | bytes accessed | tf_op | source)
XLA Modules:
  0.0 494.6 jit_solution(1715465179286114490)
XLA Ops:
  5.2 4.1 collective-permute-start
  16.3 2.8 gather_fusion
  42.3 9.3 %collective-permute-done.8.refs_1_ = bf16[4,2,24,1024]{3,2,1,0:T(8,128)(2,1)S(1)} collective-permute-done((bf16[4,2,24,1024]{3,2,1,0:T(8,128)(2,1)S(1)}, bf16[4,2,24,1024]{3,2,1,0:T(8,128)(2,1)S(1)}, u32[]{:S(2)}, u32[]{:S(2)}) %collective-permute-start.8) | collective-permute-done | bytes 393248 | tf_op jit(solution)/shard_map/ppermute | solution.py:374
  52.2 5.7 %collective-permute-done.11 = bf16[24,8448]{1,0:T(8,128)(2,1)S(1)} collective-permute-done((bf16[24,8448]{1,0:T(8,128)(2,1)}, bf16[24,8448]{1,0:T(8,128)(2,1)S(1)}, u32[]{:S(2)}, u32[]{:S(2)}) %collective-permute-start.11) | collective-permute-done | bytes 405536 | tf_op jit(solution)/shard_map/ppermute | solution.py:374
  61.5 5.5 %collective-permute-done.22 = bf16[1,2,24,2816]{3,2,1,0:T(8,128)(2,1)S(1)} collective-permute-done((bf16[1,2,24,2816]{3,2,1,0:T(8,128)(2,1)S(1)}, bf16[1,2,24,2816]{3,2,1,0:T(8,128)(2,1)S(1)}, u32[]{:S(2)}, u32[]{:S(2)}) %collective-permute-start.22) | collective-permute-done | bytes 270368 | tf_op jit(solution)/shard_map/ppermute | solution.py:374
  68.9 4.6 collective-permute-done.20
  77.7 5.5 %spread.2 = (bf16[32,24,2304]{2,1,0:T(8,128)(2,1)}, bf16[32,24,768]{2,1,0:T(8,128)(2,1)}, bf16[32,24,128]{2,1,0:T(8,128)(2,1)}) custom-call(s32[96]{0:T(128)} %reshape.1841.table_ref, bf16[4,2,24,1024]{3,2,1,0:T(8,128)(2,1)} %copy-done.36, bf16[4,2,24,1024]{3,2,1,0:T(8,128)(2,1)} %copy-done.53, bf16[4,2,24,1024]{3,2,1,0:T(8,128)(2,1)} %copy-done.57, ...), custom_call_target="tpu_custom_call" | custom-call | bytes 9830400 | tf_op jit(solution)/shard_map/spread/pallas_call | solution.py:230
  84.6 5.6 %convolution_convert_fusion.3.q_ref.k_ref.v_ref = bf16[512,2304]{1,0:T(8,128)(2,1)} fusion(bf16[768,2304]{1,0:T(8,128)(2,1)} %bitcast.269, bf16[512,768]{1,0:T(8,128)(2,1)S(1)} %get-tuple-element.488, f32[768]{0:T(1024)S(1)} %get-tuple-element.479, f32[768]{0:T(1024)S(1)} %get-tuple-element.480, f32[512]{0:T(512)S(1)} %add_rsqrt_fusion.3, ...), kind=kOutput, calls=%fused_computation.11 | convolution fusion | flops 1815478272 | bytes 6694912 | tf_op jit(solution)/shard_map/dot_general | solution.py:34
  91.5 12.8 %collective-permute-done.21 = bf16[2,2,24,2816]{3,2,1,0:T(8,128)(2,1)} collective-permute-done((bf16[2,2,24,2816]{3,2,1,0:T(8,128)(2,1)}, bf16[2,2,24,2816]{3,2,1,0:T(8,128)(2,1)}, u32[]{:S(2)}, u32[]{:S(2)}) %collective-permute-start.21) | collective-permute-done | bytes 540704 | tf_op jit(solution)/shard_map/ppermute | solution.py:374
  111.8 9.7 %attend.2 = bf16[512,768]{1,0:T(8,128)(2,1)} custom-call(s32[1]{0:T(128)} %bitcast.2.side_ref, bf16[512,2304]{1,0:T(8,128)(2,1)} %convolution_convert_fusion.3.q_ref.k_ref.v_ref, bf16[512,2304]{1,0:T(8,128)(2,1)} %convolution_convert_fusion.3.q_ref.k_ref.v_ref, bf16[512,2304]{1,0:T(8,128)(2,1)} %convolution_convert_fusion.3.q_ref.k_ref.v_ref), custom_call_target="tpu_custom_call" | custom-call | flops 402653184 | bytes 3145728 | tf_op jit(solution)/shard_map/attend/pallas_call | solution.py:138
  124.4 3.7 convolution_convert_fusion.2.q_ref.k_ref.v_ref
  128.1 9.5 %attend.3 = bf16[512,768]{1,0:T(8,128)(2,1)} custom-call(s32[1]{0:T(128)} %bitcast.2.side_ref, bf16[512,2304]{1,0:T(8,128)(2,1)} %convolution_convert_fusion.2.q_ref.k_ref.v_ref, bf16[512,2304]{1,0:T(8,128)(2,1)} %convolution_convert_fusion.2.q_ref.k_ref.v_ref, bf16[512,2304]{1,0:T(8,128)(2,1)} %convolution_convert_fusion.2.q_ref.k_ref.v_ref), custom_call_target="tpu_custom_call" | custom-call | flops 402653184 | bytes 3145728 | tf_op jit(solution)/shard_map/attend/pallas_call | solution.py:138
  138.2 9.7 %collective-permute-done.30.refs_9_ = bf16[4,2,24,2816]{3,2,1,0:T(8,128)(2,1)} collective-permute-done((bf16[4,2,24,2816]{3,2,1,0:T(8,128)(2,1)}, bf16[4,2,24,2816]{3,2,1,0:T(8,128)(2,1)}, u32[]{:S(2)}, u32[]{:S(2)}) %collective-permute-start.30) | collective-permute-done | bytes 1081376 | tf_op jit(solution)/shard_map/ppermute | solution.py:374
  147.9 4.2 fusion.123
  152.7 10.4 %spread.3 = (bf16[32,24,3072]{2,1,0:T(8,128)(2,1)}, bf16[32,24,1536]{2,1,0:T(8,128)(2,1)}, bf16[32,24,768]{2,1,0:T(8,128)(2,1)}, bf16[32,4,24,768]{3,2,1,0:T(8,128)(2,1)}) custom-call(s32[96]{0:T(128)} %reshape.1841.table_ref, bf16[4,2,24,2816]{3,2,1,0:T(8,128)(2,1)} %copy-done.26, bf16[4,2,24,2816]{3,2,1,0:T(8,128)(2,1)} %collective-permute-done.24.refs_1_, ...), custom_call_target="tpu_custom_call" | custom-call | bytes 25952256 | tf_op jit(solution)/shard_map/spread/pallas_call | solution.py:230
  163.2 15.4 %add_convert_fusion = (bf16[1024,3072]{1,0:T(8,128)(2,1)}, bf16[1024,3072]{1,0:T(8,128)(2,1)S(1)}) fusion(bf16[768,3072]{1,0:T(8,128)(2,1)} %bitcast.263, f32[1024,768]{1,0:T(8,128)S(1)} %get-tuple-element.540, f32[768]{0:T(1024)S(1)} %get-tuple-element.477, f32[768]{0:T(1024)S(1)} %get-tuple-element.478, f32[1024]{0:T(1024)S(1)} %add_rsqrt_fusion.1, ...), kind=kOutput, calls=%fused_computation.3 | convolution fusion | flops 4882956288 | bytes 20461568 | tf_op jit(solution)/shard_map/dot_general | solution.py:34
  178.6 9.4 %fusion.124 = (f32[1024]{0:T(1024)S(1)}, f32[1024,768]{1,0:T(8,128)S(1)}) fusion(f32[1024,768]{1,0:T(8,128)} %copy-done.7, bf16[1024,3072]{1,0:T(8,128)(2,1)S(1)} %get-tuple-element.208, bf16[3072,768]{1,0:T(8,128)(2,1)S(1)} %bitcast.265), kind=kOutput, calls=%fused_computation.340 | convolution fusion | flops 4833410048 | bytes 17305600 | tf_op jit(solution)/shard_map/dot_general | solution.py:34
  190.4 2.8 convolution_convert_fusion.4
  199.3 4.9 collective-permute-done.33
  214.2 5.0 %collective-permute-done.36 = bf16[4,24,768]{2,1,0:T(8,128)(2,1)S(1)} collective-permute-done((bf16[4,24,768]{2,1,0:T(8,128)(2,1)S(1)}, bf16[4,24,768]{2,1,0:T(8,128)(2,1)S(1)}, u32[]{:S(2)}, u32[]{:S(2)}) %collective-permute-start.36) | collective-permute-done | bytes 147488 | tf_op jit(solution)/shard_map/ppermute | solution.py:374
  231.7 4.3 convolution_convert_fusion.5
  237.7 4.0 multiply_reduce_fusion
  242.8 11.6 %convolution_convert_fusion.1 = bf16[3072,768]{1,0:T(8,128)(2,1)} fusion(bf16[1024,3072]{1,0:T(8,128)(2,1)} %copy-done.156, f32[1024,768]{1,0:T(8,128)S(1)} %subtract_multiply_fusion), kind=kOutput, calls=%fused_computation.9 | convolution fusion | flops 4834983936 | bytes 14155776 | tf_op jit(solution)/shard_map/dot_general | solution.py:34
  254.4 7.1 %multiply_convert_fusion = bf16[1024,3072]{1,0:T(8,128)(2,1)} fusion(bf16[1024,3072]{1,0:T(8,128)(2,1)S(1)} %bitcast.278, bf16[3072,768]{1,0:T(8,128)(2,1)S(1)} %bitcast.268, f32[1024,768]{1,0:T(8,128)S(1)} %subtract_multiply_fusion), kind=kOutput, calls=%fused_computation.2 | convolution fusion | flops 4842061824 | bytes 20447232 | tf_op jit(solution)/shard_map/dot_general | solution.py:34
  261.5 7.7 %pack.3 = (bf16[8,2,24,1792]{3,2,1,0:T(8,128)(2,1)}, bf16[8,2,24,1792]{3,2,1,0:T(8,128)(2,1)}, bf16[8,2,24,1792]{3,2,1,0:T(8,128)(2,1)}, bf16[8,2,24,1792]{3,2,1...) custom-call(s32[96]{0:T(128)} %reshape.1861.table_ref, ...), custom_call_target="tpu_custom_call" | custom-call | bytes 16515072 | tf_op jit(solution)/shard_map/pack/pallas_call | solution.py:230
  270.3 10.8 %multiply_reduce_fusion.1 = (bf16[768]{0:T(1024)(128)(2,1)}, f32[1024]{0:T(1024)S(1)}, f32[1024]{0:T(1024)S(1)}, bf16[768]{0:T(1024)(128)(2,1)}, f32[1024,768]{1,0:T(8,128)S(1)}) fusion(f32[1024,768]{1,0:T(8,128)} %copy-done.7, f32[1024]{0:T(1024)S(1)} %copy-done.99, f32[1024]{0:T(1024)S(1)} %copy-done.87, f32[768]{0:T(1024)S(1)} %copy-done.97, ...), kind=kOutput, calls=%fused_computation.21 | convolution fusion | flops 4838912000 | bytes 17324032 | tf_op jit(solution)/shard_map/dot_general | solution.py:34
  281.1 3.0 fusion.120
  285.7 3.6 far_sum.9
  291.1 10.4 %convolution_convert_fusion = bf16[768,3072]{1,0:T(8,128)(2,1)} fusion(bf16[1024,3072]{1,0:T(8,128)(2,1)} %multiply_convert_fusion, f32[1024,768]{1,0:T(8,128)} %copy-done.7, f32[768]{0:T(1024)S(1)} %copy-done.125, f32[768]{0:T(1024)S(1)} %copy-done.97, f32[1024]{0:T(1024)S(1)} %copy-done.99, f32[1024]{0:T(1024)S(1)} %copy-done.87), kind=kOutput, calls=%fused_computation.8 | convolution fusion | flops 4838129664 | bytes 14170112 | tf_op jit(solution)/shard_map/dot_general | solution.py:34
  301.6 5.2 %collective-permute-done.41.refs_2_ = bf16[4,2,24,1792]{3,2,1,0:T(8,128)(2,1)S(1)} collective-permute-done((bf16[4,2,24,1792]{3,2,1,0:T(8,128)(2,1)}, bf16[4,2,24,1792]{3,2,1,0:T(8,128)(2,1)S(1)}, u32[]{:S(2)}, u32[]{:S(2)}) %collective-permute-start.41) | collective-permute-done | bytes 688160 | tf_op jit(solution)/shard_map/ppermute | solution.py:374
  308.9 2.9 far_sum.10
  311.8 4.3 convolution_convert_fusion.7
  316.1 2.6 convolution_convert_fusion.6.grad_ref
  318.6 6.1 %pack.4 = (bf16[8,2,24,1280]{3,2,1,0:T(8,128)(2,1)}, bf16[8,2,24,1280]{3,2,1,0:T(8,128)(2,1)}, bf16[8,2,24,1280]{3,2,1,0:T(8,128)(2,1)}, bf16[8,2,24,1280]{3,2,1...) custom-call(s32[96]{0:T(128)} %reshape.1861.table_ref, ...), custom_call_target="tpu_custom_call" | custom-call | bytes 11796480 | tf_op jit(solution)/shard_map/pack/pallas_call | solution.py:230
  331.5 4.5 collective-permute-done.44.refs_3_
  341.0 12.6 %attend_back.2 = bf16[512,2304]{1,0:T(8,128)(2,1)} custom-call(s32[1]{0:T(128)} %bitcast.2.side_ref, bf16[512,2304]{1,0:T(8,128)(2,1)} %convolution_convert_fusion.2.q_ref.k_ref.v_ref, bf16[512,2304]{1,0:T(8,128)(2,1)} %convolution_convert_fusion.2.q_ref.k_ref.v_ref, bf16[512,2304]{1,0:T(8,128)(2,1)} %convolution_convert_fusion.2.q_ref.k_ref.v_ref, ...), custom_call_target="tpu_custom_call" | custom-call | flops 1006632960 | bytes 5505024 | tf_op jit(solution)/shard_map/attend_back/pallas_call | solution.py:160
  358.6 3.0 far_sum.12
  364.3 5.2 %multiply_reduce_fusion.8 = (f32[768]{0:T(1024)S(1)}, f32[512]{0:T(512)S(1)}, f32[512]{0:T(512)S(1)}, f32[768]{0:T(1024)S(1)}, f32[512,768]{1,0:T(8,128)S(1)}) fusion(bf16[512,768]{1,0:T(8,128)(2,1)} %copy-done.13, f32[512]{0:T(512)S(1)} %copy-done.113, f32[512]{0:T(512)S(1)} %copy-done.95, f32[768]{0:T(1024)S(1)} %copy-done.91, ...), kind=kOutput, calls=%fused_computation.43 | convolution fusion | flops 1815868928 | bytes 8274944 | tf_op jit(solution)/shard_map/dot_general | solution.py:34
  371.0 12.4 %attend_back.3 = bf16[512,2304]{1,0:T(8,128)(2,1)} custom-call(s32[1]{0:T(128)} %bitcast.2.side_ref, bf16[512,2304]{1,0:T(8,128)(2,1)} %convolution_convert_fusion.3.q_ref.k_ref.v_ref, bf16[512,2304]{1,0:T(8,128)(2,1)} %convolution_convert_fusion.3.q_ref.k_ref.v_ref, bf16[512,2304]{1,0:T(8,128)(2,1)} %convolution_convert_fusion.3.q_ref.k_ref.v_ref, ...), custom_call_target="tpu_custom_call" | custom-call | flops 1006632960 | bytes 5505024 | tf_op jit(solution)/shard_map/attend_back/pallas_call | solution.py:160
  384.3 6.9 %fusion.117 = f32[768,2304]{1,0:T(8,128)} fusion(bf16[512,2304]{1,0:T(8,128)(2,1)} %attend_back.2, bf16[512,768]{1,0:T(8,128)(2,1)S(1)} %copy-done.14, f32[512]{0:T(512)S(1)} %copy-done.113, f32[512]{0:T(512)S(1)} %copy-done.95, f32[768]{0:T(1024)S(1)} %copy-done.123, f32[768]{0:T(1024)S(1)} %copy-done.91), kind=kOutput, calls=%fused_computation.333 | convolution fusion | flops 1814298624 | bytes 10233856 | tf_op jit(solution)/shard_map/dot_general | solution.py:34
  392.9 2.7 far_sum.13
  395.6 6.8 %multiply_reduce_fusion.9 = (f32[768]{0:T(1024)S(1)}, f32[512]{0:T(512)}, f32[512]{0:T(512)}, f32[768]{0:T(1024)S(1)}, f32[512,768]{1,0:T(8,128)}) fusion(bf16[512,768]{1,0:T(8,128)(2,1)S(1)} %copy-done.6, f32[512]{0:T(512)S(1)} %copy-done.110, f32[512]{0:T(512)S(1)} %copy-done.93, f32[768]{0:T(1024)S(1)} %copy-done.91, bf16[512,2304]{1,0:T(8,128)(2,1)} %attend_back.3, ...), kind=kOutput, calls=%fused_computation.44 | convolution fusion | flops 1815868928 | bytes 8274944 | tf_op jit(solution)/shard_map/dot_general | solution.py:34
  402.5 4.3 add_convert_fusion.1
  408.0 4.8 pack.5
  440.3 3.9 broadcast_select_fusion
  446.4 3.0 own_sum.3
  467.4 2.9 collective-permute-start.76
  486.9 3.2 collective-permute-done.75
  (658 shorter events, 186.2 us)
Async XLA Ops:
  5.2 18.5 %collective-permute-start = (bf16[24,3200]{1,0:T(8,128)(2,1)}, bf16[24,3200]{1,0:T(8,128)(2,1)S(1)}, u32[]{:S(2)}, u32[]{:S(2)}) collective-permute-start(bf16[24,3200]{1,0:T(8,128)(2,1)} %get-tuple-element.181), channel_id=1, source_target_pairs={{0,16},{1,17},{2,18},{3,19},{4,20},{5,21},{6,22},{7,23},{8,24},{9,... | collective-permute-start | bytes 460808 | tf_op jit(solution)/shard_map/ppermute | solution.py:374
  38.4 13.2 %collective-permute-start.8 = (bf16[4,2,24,1024]{3,2,1,0:T(8,128)(2,1)S(1)}, bf16[4,2,24,1024]{3,2,1,0:T(8,128)(2,1)S(1)}, u32[]{:S(2)}, u32[]{:S(2)}) collective-permute-start(bf16[4,2,24,1024]{3,2,1,0:T(8,128)(2,1)S(1)} %pad_maximum_fusion.15.refs_0_), channel_id=1, source_target_pairs={{0,8},{1,9},{2,10},{3,11},{4,12},{5,13},{6,14},{7,15},{8,0},{9,1},... | collective-permute-start | bytes 1179656 | tf_op jit(solution)/shard_map/ppermute | solution.py:374
  40.5 11.2 %collective-permute-start.9 = (bf16[4,2,24,1024]{3,2,1,0:T(8,128)(2,1)S(1)}, bf16[4,2,24,1024]{3,2,1,0:T(8,128)(2,1)S(1)}, u32[]{:S(2)}, u32[]{:S(2)}) collective-permute-start(bf16[4,2,24,1024]{3,2,1,0:T(8,128)(2,1)S(1)} %pad_maximum_fusion.16.refs_4_), channel_id=1, source_target_pairs={{0,1},{1,0},{2,3},{3,2},{4,5},{5,4},{6,7},{7,6},{8,9},{9,8},{10,11... | collective-permute-start | bytes 1179656 | tf_op jit(solution)/shard_map/ppermute | solution.py:374
  40.5 17.3 %collective-permute-start.11 = (bf16[24,8448]{1,0:T(8,128)(2,1)}, bf16[24,8448]{1,0:T(8,128)(2,1)S(1)}, u32[]{:S(2)}, u32[]{:S(2)}) collective-permute-start(bf16[24,8448]{1,0:T(8,128)(2,1)} %get-tuple-element.191), channel_id=1, source_target_pairs={{0,16},{1,17},{2,18},{3,19},{4,20},{5,21},{6,22},{7,23},{8,24},{9,... | collective-permute-start | bytes 1216520 | tf_op jit(solution)/shard_map/ppermute | solution.py:374
  40.9 17.0 %collective-permute-start.10 = (bf16[4,2,24,1152]{3,2,1,0:T(8,128)(2,1)S(1)}, bf16[4,2,24,1152]{3,2,1,0:T(8,128)(2,1)}, u32[]{:S(2)}, u32[]{:S(2)}) collective-permute-start(bf16[4,2,24,1152]{3,2,1,0:T(8,128)(2,1)S(1)} %pad_maximum_fusion.14.refs_8_), channel_id=1, source_target_pairs={{0,4},{1,5},{2,6},{3,7},{4,0},{5,1},{6,2},{7,3},{8,12},{9,13},{10,... | collective-permute-start | bytes 1327112 | tf_op jit(solution)/shard_map/ppermute | solution.py:374
  42.3 25.9 %collective-permute-start.12 = (bf16[4,2,24,1024]{3,2,1,0:T(8,128)(2,1)S(1)}, bf16[4,2,24,1024]{3,2,1,0:T(8,128)(2,1)S(1)}, u32[]{:S(2)}, u32[]{:S(2)}) collective-permute-start(bf16[4,2,24,1024]{3,2,1,0:T(8,128)(2,1)S(1)} %pad_maximum_fusion.15.refs_0_), channel_id=1, source_target_pairs={{0,2},{1,3},{2,0},{3,1},{4,6},{5,7},{6,4},{7,5},{8,10},{9,11},{10,... | collective-permute-start | bytes 1179656 | tf_op jit(solution)/shard_map/ppermute | solution.py:374
  51.7 22.8 %collective-permute-start.14 = (bf16[4,2,24,1024]{3,2,1,0:T(8,128)(2,1)S(1)}, bf16[4,2,24,1024]{3,2,1,0:T(8,128)(2,1)S(1)}, u32[]{:S(2)}, u32[]{:S(2)}) collective-permute-start(bf16[4,2,24,1024]{3,2,1,0:T(8,128)(2,1)S(1)} %pad_maximum_fusion.16.refs_4_), channel_id=1, source_target_pairs={{0,2},{1,3},{2,0},{3,1},{4,6},{5,7},{6,4},{7,5},{8,10},{9,11},{10,... | collective-permute-start | bytes 1179656 | tf_op jit(solution)/shard_map/ppermute | solution.py:374
  51.7 22.9 %collective-permute-start.16 = (bf16[4,2,24,1152]{3,2,1,0:T(8,128)(2,1)S(1)}, bf16[4,2,24,1152]{3,2,1,0:T(8,128)(2,1)S(1)}, u32[]{:S(2)}, u32[]{:S(2)}) collective-permute-start(bf16[4,2,24,1152]{3,2,1,0:T(8,128)(2,1)S(1)} %pad_maximum_fusion.14.refs_8_), channel_id=1, source_target_pairs={{0,2},{1,3},{2,0},{3,1},{4,6},{5,7},{6,4},{7,5},{8,10},{9,11},{10,... | collective-permute-start | bytes 1327112 | tf_op jit(solution)/shard_map/ppermute | solution.py:374
  74.5 47.1 %collective-permute-start.1 = (bf16[512,768]{1,0:T(8,128)(2,1)}, bf16[512,768]{1,0:T(8,128)(2,1)S(1)}, u32[]{:S(2)}, u32[]{:S(2)}) collective-permute-start(bf16[512,768]{1,0:T(8,128)(2,1)} %get-tuple-element.182), channel_id=1, source_target_pairs={{0,16},{1,17},{2,18},{3,19},{4,20},{5,21},{6,22},{7,23},{8,24},{9,... | collective-permute-start | bytes 2359304 | tf_op jit(solution)/shard_map/ppermute | solution.py:374
  74.6 15.6 %collective-permute-start.19 = (bf16[2,2,24,2816]{3,2,1,0:T(8,128)(2,1)S(1)}, bf16[2,2,24,2816]{3,2,1,0:T(8,128)(2,1)}, u32[]{:S(2)}, u32[]{:S(2)}) collective-permute-start(bf16[2,2,24,2816]{3,2,1,0:T(8,128)(2,1)S(1)} %pad_maximum_fusion.11), channel_id=1, source_target_pairs={{0,4},{1,5},{2,6},{3,7},{4,0},{5,1},{6,2},{7,3},{8,12},{9,13},{10,... | collective-permute-start | bytes 1622024 | tf_op jit(solution)/shard_map/ppermute | solution.py:374
  75.4 28.8 %collective-permute-start.21 = (bf16[2,2,24,2816]{3,2,1,0:T(8,128)(2,1)}, bf16[2,2,24,2816]{3,2,1,0:T(8,128)(2,1)}, u32[]{:S(2)}, u32[]{:S(2)}) collective-permute-start(bf16[2,2,24,2816]{3,2,1,0:T(8,128)(2,1)} %pad_maximum_fusion.12), channel_id=1, source_target_pairs={{0,8},{1,9},{2,10},{3,11},{4,12},{5,13},{6,14},{7,15},{8,0},{9,1},... | collective-permute-start | bytes 1622024 | tf_op jit(solution)/shard_map/ppermute | solution.py:374
  77.0 29.5 %collective-permute-start.23 = (bf16[2,2,24,2816]{3,2,1,0:T(8,128)(2,1)}, bf16[2,2,24,2816]{3,2,1,0:T(8,128)(2,1)}, u32[]{:S(2)}, u32[]{:S(2)}) collective-permute-start(bf16[2,2,24,2816]{3,2,1,0:T(8,128)(2,1)} %pad_maximum_fusion.13), channel_id=1, source_target_pairs={{0,1},{1,0},{2,3},{3,2},{4,5},{5,4},{6,7},{7,6},{8,9},{9,8},{10,11... | collective-permute-start | bytes 1622024 | tf_op jit(solution)/shard_map/ppermute | solution.py:374
  108.6 29.0 %collective-permute-start.25 = (bf16[4,2,24,2816]{3,2,1,0:T(8,128)(2,1)S(1)}, bf16[4,2,24,2816]{3,2,1,0:T(8,128)(2,1)}, u32[]{:S(2)}, u32[]{:S(2)}) collective-permute-start(bf16[4,2,24,2816]{3,2,1,0:T(8,128)(2,1)S(1)} %pad_maximum_fusion.6.refs_0_), channel_id=1, source_target_pairs={{0,2},{1,3},{2,0},{3,1},{4,6},{5,7},{6,4},{7,5},{8,10},{9,11},{10,... | collective-permute-start | bytes 3244040 | tf_op jit(solution)/shard_map/ppermute | solution.py:374
  108.6 29.0 %collective-permute-start.24 = (bf16[4,2,24,2816]{3,2,1,0:T(8,128)(2,1)S(1)}, bf16[4,2,24,2816]{3,2,1,0:T(8,128)(2,1)}, u32[]{:S(2)}, u32[]{:S(2)}) collective-permute-start(bf16[4,2,24,2816]{3,2,1,0:T(8,128)(2,1)S(1)} %pad_maximum_fusion.6.refs_0_), channel_id=1, source_target_pairs={{0,8},{1,9},{2,10},{3,11},{4,12},{5,13},{6,14},{7,15},{8,0},{9,1},... | collective-permute-start | bytes 3244040 | tf_op jit(solution)/shard_map/ppermute | solution.py:374
  111.1 41.6 %collective-permute-start.28 = (bf16[4,2,24,2816]{3,2,1,0:T(8,128)(2,1)}, bf16[4,2,24,2816]{3,2,1,0:T(8,128)(2,1)}, u32[]{:S(2)}, u32[]{:S(2)}) collective-permute-start(bf16[4,2,24,2816]{3,2,1,0:T(8,128)(2,1)} %pad_maximum_fusion.7.refs_4_), channel_id=1, source_target_pairs={{0,2},{1,3},{2,0},{3,1},{4,6},{5,7},{6,4},{7,5},{8,10},{9,11},{10,... | collective-permute-start | bytes 3244040 | tf_op jit(solution)/shard_map/ppermute | solution.py:374
  111.3 26.8 %collective-permute-start.27 = (bf16[4,2,24,2816]{3,2,1,0:T(8,128)(2,1)}, bf16[4,2,24,2816]{3,2,1,0:T(8,128)(2,1)}, u32[]{:S(2)}, u32[]{:S(2)}) collective-permute-start(bf16[4,2,24,2816]{3,2,1,0:T(8,128)(2,1)} %pad_maximum_fusion.7.refs_4_), channel_id=1, source_target_pairs={{0,1},{1,0},{2,3},{3,2},{4,5},{5,4},{6,7},{7,6},{8,9},{9,8},{10,11... | collective-permute-start | bytes 3244040 | tf_op jit(solution)/shard_map/ppermute | solution.py:374
  121.8 26.2 %collective-permute-start.30 = (bf16[4,2,24,2816]{3,2,1,0:T(8,128)(2,1)}, bf16[4,2,24,2816]{3,2,1,0:T(8,128)(2,1)}, u32[]{:S(2)}, u32[]{:S(2)}) collective-permute-start(bf16[4,2,24,2816]{3,2,1,0:T(8,128)(2,1)} %pad_maximum_fusion.8.refs_8_), channel_id=1, source_target_pairs={{0,4},{1,5},{2,6},{3,7},{4,0},{5,1},{6,2},{7,3},{8,12},{9,13},{10,... | collective-permute-start | bytes 3244040 | tf_op jit(solution)/shard_map/ppermute | solution.py:374
  137.6 15.0 %collective-permute-start.31 = (bf16[4,2,24,2816]{3,2,1,0:T(8,128)(2,1)}, bf16[4,2,24,2816]{3,2,1,0:T(8,128)(2,1)}, u32[]{:S(2)}, u32[]{:S(2)}) collective-permute-start(bf16[4,2,24,2816]{3,2,1,0:T(8,128)(2,1)} %pad_maximum_fusion.8.refs_8_), channel_id=1, source_target_pairs={{0,2},{1,3},{2,0},{3,1},{4,6},{5,7},{6,4},{7,5},{8,10},{9,11},{10,... | collective-permute-start | bytes 3244040 | tf_op jit(solution)/shard_map/ppermute | solution.py:374
  137.6 15.0 %collective-permute-start.26 = (bf16[4,2,24,2816]{3,2,1,0:T(8,128)(2,1)}, bf16[4,2,24,2816]{3,2,1,0:T(8,128)(2,1)}, u32[]{:S(2)}, u32[]{:S(2)}) collective-permute-start(bf16[4,2,24,2816]{3,2,1,0:T(8,128)(2,1)} %collective-permute-done.24.refs_1_), channel_id=1, source_target_pairs={{0,2},{1,3},{2,0},{3,1},{4,6},{5,7},{6,4},{7,5},{8,10},{9,11},{10,... | collective-permute-start | bytes 3244040 | tf_op jit(solution)/shard_map/ppermute | solution.py:374
  138.2 14.6 %collective-permute-start.29 = (bf16[4,2,24,2816]{3,2,1,0:T(8,128)(2,1)}, bf16[4,2,24,2816]{3,2,1,0:T(8,128)(2,1)}, u32[]{:S(2)}, u32[]{:S(2)}) collective-permute-start(bf16[4,2,24,2816]{3,2,1,0:T(8,128)(2,1)} %collective-permute-done.27.refs_5_), channel_id=1, source_target_pairs={{0,2},{1,3},{2,0},{3,1},{4,6},{5,7},{6,4},{7,5},{8,10},{9,11},{10,... | collective-permute-start | bytes 3244040 | tf_op jit(solution)/shard_map/ppermute | solution.py:374
  269.2 14.9 %collective-permute-start.38 = (bf16[8,2,24,1792]{3,2,1,0:T(8,128)(2,1)}, bf16[8,2,24,1792]{3,2,1,0:T(8,128)(2,1)S(1)}, u32[]{:S(2)}, u32[]{:S(2)}) collective-permute-start(bf16[8,2,24,1792]{3,2,1,0:T(8,128)(2,1)} %get-tuple-element.221), channel_id=1, source_target_pairs={{0,2},{1,3},{2,0},{3,1},{4,6},{5,7},{6,4},{7,5},{8,10},{9,11},{10,... | collective-permute-start | bytes 4128776 | tf_op jit(solution)/shard_map/ppermute | solution.py:374
  269.8 14.4 %collective-permute-start.39 = (bf16[8,2,24,1792]{3,2,1,0:T(8,128)(2,1)}, bf16[8,2,24,1792]{3,2,1,0:T(8,128)(2,1)S(1)}, u32[]{:S(2)}, u32[]{:S(2)}) collective-permute-start(bf16[8,2,24,1792]{3,2,1,0:T(8,128)(2,1)} %get-tuple-element.223), channel_id=1, source_target_pairs={{0,2},{1,3},{2,0},{3,1},{4,6},{5,7},{6,4},{7,5},{8,10},{9,11},{10,... | collective-permute-start | bytes 4128776 | tf_op jit(solution)/shard_map/ppermute | solution.py:374
  269.9 14.3 %collective-permute-start.40 = (bf16[8,2,24,1792]{3,2,1,0:T(8,128)(2,1)}, bf16[8,2,24,1792]{3,2,1,0:T(8,128)(2,1)}, u32[]{:S(2)}, u32[]{:S(2)}) collective-permute-start(bf16[8,2,24,1792]{3,2,1,0:T(8,128)(2,1)} %get-tuple-element.225), channel_id=1, source_target_pairs={{0,2},{1,3},{2,0},{3,1},{4,6},{5,7},{6,4},{7,5},{8,10},{9,11},{10,... | collective-permute-start | bytes 4128776 | tf_op jit(solution)/shard_map/ppermute | solution.py:374
  289.3 17.4 %collective-permute-start.41 = (bf16[4,2,24,1792]{3,2,1,0:T(8,128)(2,1)}, bf16[4,2,24,1792]{3,2,1,0:T(8,128)(2,1)S(1)}, u32[]{:S(2)}, u32[]{:S(2)}) collective-permute-start(bf16[4,2,24,1792]{3,2,1,0:T(8,128)(2,1)} %get-tuple-element.231), channel_id=1, source_target_pairs={{0,8},{1,9},{2,10},{3,11},{4,12},{5,13},{6,14},{7,15},{8,0},{9,1},... | collective-permute-start | bytes 2064392 | tf_op jit(solution)/shard_map/ppermute | solution.py:374
  289.3 17.4 %collective-permute-start.42 = (bf16[4,2,24,1792]{3,2,1,0:T(8,128)(2,1)}, bf16[4,2,24,1792]{3,2,1,0:T(8,128)(2,1)S(1)}, u32[]{:S(2)}, u32[]{:S(2)}) collective-permute-start(bf16[4,2,24,1792]{3,2,1,0:T(8,128)(2,1)} %get-tuple-element.232), channel_id=1, source_target_pairs={{0,1},{1,0},{2,3},{3,2},{4,5},{5,4},{6,7},{7,6},{8,9},{9,8},{10,11... | collective-permute-start | bytes 2064392 | tf_op jit(solution)/shard_map/ppermute | solution.py:374
  290.8 17.2 %collective-permute-start.43 = (bf16[4,2,24,1792]{3,2,1,0:T(8,128)(2,1)}, bf16[4,2,24,1792]{3,2,1,0:T(8,128)(2,1)S(1)}, u32[]{:S(2)}, u32[]{:S(2)}) collective-permute-start(bf16[4,2,24,1792]{3,2,1,0:T(8,128)(2,1)} %get-tuple-element.233), channel_id=1, source_target_pairs={{0,4},{1,5},{2,6},{3,7},{4,0},{5,1},{6,2},{7,3},{8,12},{9,13},{10,... | collective-permute-start | bytes 2064392 | tf_op jit(solution)/shard_map/ppermute | solution.py:374
  324.7 31.5 %collective-permute-start.47 = (bf16[8,2,24,1280]{3,2,1,0:T(8,128)(2,1)}, bf16[8,2,24,1280]{3,2,1,0:T(8,128)(2,1)S(1)}, u32[]{:S(2)}, u32[]{:S(2)}) collective-permute-start(bf16[8,2,24,1280]{3,2,1,0:T(8,128)(2,1)} %get-tuple-element.254), channel_id=1, source_target_pairs={{0,2},{1,3},{2,0},{3,1},{4,6},{5,7},{6,4},{7,5},{8,10},{9,11},{10,... | collective-permute-start | bytes 2949128 | tf_op jit(solution)/shard_map/ppermute | solution.py:374
  324.8 31.4 %collective-permute-start.48 = (bf16[8,2,24,1280]{3,2,1,0:T(8,128)(2,1)}, bf16[8,2,24,1280]{3,2,1,0:T(8,128)(2,1)S(1)}, u32[]{:S(2)}, u32[]{:S(2)}) collective-permute-start(bf16[8,2,24,1280]{3,2,1,0:T(8,128)(2,1)} %get-tuple-element.256), channel_id=1, source_target_pairs={{0,2},{1,3},{2,0},{3,1},{4,6},{5,7},{6,4},{7,5},{8,10},{9,11},{10,... | collective-permute-start | bytes 2949128 | tf_op jit(solution)/shard_map/ppermute | solution.py:374
  325.3 31.0 %collective-permute-start.49 = (bf16[8,2,24,1280]{3,2,1,0:T(8,128)(2,1)}, bf16[8,2,24,1280]{3,2,1,0:T(8,128)(2,1)S(1)}, u32[]{:S(2)}, u32[]{:S(2)}) collective-permute-start(bf16[8,2,24,1280]{3,2,1,0:T(8,128)(2,1)} %get-tuple-element.258), channel_id=1, source_target_pairs={{0,2},{1,3},{2,0},{3,1},{4,6},{5,7},{6,4},{7,5},{8,10},{9,11},{10,... | collective-permute-start | bytes 2949128 | tf_op jit(solution)/shard_map/ppermute | solution.py:374
  325.4 10.6 %collective-permute-start.44 = (bf16[2,2,24,1792]{3,2,1,0:T(8,128)(2,1)}, bf16[2,2,24,1792]{3,2,1,0:T(8,128)(2,1)S(1)}, u32[]{:S(2)}, u32[]{:S(2)}) collective-permute-start(bf16[2,2,24,1792]{3,2,1,0:T(8,128)(2,1)} %get-tuple-element.246), channel_id=1, source_target_pairs={{0,4},{1,5},{2,6},{3,7},{4,0},{5,1},{6,2},{7,3},{8,12},{9,13},{10,... | collective-permute-start | bytes 1032200 | tf_op jit(solution)/shard_map/ppermute | solution.py:374
  329.8 23.8 %collective-permute-start.45 = (bf16[2,2,24,1792]{3,2,1,0:T(8,128)(2,1)}, bf16[2,2,24,1792]{3,2,1,0:T(8,128)(2,1)}, u32[]{:S(2)}, u32[]{:S(2)}) collective-permute-start(bf16[2,2,24,1792]{3,2,1,0:T(8,128)(2,1)} %get-tuple-element.247), channel_id=1, source_target_pairs={{0,8},{1,9},{2,10},{3,11},{4,12},{5,13},{6,14},{7,15},{8,0},{9,1},... | collective-permute-start | bytes 1032200 | tf_op jit(solution)/shard_map/ppermute | solution.py:374
  336.0 17.7 %collective-permute-start.46 = (bf16[2,2,24,1792]{3,2,1,0:T(8,128)(2,1)}, bf16[2,2,24,1792]{3,2,1,0:T(8,128)(2,1)}, u32[]{:S(2)}, u32[]{:S(2)}) collective-permute-start(bf16[2,2,24,1792]{3,2,1,0:T(8,128)(2,1)} %get-tuple-element.248), channel_id=1, source_target_pairs={{0,1},{1,0},{2,3},{3,2},{4,5},{5,4},{6,7},{7,6},{8,9},{9,8},{10,11... | collective-permute-start | bytes 1032200 | tf_op jit(solution)/shard_map/ppermute | solution.py:374
  361.6 29.6 %collective-permute-start.50 = (bf16[4,2,24,1280]{3,2,1,0:T(8,128)(2,1)}, bf16[4,2,24,1280]{3,2,1,0:T(8,128)(2,1)S(1)}, u32[]{:S(2)}, u32[]{:S(2)}) collective-permute-start(bf16[4,2,24,1280]{3,2,1,0:T(8,128)(2,1)} %get-tuple-element.264), channel_id=1, source_target_pairs={{0,8},{1,9},{2,10},{3,11},{4,12},{5,13},{6,14},{7,15},{8,0},{9,1},... | collective-permute-start | bytes 1474568 | tf_op jit(solution)/shard_map/ppermute | solution.py:374
  363.0 28.2 %collective-permute-start.51 = (bf16[4,2,24,1280]{3,2,1,0:T(8,128)(2,1)}, bf16[4,2,24,1280]{3,2,1,0:T(8,128)(2,1)S(1)}, u32[]{:S(2)}, u32[]{:S(2)}) collective-permute-start(bf16[4,2,24,1280]{3,2,1,0:T(8,128)(2,1)} %get-tuple-element.265), channel_id=1, source_target_pairs={{0,1},{1,0},{2,3},{3,2},{4,5},{5,4},{6,7},{7,6},{8,9},{9,8},{10,11... | collective-permute-start | bytes 1474568 | tf_op jit(solution)/shard_map/ppermute | solution.py:374
  363.9 27.3 %collective-permute-start.52 = (bf16[4,2,24,1280]{3,2,1,0:T(8,128)(2,1)}, bf16[4,2,24,1280]{3,2,1,0:T(8,128)(2,1)S(1)}, u32[]{:S(2)}, u32[]{:S(2)}) collective-permute-start(bf16[4,2,24,1280]{3,2,1,0:T(8,128)(2,1)} %get-tuple-element.266), channel_id=1, source_target_pairs={{0,4},{1,5},{2,6},{3,7},{4,0},{5,1},{6,2},{7,3},{8,12},{9,13},{10,... | collective-permute-start | bytes 1474568 | tf_op jit(solution)/shard_map/ppermute | solution.py:374
  383.3 42.5 %collective-permute-start.53 = (bf16[512,768]{1,0:T(8,128)(2,1)}, bf16[512,768]{1,0:T(8,128)(2,1)S(1)}, u32[]{:S(2)}, u32[]{:S(2)}) collective-permute-start(bf16[512,768]{1,0:T(8,128)(2,1)} %fusion.5), channel_id=1, source_target_pairs={{0,16},{1,17},{2,18},{3,19},{4,20},{5,21},{6,22},{7,23},{8,24},{9,... | collective-permute-start | bytes 2359304 | tf_op jit(solution)/shard_map/ppermute | solution.py:374
  412.8 14.7 %collective-permute-start.54 = (bf16[8,2,24,768]{3,2,1,0:T(8,128)(2,1)}, bf16[8,2,24,768]{3,2,1,0:T(8,128)(2,1)S(1)}, u32[]{:S(2)}, u32[]{:S(2)}) collective-permute-start(bf16[8,2,24,768]{3,2,1,0:T(8,128)(2,1)} %get-tuple-element.273), channel_id=1, source_target_pairs={{0,2},{1,3},{2,0},{3,1},{4,6},{5,7},{6,4},{7,5},{8,10},{9,11},{10,... | collective-permute-start | bytes 1769480 | tf_op jit(solution)/shard_map/ppermute | solution.py:374
  412.9 16.2 %collective-permute-start.62 = (bf16[8,2,24,896]{3,2,1,0:T(8,128)(2,1)}, bf16[8,2,24,896]{3,2,1,0:T(8,128)(2,1)S(1)}, u32[]{:S(2)}, u32[]{:S(2)}) collective-permute-start(bf16[8,2,24,896]{3,2,1,0:T(8,128)(2,1)} %get-tuple-element.283), channel_id=1, source_target_pairs={{0,2},{1,3},{2,0},{3,1},{4,6},{5,7},{6,4},{7,5},{8,10},{9,11},{10,... | collective-permute-start | bytes 2064392 | tf_op jit(solution)/shard_map/ppermute | solution.py:374
  414.0 14.7 %collective-permute-start.61 = (bf16[8,2,24,768]{3,2,1,0:T(8,128)(2,1)}, bf16[8,2,24,768]{3,2,1,0:T(8,128)(2,1)S(1)}, u32[]{:S(2)}, u32[]{:S(2)}) collective-permute-start(bf16[8,2,24,768]{3,2,1,0:T(8,128)(2,1)} %get-tuple-element.281), channel_id=1, source_target_pairs={{0,2},{1,3},{2,0},{3,1},{4,6},{5,7},{6,4},{7,5},{8,10},{9,11},{10,... | collective-permute-start | bytes 1769480 | tf_op jit(solution)/shard_map/ppermute | solution.py:374
  424.2 12.8 %collective-permute-start.58 = (bf16[2,2,24,1280]{3,2,1,0:T(8,128)(2,1)}, bf16[2,2,24,1280]{3,2,1,0:T(8,128)(2,1)}, u32[]{:S(2)}, u32[]{:S(2)}) collective-permute-start(bf16[2,2,24,1280]{3,2,1,0:T(8,128)(2,1)} %get-tuple-element.277), channel_id=1, source_target_pairs={{0,4},{1,5},{2,6},{3,7},{4,0},{5,1},{6,2},{7,3},{8,12},{9,13},{10,... | collective-permute-start | bytes 737288 | tf_op jit(solution)/shard_map/ppermute | solution.py:374
  425.8 11.2 %collective-permute-start.59 = (bf16[2,2,24,1280]{3,2,1,0:T(8,128)(2,1)}, bf16[2,2,24,1280]{3,2,1,0:T(8,128)(2,1)}, u32[]{:S(2)}, u32[]{:S(2)}) collective-permute-start(bf16[2,2,24,1280]{3,2,1,0:T(8,128)(2,1)} %get-tuple-element.278), channel_id=1, source_target_pairs={{0,8},{1,9},{2,10},{3,11},{4,12},{5,13},{6,14},{7,15},{8,0},{9,1},... | collective-permute-start | bytes 737288 | tf_op jit(solution)/shard_map/ppermute | solution.py:374
  427.6 9.4 %collective-permute-start.60 = (bf16[2,2,24,1280]{3,2,1,0:T(8,128)(2,1)}, bf16[2,2,24,1280]{3,2,1,0:T(8,128)(2,1)}, u32[]{:S(2)}, u32[]{:S(2)}) collective-permute-start(bf16[2,2,24,1280]{3,2,1,0:T(8,128)(2,1)} %get-tuple-element.279), channel_id=1, source_target_pairs={{0,1},{1,0},{2,3},{3,2},{4,5},{5,4},{6,7},{7,6},{8,9},{9,8},{10,11... | collective-permute-start | bytes 737288 | tf_op jit(solution)/shard_map/ppermute | solution.py:374
  437.0 12.5 %collective-permute-start.63 = (bf16[4,2,24,768]{3,2,1,0:T(8,128)(2,1)}, bf16[4,2,24,768]{3,2,1,0:T(8,128)(2,1)}, u32[]{:S(2)}, u32[]{:S(2)}) collective-permute-start(bf16[4,2,24,768]{3,2,1,0:T(8,128)(2,1)} %get-tuple-element.287), channel_id=1, source_target_pairs={{0,8},{1,9},{2,10},{3,11},{4,12},{5,13},{6,14},{7,15},{8,0},{9,1},... | collective-permute-start | bytes 884744 | tf_op jit(solution)/shard_map/ppermute | solution.py:374
  438.8 10.7 %collective-permute-start.64 = (bf16[4,2,24,768]{3,2,1,0:T(8,128)(2,1)}, bf16[4,2,24,768]{3,2,1,0:T(8,128)(2,1)}, u32[]{:S(2)}, u32[]{:S(2)}) collective-permute-start(bf16[4,2,24,768]{3,2,1,0:T(8,128)(2,1)} %get-tuple-element.288), channel_id=1, source_target_pairs={{0,1},{1,0},{2,3},{3,2},{4,5},{5,4},{6,7},{7,6},{8,9},{9,8},{10,11... | collective-permute-start | bytes 884744 | tf_op jit(solution)/shard_map/ppermute | solution.py:374
  439.9 9.6 %collective-permute-start.65 = (bf16[4,2,24,896]{3,2,1,0:T(8,128)(2,1)}, bf16[4,2,24,896]{3,2,1,0:T(8,128)(2,1)}, u32[]{:S(2)}, u32[]{:S(2)}) collective-permute-start(bf16[4,2,24,896]{3,2,1,0:T(8,128)(2,1)} %get-tuple-element.289), channel_id=1, source_target_pairs={{0,4},{1,5},{2,6},{3,7},{4,0},{5,1},{6,2},{7,3},{8,12},{9,13},{10,... | collective-permute-start | bytes 1032200 | tf_op jit(solution)/shard_map/ppermute | solution.py:374
  449.5 16.4 %collective-permute-start.77 = (bf16[24,5376]{1,0:T(8,128)(2,1)}, bf16[24,5376]{1,0:T(8,128)(2,1)S(1)}, u32[]{:S(2)}, u32[]{:S(2)}) collective-permute-start(bf16[24,5376]{1,0:T(8,128)(2,1)} %get-tuple-element.330), channel_id=1, source_target_pairs={{0,16},{1,17},{2,18},{3,19},{4,20},{5,21},{6,22},{7,23},{8,24},{9,... | collective-permute-start | bytes 774152 | tf_op jit(solution)/shard_map/ppermute | solution.py:374
  457.9 9.4 %collective-permute-start.69 = (bf16[2,2,24,768]{3,2,1,0:T(8,128)(2,1)}, bf16[2,2,24,768]{3,2,1,0:T(8,128)(2,1)S(1)}, u32[]{:S(2)}, u32[]{:S(2)}) collective-permute-start(bf16[2,2,24,768]{3,2,1,0:T(8,128)(2,1)} %get-tuple-element.312), channel_id=1, source_target_pairs={{0,4},{1,5},{2,6},{3,7},{4,0},{5,1},{6,2},{7,3},{8,12},{9,13},{10,... | collective-permute-start | bytes 442376 | tf_op jit(solution)/shard_map/ppermute | solution.py:374
  467.4 17.9 %collective-permute-start.76 = (bf16[24,3840]{1,0:T(8,128)(2,1)S(1)}, bf16[24,3840]{1,0:T(8,128)(2,1)S(1)}, u32[]{:S(2)}, u32[]{:S(2)}) collective-permute-start(bf16[24,3840]{1,0:T(8,128)(2,1)S(1)} %copy-done.154), channel_id=1, source_target_pairs={{0,16},{1,17},{2,18},{3,19},{4,20},{5,21},{6,22},{7,23},{8,24},{9,... | collective-permute-start | bytes 552968 | tf_op jit(solution)/shard_map/ppermute | solution.py:374
  (192 other events, 2448.7 us)
